TPU v7x, 32 devices: a whole 2x2x4 slice. The times are simulated.
32 devices in a mesh: groups: 2 (over x), slab: 16 (over z, y, core).
Axes of the slice: x: 2, y: 2, z: 4, core: 2. Of those that a mesh axis runs over, the one named last changes fastest.
Arguments:
- volume: float32 [2, 1024, 1024], P('groups', 'slab'), parts along dimension 0, may hold values from -6 to 6
- noise: float32 [2, 1024, 1024], P('groups', 'slab'), parts along dimension 0, may hold values from -6 to 6
- measured: float32 [2, 1024, 16, 1024], P('groups', 'slab'), parts along dimension 0, may hold values from -20 to 20
- angles: int32 [32], P('groups'), parts along dimension 0, may hold values from 0 to 179
- offsets: int32 [32], P('groups'), parts along dimension 0, may hold values from -32 to 32
- step_size: float32 [2], P('groups'), parts along dimension 0, may hold values from 0.1 to 0.4
- lift_w: float32 [64], replicated, may hold values from -4 to 4
- lift_b: float32 [64], replicated, may hold values from -4 to 4
- conv_a: bfloat16 [9, 64, 64], replicated, may hold values from -0.25 to 0.25
- bias_a: float32 [64], replicated, may hold values from -4 to 4
- conv_b: bfloat16 [9, 64, 64], replicated, may hold values from -0.25 to 0.25
- out_w: float32 [64], replicated, may hold values from -0.75 to 0.75
Outputs:
- updated: float32 [2, 1024, 1024], P('groups', 'slab'), parts along dimension 0
There are 2 independent parts, one for each index of `groups`. A program takes and returns all parts, laid end to end along the dimension named above; an argument that names none is the same for every part. Nothing has to cross between parts.
All inputs are finite; a program needn't handle non-finite values.
Results may differ from a plain program's by a relative error of at most 0.0025.
Values may be sent and summed in bfloat16 or wider, within the bound.
No kernel may reach another device: no remote copies, remote signals or barrier semaphores. Data moves between devices by JAX's collectives and lax.ppermute only.
A program may use at most 256 MiB of HBM per device.

v0:
```python
import jax
import jax.numpy as jnp
from jax import lax
from jax.sharding import PartitionSpec as P

NX = 1024
NY = 1024
DET = 1024
VIEWS = 16
ANGLES = 180
SLICES = 1


data_gain = 0.25


def padded_2(block, sides, width):
    for axis, dim in sides:
        count = lax.axis_size(axis)
        forward = [(i, i + 1) for i in range(count - 1)]
        backward = [(target, source) for source, target in forward]
        low = lax.ppermute(
            lax.slice_in_dim(block, block.shape[dim] - width, None, axis=dim), axis, forward
        )
        high = lax.ppermute(lax.slice_in_dim(block, 0, width, axis=dim), axis, backward)
        block = jnp.concatenate([low, block, high], axis=dim)
    return block


def conv_rows(padded_rows, kernel):
    rows = padded_rows.shape[-2] - 2
    width = padded_rows.shape[-1]
    padded = jnp.pad(padded_rows, [(0, 0)] * (padded_rows.ndim - 1) + [(1, 1)])
    total = None
    for i in range(3):
        for j in range(3):
            piece = padded[..., i : i + rows, j : j + width]
            flat = piece.reshape(piece.shape[0], -1)
            term = jnp.dot(kernel[3 * i + j], flat, preferred_element_type=jnp.float32)
            term = term.reshape((kernel.shape[1],) + piece.shape[1:])
            total = term if total is None else total + term
    return total


def inside_rows(first, count):
    index = first + jnp.arange(count, dtype=jnp.int32)
    return (index >= 0) & (index < NX)


def make_tent(angle, offset):
    level = jnp.abs(jnp.cos(jnp.pi * angle.astype(jnp.float32) / ANGLES))
    spread = 0.6 + 0.4 * level
    bins = jnp.arange(DET, dtype=jnp.float32)[:, None]
    cells = jnp.arange(NX, dtype=jnp.float32)[None, :]
    target = (DET - 1) * 0.5 + (cells - (NX - 1) * 0.5) * spread + offset.astype(jnp.float32)
    return jnp.maximum(0.0, 1.0 - jnp.abs(bins - target)).astype(jnp.bfloat16)


def per_device(
    volume,
    noise,
    measured,
    angles,
    offsets,
    step_size,
    lift_w,
    lift_b,
    conv_a,
    bias_a,
    conv_b,
    out_w,
):
    slices, rows, width = volume.shape
    anchor = lax.axis_index("slab") * rows
    extended = padded_2(volume, (("slab", 1),), 2)
    value = jax.nn.silu(lift_w[:, None, None, None] * extended[None] + lift_b[:, None, None, None])
    keep = inside_rows(anchor - 2, extended.shape[1])
    h0 = jnp.where(keep[None, None, :, None], value, 0.0).astype(jnp.bfloat16)
    first_pass = jax.nn.silu(conv_rows(h0, conv_a) + bias_a[:, None, None, None])
    keep = inside_rows(anchor - 1, rows + 2)
    h1_wide = jnp.where(keep[None, None, :, None], first_pass, 0.0).astype(jnp.bfloat16)
    h0_core = h0[:, :, 2:-2]
    mixed = conv_rows(h1_wide, conv_b) + h0_core.astype(jnp.float32)
    score = jnp.sum(out_w[:, None, None, None] * mixed, axis=0)
    turned = jnp.transpose(volume.astype(jnp.bfloat16), (0, 2, 1))
    cells = lax.all_to_all(turned, "slab", split_axis=1, concat_axis=2, tiled=True)
    columns = cells.shape[1]
    flat_cells = cells.reshape(-1, NX)

    def one_view(view, carry):
        back, misfit = carry
        tent = make_tent(angles[view], offsets[view])
        seen = lax.dynamic_index_in_dim(measured, view, 2, keepdims=False)
        proj = jnp.dot(flat_cells, tent.T, preferred_element_type=jnp.float32)
        misfit_rows = proj - seen.reshape(-1, DET)
        misfit = misfit + jnp.sum(misfit_rows * misfit_rows)
        low_rows = misfit_rows.astype(jnp.bfloat16)
        back = back + jnp.dot(low_rows, tent, preferred_element_type=jnp.float32)
        return (back, misfit)

    start = (jnp.zeros((slices * columns, NX), jnp.float32), jnp.zeros((), jnp.float32))
    back, misfit_part = lax.fori_loop(0, VIEWS, one_view, start)
    returned = lax.all_to_all(
        back.reshape(slices, columns, NX).astype(jnp.bfloat16),
        "slab",
        split_axis=2,
        concat_axis=1,
        tiled=True,
    ).astype(jnp.float32)
    backproj = jnp.transpose(returned, (0, 2, 1))
    misfit = lax.psum(misfit_part, "slab")
    weight = data_gain / jnp.sqrt(misfit / (SLICES * NY * VIEWS * DET) + 1e-06)
    step = step_size[0]
    return volume + step * (score - weight * backproj) + jnp.sqrt(2.0 * step) * noise


def solution(mesh):
    placed = (
        P("groups", "slab", None),
        P("groups", "slab", None),
        P("groups", "slab", None, None),
        P("groups"),
        P("groups"),
        P("groups"),
        P(),
        P(),
        P(),
        P(),
        P(),
        P(),
    )
    return jax.shard_map(
        per_device, mesh=mesh, in_specs=placed, out_specs=P("groups", "slab", None), check_vma=False
    )
```

profile of v0, /device:TPU:0, one launch (start us, length us, event | category | flops | bytes accessed | tf_op | source)
XLA Modules:
  0.0 832.8 jit_solution(16712048890373271529)
XLA Ops:
  28.9 44.1 %pad_slice_fusion.6 = (bf16[64,1,66,1024]{3,2,0,1:T(8,128)(2,1)}, bf16[64,1,66,1024]{3,2,0,1:T(8,128)(2,1)}, bf16[64,1,66,1024]{3,2,0,1:T(8,128)(2,1)}, bf16[64,...) fusion(bf16[64,1,68,1024]{3,2,0,1:T(8,128)(2,1)S(1)} %select_co, ...), kind=kLoop, calls=%fused_computation.49 | loop fusion | bytes 115605504 | tf_op jit(solution)/shard_map/slice | solution.py:37
  97.7 12.6 %copy.39 = bf16[8,8,66,1024]{3,1,2,0:T(8,128)(2,1)} copy(bf16[8,8,66,1024]{3,2,1,0:T(8,128)(2,1)} %bitcast.222) | data formatting | bytes 17301504
  172.1 12.8 %copy.36 = bf16[8,8,66,1024]{3,1,2,0:T(8,128)(2,1)} copy(bf16[8,8,66,1024]{3,2,1,0:T(8,128)(2,1)} %bitcast.216) | data formatting | bytes 17301504
  196.8 16.8 %convolution_add_fusion.7 = f32[67584,64]{0,1:T(8,128)} fusion(f32[67584,64]{0,1:T(8,128)} %fusion.40, bf16[64,67584]{1,0:T(8,128)(2,1)} %bitcast.238, bf16[9,64,64]{2,1,0:T(8,128)(2,1)S(1)} %copy-done.4), kind=kOutput, calls=%fused_computation.28 | convolution fusion | flops 557973504 | bytes 43270144 | tf_op jit(solution)/shard_map/dot_general | solution.py:39
  213.6 14.6 %convolution_add_fusion.6 = f32[67584,64]{0,1:T(8,128)} fusion(f32[67584,64]{0,1:T(8,128)} %convolution_add_fusion.7, bf16[64,67584]{1,0:T(8,128)(2,1)S(1)} %bitcast.236, bf16[9,64,64]{2,1,0:T(8,128)(2,1)S(1)} %copy-done.4), kind=kOutput, calls=%fused_computation.27 | convolution fusion | flops 557973504 | bytes 43270144 | tf_op jit(solution)/shard_map/dot_general | solution.py:39
  228.2 16.9 %convolution_add_fusion.5 = f32[67584,64]{0,1:T(8,128)} fusion(f32[67584,64]{0,1:T(8,128)} %convolution_add_fusion.6, bf16[64,67584]{1,0:T(8,128)(2,1)} %bitcast.233, bf16[9,64,64]{2,1,0:T(8,128)(2,1)S(1)} %copy-done.4), kind=kOutput, calls=%fused_computation.26 | convolution fusion | flops 557973504 | bytes 43270144 | tf_op jit(solution)/shard_map/dot_general | solution.py:39
  245.1 17.0 %convolution_add_fusion.4 = f32[67584,64]{0,1:T(8,128)} fusion(f32[67584,64]{0,1:T(8,128)} %convolution_add_fusion.5, bf16[64,67584]{1,0:T(8,128)(2,1)} %bitcast.237, bf16[9,64,64]{2,1,0:T(8,128)(2,1)S(1)} %copy-done.4), kind=kOutput, calls=%fused_computation.25 | convolution fusion | flops 557973504 | bytes 43270144 | tf_op jit(solution)/shard_map/dot_general | solution.py:39
  262.1 14.6 %convolution_add_fusion.3 = f32[67584,64]{0,1:T(8,128)} fusion(f32[67584,64]{0,1:T(8,128)} %convolution_add_fusion.4, bf16[64,67584]{1,0:T(8,128)(2,1)S(1)} %bitcast.232, bf16[9,64,64]{2,1,0:T(8,128)(2,1)S(1)} %copy-done.4), kind=kOutput, calls=%fused_computation.24 | convolution fusion | flops 557973504 | bytes 43270144 | tf_op jit(solution)/shard_map/dot_general | solution.py:39
  276.7 16.9 %convolution_add_fusion.2 = f32[67584,64]{0,1:T(8,128)} fusion(f32[67584,64]{0,1:T(8,128)} %convolution_add_fusion.3, bf16[64,67584]{1,0:T(8,128)(2,1)} %bitcast.229, bf16[9,64,64]{2,1,0:T(8,128)(2,1)S(1)} %copy-done.4), kind=kOutput, calls=%fused_computation.23 | convolution fusion | flops 557973504 | bytes 43270144 | tf_op jit(solution)/shard_map/dot_general | solution.py:39
  293.6 16.8 %convolution_add_fusion.1 = f32[67584,64]{0,1:T(8,128)} fusion(f32[67584,64]{0,1:T(8,128)} %convolution_add_fusion.2, bf16[64,67584]{1,0:T(8,128)(2,1)} %bitcast.228, bf16[9,64,64]{2,1,0:T(8,128)(2,1)S(1)} %copy-done.4), kind=kOutput, calls=%fused_computation.22 | convolution fusion | flops 557973504 | bytes 43270144 | tf_op jit(solution)/shard_map/dot_general | solution.py:39
  310.3 14.6 %fusion.16 = f32[64,67584]{1,0:T(8,128)} fusion(f32[67584,64]{0,1:T(8,128)} %convolution_add_fusion.1, bf16[64,67584]{1,0:T(8,128)(2,1)S(1)} %bitcast.227, bf16[9,64,64]{2,1,0:T(8,128)(2,1)S(1)} %copy-done.4), kind=kOutput, calls=%fused_computation.29 | convolution fusion | flops 557973504 | bytes 43270144 | tf_op jit(solution)/shard_map/dot_general | solution.py:39
  324.9 15.2 %reshape.495 = f32[64,1,66,1024]{3,2,0,1:T(8,128)} reshape(f32[64,67584]{1,0:T(8,128)} %fusion.16) | data formatting | bytes 34603008 | tf_op jit(solution)/shard_map/add | solution.py:41
  350.3 40.4 %pad_slice_fusion = (bf16[64,1,64,1024]{3,2,0,1:T(8,128)(2,1)}, bf16[64,1,64,1024]{3,2,0,1:T(8,128)(2,1)}, bf16[64,1,64,1024]{3,2,0,1:T(8,128)(2,1)}, bf16[64,1,...) fusion(bf16[64,1,66,1024]{3,2,0,1:T(8,128)(2,1)S(1)} %select_co, ...), kind=kLoop, calls=%fused_computation.43 | loop fusion | bytes 110100480 | tf_op jit(solution)/shard_map/slice | solution.py:37
  510.9 14.0 %convolution_add_fusion.15 = f32[65536,64]{0,1:T(8,128)} fusion(f32[65536,64]{0,1:T(8,128)} %fusion.30, bf16[64,65536]{1,0:T(8,128)(2,1)S(1)} %bitcast.254, bf16[9,64,64]{2,1,0:T(8,128)(2,1)S(1)} %copy-done.5), kind=kOutput, calls=%fused_computation.37 | convolution fusion | flops 541065216 | bytes 41959424 | tf_op jit(solution)/shard_map/dot_general | solution.py:39
  524.9 16.4 %convolution_add_fusion.14 = f32[65536,64]{0,1:T(8,128)} fusion(f32[65536,64]{0,1:T(8,128)} %convolution_add_fusion.15, bf16[64,65536]{1,0:T(8,128)(2,1)} %bitcast.250, bf16[9,64,64]{2,1,0:T(8,128)(2,1)S(1)} %copy-done.5), kind=kOutput, calls=%fused_computation.36 | convolution fusion | flops 541065216 | bytes 41959424 | tf_op jit(solution)/shard_map/dot_general | solution.py:39
  541.2 13.8 %convolution_add_fusion.13 = f32[65536,64]{0,1:T(8,128)} fusion(f32[65536,64]{0,1:T(8,128)} %convolution_add_fusion.14, bf16[64,65536]{1,0:T(8,128)(2,1)S(1)} %bitcast.249, bf16[9,64,64]{2,1,0:T(8,128)(2,1)S(1)} %copy-done.5), kind=kOutput, calls=%fused_computation.35 | convolution fusion | flops 541065216 | bytes 41959424 | tf_op jit(solution)/shard_map/dot_general | solution.py:39
  555.1 16.4 %convolution_add_fusion.12 = f32[65536,64]{0,1:T(8,128)} fusion(f32[65536,64]{0,1:T(8,128)} %convolution_add_fusion.13, bf16[64,65536]{1,0:T(8,128)(2,1)} %bitcast.251, bf16[9,64,64]{2,1,0:T(8,128)(2,1)S(1)} %copy-done.5), kind=kOutput, calls=%fused_computation.34 | convolution fusion | flops 541065216 | bytes 41959424 | tf_op jit(solution)/shard_map/dot_general | solution.py:39
  571.5 16.6 %convolution_add_fusion.11 = f32[65536,64]{0,1:T(8,128)} fusion(f32[65536,64]{0,1:T(8,128)} %convolution_add_fusion.12, bf16[64,65536]{1,0:T(8,128)(2,1)} %bitcast.246, bf16[9,64,64]{2,1,0:T(8,128)(2,1)S(1)} %copy-done.5), kind=kOutput, calls=%fused_computation.33 | convolution fusion | flops 541065216 | bytes 41959424 | tf_op jit(solution)/shard_map/dot_general | solution.py:39
  588.1 14.0 %convolution_add_fusion.10 = f32[65536,64]{0,1:T(8,128)} fusion(f32[65536,64]{0,1:T(8,128)} %convolution_add_fusion.11, bf16[64,65536]{1,0:T(8,128)(2,1)S(1)} %bitcast.245, bf16[9,64,64]{2,1,0:T(8,128)(2,1)S(1)} %copy-done.5), kind=kOutput, calls=%fused_computation.32 | convolution fusion | flops 541065216 | bytes 41959424 | tf_op jit(solution)/shard_map/dot_general | solution.py:39
  602.1 16.4 %convolution_add_fusion.9 = f32[65536,64]{0,1:T(8,128)} fusion(f32[65536,64]{0,1:T(8,128)} %convolution_add_fusion.10, bf16[64,65536]{1,0:T(8,128)(2,1)} %bitcast.242, bf16[9,64,64]{2,1,0:T(8,128)(2,1)S(1)} %copy-done.5), kind=kOutput, calls=%fused_computation.31 | convolution fusion | flops 541065216 | bytes 41959424 | tf_op jit(solution)/shard_map/dot_general | solution.py:39
  618.5 13.8 %convolution_add_fusion.8 = f32[65536,64]{0,1:T(8,128)} fusion(f32[65536,64]{0,1:T(8,128)} %convolution_add_fusion.9, bf16[64,65536]{1,0:T(8,128)(2,1)S(1)} %bitcast.241, bf16[9,64,64]{2,1,0:T(8,128)(2,1)S(1)} %copy-done.5), kind=kOutput, calls=%fused_computation.30 | convolution fusion | flops 541065216 | bytes 41959424 | tf_op jit(solution)/shard_map/dot_general | solution.py:39
  632.3 17.9 %copy.54 = f32[8,8,64,1024]{3,2,1,0:T(8,128)} copy(f32[8,8,64,1024]{3,1,2,0:T(8,128)} %bitcast.213) | data formatting | bytes 33554432
  652.5 122.3 %while.18 = (s32[]{:T(128)}, f32[64,1024]{1,0:T(8,128)S(1)}, f32[]{:T(128)}, s32[16]{0:T(128)S(1)}, s32[16]{0:T(128)S(1)}, /*index=5*/bf16[64,1024]{1,0:T(8,128)...) while((s32[]{:T(128)}, f32[64,1024]{1,0:T(8,128)S(1)}, ...), condition=%wide.region_3.4_spmd.clone, body=%wide.region_1.3_spmd.clone.sunk | while | flops 279318528 | bytes 1716479 | solution.py:102
  794.5 34.9 %psum.7 = f32[]{:T(128)} all-reduce(f32[]{:T(128)} %get-tuple-element.183), channel_id=1, replica_groups=mesh['groups'=2,'slab'=16] {'slab'}, use_global_device_ids=true, to_apply=%region_4.5 | all-reduce | flops 1 | bytes 8 | tf_op jit(solution)/shard_map/psum | solution.py:111
  (213 shorter events, 370.0 us)
Async XLA Ops:
  0.8 20.1 %collective-permute-start = (f32[1,2,1024]{2,1,0:T(2,128)S(1)}, f32[1,2,1024]{2,1,0:T(2,128)S(1)}, u32[]{:S(2)}, u32[]{:S(2)}) collective-permute-start(f32[1,2,1024]{2,1,0:T(2,128)S(1)} %get-tuple-element.278), channel_id=1, source_target_pairs={{0,1},{1,2},{2,3},{3,4},{4,5},{5,6},{6,7},{7,8},{8,9},{9,10},{10,1... | collective-permute-start | bytes 24584 | tf_op jit(solution)/shard_map/ppermute | solution.py:22
  3.2 17.7 %collective-permute-start.1 = (f32[1,2,1024]{2,1,0:T(2,128)S(1)}, f32[1,2,1024]{2,1,0:T(2,128)S(1)}, u32[]{:S(2)}, u32[]{:S(2)}) collective-permute-start(f32[1,2,1024]{2,1,0:T(2,128)S(1)} %get-tuple-element.279), channel_id=1, source_target_pairs={{1,0},{2,1},{3,2},{4,3},{5,4},{6,5},{7,6},{8,7},{9,8},{10,9},{11,1... | collective-permute-start | bytes 24584 | tf_op jit(solution)/shard_map/ppermute | solution.py:25
  10.2 640.0 %all-to-all-start = ((bf16[16,2,2048]{2,1,0:T(2,128)(2,1)}), bf16[16,2,2048]{2,1,0:T(2,128)(2,1)}, u32[]{:S(2)}, u32[]{:S(2)}) async-start(bf16[16,2,2048]{2,1,0:T(2,128)(2,1)} %reshape.499), calls=%async_computation | async-start | bytes 262144 | tf_op jit(solution)/shard_map/all_to_all | solution.py:86
  28.8 44.1 %copy-start = (bf16[64,1,68,1024]{3,2,0,1:T(8,128)(2,1)}, bf16[64,1,68,1024]{3,2,0,1:T(8,128)(2,1)S(1)}, u32[]{:S(2)}) copy-start(bf16[64,1,68,1024]{3,2,0,1:T(8,128)(2,1)S(1)} %select_convert_fusion.1) | copy-start | bytes 26738692
  184.8 28.7 %slice-start.6 = ((s8[8650752]{0:T(1024)(128)(4,1)}), s8[4194304]{0:T(1024)(128)(4,1)S(1)}, s32[]{:S(2)}) async-start(s8[8650752]{0:T(1024)(128)(4,1)} %bitcast.234), calls=%async_computation.8 | async-start | bytes 8388608
  184.8 28.7 %slice-start.7 = ((s8[8650752]{0:T(1024)(128)(4,1)}), s8[4194304]{0:T(1024)(128)(4,1)S(1)}, s32[]{:S(2)}) async-start(s8[8650752]{0:T(1024)(128)(4,1)} %bitcast.234), calls=%async_computation.9 | async-start | bytes 8388608
  196.8 16.8 %slice-start.8 = ((s8[8650752]{0:T(1024)(128)(4,1)}), s8[262144]{0:T(1024)(128)(4,1)S(1)}, s32[]{:S(2)}) async-start(s8[8650752]{0:T(1024)(128)(4,1)} %bitcast.234), calls=%async_computation.10 | async-start | bytes 524288
  228.2 33.9 %slice-start.3 = ((s8[8650752]{0:T(1024)(128)(4,1)}), s8[4194304]{0:T(1024)(128)(4,1)S(1)}, s32[]{:S(2)}) async-start(s8[8650752]{0:T(1024)(128)(4,1)} %bitcast.230), calls=%async_computation.5 | async-start | bytes 8388608
  228.2 33.9 %slice-start.4 = ((s8[8650752]{0:T(1024)(128)(4,1)}), s8[4194304]{0:T(1024)(128)(4,1)S(1)}, s32[]{:S(2)}) async-start(s8[8650752]{0:T(1024)(128)(4,1)} %bitcast.230), calls=%async_computation.6 | async-start | bytes 8388608
  245.1 17.0 %slice-start.5 = ((s8[8650752]{0:T(1024)(128)(4,1)}), s8[262144]{0:T(1024)(128)(4,1)S(1)}, s32[]{:S(2)}) async-start(s8[8650752]{0:T(1024)(128)(4,1)} %bitcast.230), calls=%async_computation.7 | async-start | bytes 524288
  276.7 33.6 %slice-start = ((s8[8650752]{0:T(1024)(128)(4,1)}), s8[4194304]{0:T(1024)(128)(4,1)S(1)}, s32[]{:S(2)}) async-start(s8[8650752]{0:T(1024)(128)(4,1)} %bitcast.225), calls=%async_computation.2 | async-start | bytes 8388608
  276.7 33.6 %slice-start.1 = ((s8[8650752]{0:T(1024)(128)(4,1)}), s8[4194304]{0:T(1024)(128)(4,1)S(1)}, s32[]{:S(2)}) async-start(s8[8650752]{0:T(1024)(128)(4,1)} %bitcast.225), calls=%async_computation.3 | async-start | bytes 8388608
  293.6 16.8 %slice-start.2 = ((s8[8650752]{0:T(1024)(128)(4,1)}), s8[262144]{0:T(1024)(128)(4,1)S(1)}, s32[]{:S(2)}) async-start(s8[8650752]{0:T(1024)(128)(4,1)} %bitcast.225), calls=%async_computation.4 | async-start | bytes 524288
  487.0 23.9 %slice-start.15 = ((s8[8388608]{0:T(1024)(128)(4,1)}), s8[4194304]{0:T(1024)(128)(4,1)S(1)}, s32[]{:S(2)}) async-start(s8[8388608]{0:T(1024)(128)(4,1)} %bitcast.252), calls=%async_computation.17 | async-start | bytes 8388608
  510.9 30.4 %slice-start.13 = ((s8[8388608]{0:T(1024)(128)(4,1)}), s8[4194304]{0:T(1024)(128)(4,1)S(1)}, s32[]{:S(2)}) async-start(s8[8388608]{0:T(1024)(128)(4,1)} %bitcast.247), calls=%async_computation.15 | async-start | bytes 8388608
  555.1 33.0 %slice-start.11 = ((s8[8388608]{0:T(1024)(128)(4,1)}), s8[4194304]{0:T(1024)(128)(4,1)S(1)}, s32[]{:S(2)}) async-start(s8[8388608]{0:T(1024)(128)(4,1)} %bitcast.243), calls=%async_computation.13 | async-start | bytes 8388608
  588.1 30.4 %slice-start.9 = ((s8[8388608]{0:T(1024)(128)(4,1)}), s8[4194304]{0:T(1024)(128)(4,1)S(1)}, s32[]{:S(2)}) async-start(s8[8388608]{0:T(1024)(128)(4,1)} %bitcast.239), calls=%async_computation.11 | async-start | bytes 8388608
  632.3 20.2 %copy-start.2 = (f32[64,1024]{1,0:T(8,128)S(1)}, f32[64,1024]{1,0:T(8,128)}, u32[]{:S(2)}) copy-start(f32[64,1024]{1,0:T(8,128)} %custom-call) | copy-start | bytes 786436
  632.3 20.2 %copy-start.9 = (s32[16]{0:T(128)S(1)}, s32[16]{0:T(128)}, u32[]{:S(2)}) copy-start(s32[16]{0:T(128)} %param.17) | copy-start | bytes 196
  632.3 20.2 %copy-start.10 = (s32[16]{0:T(128)S(1)}, s32[16]{0:T(128)}, u32[]{:S(2)}) copy-start(s32[16]{0:T(128)} %param.18) | copy-start | bytes 196
  652.5 132.0 %copy-start.7 = (f32[64]{0:T(128)S(1)}, f32[64]{0:T(128)}, u32[]{:S(2)}) copy-start(f32[64]{0:T(128)} %param.25) | copy-start | bytes 772
  778.5 51.6 %all-to-all-start.1 = ((bf16[16,2,2048]{2,1,0:T(2,128)(2,1)}), bf16[16,2,2048]{2,1,0:T(2,128)(2,1)S(1)}, u32[]{:S(2)}, u32[]{:S(2)}) async-start(bf16[16,2,2048]{2,1,0:T(2,128)(2,1)} %reshape.501), calls=%async_computation.1 | async-start | bytes 262144 | tf_op jit(solution)/shard_map/all_to_all | solution.py:103
  784.5 47.1 %copy-start.1 = (f32[1,64,1024]{2,1,0:T(8,128)S(1)}, f32[1,64,1024]{2,1,0:T(8,128)}, u32[]{:S(2)}) copy-start(f32[1,64,1024]{2,1,0:T(8,128)} %param.14) | copy-start | bytes 786436
  784.5 47.0 %copy-start.3 = (f32[1,64,1024]{2,1,0:T(8,128)S(1)}, f32[1,64,1024]{2,1,0:T(8,128)}, u32[]{:S(2)}) copy-start(f32[1,64,1024]{2,1,0:T(8,128)} %param.15) | copy-start | bytes 786436
  (8 other events, 116.4 us)
where the time goes:
time: 842 us; the launch traced here: 833 us
  local copies, waits for them, and re-layouts  393 us (47%)
  matrix products  314 us (37%)
  other arithmetic  35.9 us (4%)
  blocking collectives  34.9 us (4%)
  loops' own time  33.2 us (4%)
  starting transfers between devices  19 us (2%)
    dot_general x18, matrix products, conv_rows(): term = jnp.dot(kernel[3 * i + j], flat, preferred_element_type=jnp.float32)  273 us
    unnamed x81, local copies, waits for them, and re-layouts  243 us
    slice x2, local copies, waits for them, and re-layouts, conv_rows(): piece = padded[..., i:i + rows, j:j + width]  84.5 us
    psum x1, blocking collectives, per_device(): misfit = lax.psum(misfit_part, 'slab')  34.9 us
    another operation x1, loops' own time, per_device(): back, misfit_part = lax.fori_loop(0, VIEWS, one_view, start)  33.2 us
    dynamic_slice x16, local copies, waits for them, and re-layouts, one_view(): seen = lax.dynamic_index_in_dim(measured, view, 2, keepdims=False)  29.1 us
    dot_general x16, matrix products, one_view(): proj = jnp.dot(flat_cells, tent.T, preferred_element_type=jnp.float32)  25.5 us
    dynamic_slice x32, local copies, waits for them, and re-layouts, one_view(): tent = make_tent(angles[view], offsets[view])  18.8 us
  transfers between devices with their start and end apart: 4, of which 0 were waited for; matrix products, arithmetic and copies ran while one was open for 78% of the time, Pallas kernels for 0%

commit v1 on v0

v1 whole, which is shorter than its diff:
```python
import functools

import jax
import jax.numpy as jnp
from jax import lax
from jax.experimental import pallas as pl
from jax.experimental.pallas import tpu as pltpu
from jax.sharding import PartitionSpec as P

ANGLES = 180
LANES = 128

data_gain = 0.25

f32 = jnp.float32
bf16 = jnp.bfloat16
VMEM = pl.BlockSpec(memory_space=pltpu.VMEM)
SMEM = pl.BlockSpec(memory_space=pltpu.SMEM)


def pack_kernel(volume_ref, out_ref, first_ref, last_ref):
    rows = volume_ref.shape[1]
    peers = out_ref.shape[0]
    chunks = LANES // rows
    depth = rows // chunks
    for peer in range(peers):
        piece = volume_ref[0, :, peer * rows : (peer + 1) * rows]
        wide = jnp.concatenate([piece[k * depth : (k + 1) * depth] for k in range(chunks)], axis=1)
        out_ref[peer] = wide.astype(bf16)
    first_ref[...] = volume_ref[0, :2, :]
    last_ref[...] = volume_ref[0, rows - 2 :, :]


def split(value):
    high = value.astype(bf16).astype(f32)
    return high, (value - high).astype(bf16).astype(f32)


def prep_kernel(
    angles_ref, gain_ref, base_ref, conv_a_ref, bias_ref, conv_b_ref, own_ref,
    wa_ref, wb_ref, wr_ref, lift_ref, shift_ref, spread_ref,
):
    channels = conv_a_ref.shape[1]

    def column(row):
        return jnp.broadcast_to(row, (LANES, channels)).T

    lift_ref[0] = column(0.5 * gain_ref[...])
    lift_ref[1] = column(0.5 * base_ref[...])
    shift = column(0.5 * bias_ref[...])
    shift_ref[:channels] = shift
    shift_ref[channels:] = shift

    taps = [conv_a_ref[t].astype(f32) * 0.5 for t in range(9)]
    zero = jnp.zeros((channels, channels), f32)
    for r in range(2):
        for j in range(3):
            for e in range(0, 4, 2):
                pair = [taps[3 * (k - r) + j] if 0 <= k - r < 3 else zero for k in (e, e + 1)]
                at = (4 * j + e) * channels
                wa_ref[r * channels : (r + 1) * channels, at : at + 2 * channels] = jnp.concatenate(
                    pair, axis=1
                ).astype(bf16)

    own = column(own_ref[...])[:, :channels]
    row = lax.broadcasted_iota(jnp.int32, (8, LANES), 0)
    half = lax.broadcasted_iota(jnp.int32, (8, LANES), 1) // channels

    def both(line):
        return jnp.broadcast_to(jnp.concatenate([line, line], axis=1), (8, LANES))

    folded = [split(jnp.sum(own * conv_b_ref[t].astype(f32), axis=0, keepdims=True)) for t in range(9)]
    mine = split(own_ref[...])
    for q in range(5):
        at = slice(q * LANES, (q + 1) * LANES)
        for j in range(3):
            parts = []
            for s in range(2):
                block = jnp.zeros((8, LANES), f32)
                for i in range(3):
                    block = jnp.where(half + 2 * q - row == i, both(folded[3 * i + j][s]), block)
                parts.append(block)
            wb_ref[16 * j : 16 * j + 16, at] = jnp.concatenate(parts, axis=0).astype(bf16)
        if q < 4:
            parts = [jnp.where(half + 2 * q == row, both(mine[s]), 0.0) for s in range(2)]
            wr_ref[:, at] = jnp.concatenate(parts, axis=0).astype(bf16)

    level = jnp.abs(jnp.cos(jnp.pi * angles_ref[...].astype(f32) / ANGLES))
    spread_ref[...] = 0.6 + 0.4 * level


def shifted(block, step):
    width = block.shape[1]
    moved = pltpu.roll(block, (-step) % width, 1)
    lane = lax.broadcasted_iota(jnp.int32, (block.shape[0], LANES), 1)
    if step < 0:
        edge = jnp.where(lane == 0, jnp.zeros_like(moved[:, :LANES]), moved[:, :LANES])
        return jnp.concatenate([edge, moved[:, LANES:]], axis=1)
    edge = jnp.where(lane == LANES - 1, jnp.zeros_like(moved[:, -LANES:]), moved[:, -LANES:])
    return jnp.concatenate([moved[:, :-LANES], edge], axis=1)


def score_kernel(
    anchor_ref, low_ref, volume_ref, high_ref, lift_ref, bias_ref, wa_ref, wb_ref, wr_ref,
    out_ref, ext_ref, ring_a, ring_b, ring_c, h0_ref, h1_ref, *, height,
):
    rows, width = out_ref.shape
    ext_ref[6:8] = low_ref[...]
    ext_ref[8 : 8 + rows] = volume_ref[0]
    ext_ref[8 + rows : 16 + rows] = jnp.zeros((8, width), f32)
    ext_ref[8 + rows : 10 + rows] = high_ref[...]
    channels = lift_ref.shape[1]
    pairs = (rows + 2) // 2
    anchor = anchor_ref[0]
    tiles = width // LANES

    def lift(pair, ring):
        for k in range(2):
            row = 2 * pair + k
            place = anchor + row - 2
            keep = jnp.where((place >= 0) & (place < height), 1.0, 0.0).astype(f32)
            line = ext_ref[pl.ds(row + 6, 1), :]
            for c in range(0, channels, 16):
                gain = jnp.concatenate([lift_ref[0, c : c + 16] * keep] * tiles, axis=1)
                base = jnp.concatenate([lift_ref[1, c : c + 16] * keep] * tiles, axis=1)
                z = gain * line + base
                h = (z * jnp.tanh(z) + z).astype(bf16)
                at = k * channels + c
                ring[0, at : at + 16] = shifted(h, -1)
                ring[1, at : at + 16] = h
                ring[2, at : at + 16] = shifted(h, 1)
                h0_ref[pl.ds(pl.multiple_of(row * channels + c, 16), 16), :] = h

    def step(g, p0, p1, p2):
        lift(g + 2, p2)
        for n in range(0, width, 256):
            rhs = jnp.concatenate([r[j, :, n : n + 256] for j in range(3) for r in (p0, p1)], axis=0)
            acc = jnp.dot(wa_ref[...], rhs, preferred_element_type=f32)
            z = acc + jnp.concatenate([bias_ref[...]] * 2, axis=1)
            h = (z * jnp.tanh(z) + z).astype(bf16)
            h1_ref[pl.ds(pl.multiple_of(g * 2 * channels, 128), 2 * channels), n : n + 256] = h

    lift(0, ring_a)
    lift(1, ring_b)

    def three(it, carry):
        g = it * 3
        step(g, ring_a, ring_b, ring_c)
        step(g + 1, ring_b, ring_c, ring_a)
        step(g + 2, ring_c, ring_a, ring_b)
        return carry

    lax.fori_loop(0, pairs // 3, three, 0)

    @pl.when(anchor == 0)
    def _():
        h1_ref[0:channels] = jnp.zeros((channels, width), bf16)

    @pl.when(anchor + rows == height)
    def _():
        h1_ref[(rows + 1) * channels : (rows + 2) * channels] = jnp.zeros((channels, width), bf16)

    def eight(t, carry):
        at = pl.multiple_of(t * 8 * channels, 128)
        conv = jnp.dot(wb_ref[...], h1_ref[pl.ds(at, 10 * channels), :], preferred_element_type=f32)
        kept = jnp.dot(wr_ref[...], h0_ref[pl.ds(at + 2 * channels, 8 * channels), :], preferred_element_type=f32)
        total = kept[0:8] + kept[8:16] + (conv[16:24] + conv[24:32])
        total = total + shifted(conv[0:8] + conv[8:16], -1)
        total = total + shifted(conv[32:40] + conv[40:48], 1)
        out_ref[pl.ds(pl.multiple_of(t * 8, 8), 8), :] = total
        return carry

    lax.fori_loop(0, rows // 8, eight, 0)


def data_kernel(spread_ref, offset_ref, cells_in_ref, measured_ref, out_ref, cells_ref, *scratch):
    rows, views, det = measured_ref.shape[1:]
    peers = cells_in_ref.shape[0]
    nx = cells_ref.shape[1]
    chunks = LANES // rows
    depth = rows // chunks
    blocks = nx // LANES
    back_ref, sum_ref = scratch[:2]
    sets = [scratch[2 + 3 * k : 5 + 3 * k] for k in range(2)]

    for tile in range(nx // LANES):
        pieces = []
        for peer in range(tile * chunks, (tile + 1) * chunks):
            got = cells_in_ref[peer].astype(f32)
            pieces += [got[:, k * rows : (k + 1) * rows] for k in range(chunks)]
        cells_ref[:, tile * LANES : (tile + 1) * LANES] = jnp.concatenate(pieces, axis=0).T.astype(bf16)

    back_ref[...] = jnp.zeros_like(back_ref)
    sum_ref[...] = jnp.zeros_like(sum_ref)
    for line_ref, low_ref, _ in sets:
        low_ref[...] = jnp.zeros_like(low_ref)

    lane = lax.broadcasted_iota(jnp.int32, (LANES, 2 * LANES), 1).astype(f32)
    cell = lax.broadcasted_iota(jnp.int32, (LANES, 2 * LANES), 0).astype(f32)

    def window(view, b):
        spread = spread_ref[0, view]
        offset = offset_ref[0, view].astype(f32)
        begin = (det - 1) * 0.5 + (b * LANES - (nx - 1) * 0.5) * spread + offset
        return (begin + LANES).astype(jnp.int32) // LANES * LANES

    def forward(view, line_ref, low_ref, tent_ref):
        spread = spread_ref[0, view]
        offset = offset_ref[0, view].astype(f32)
        line_ref[:, :LANES] = jnp.zeros((rows, LANES), f32)
        line_ref[:, LANES + det :] = jnp.zeros((rows, LANES), f32)
        line_ref[:, LANES : LANES + det] = -measured_ref[0, :, view, :]
        for b in range(blocks):
            first = window(view, b)
            target = (det - 1) * 0.5 + (cell + (b * LANES - (nx - 1) * 0.5)) * spread + offset
            bins = lane + (first - LANES).astype(f32)
            tent = jnp.maximum(0.0, 1.0 - jnp.abs(bins - target)).astype(bf16)
            tent_ref[b] = tent
            at = pl.ds(pl.multiple_of(first, LANES), 2 * LANES)
            line_ref[:, at] += jnp.dot(
                cells_ref[:, b * LANES : (b + 1) * LANES], tent, preferred_element_type=f32
            )
        misfit = line_ref[:, LANES : LANES + det]
        low_ref[:, LANES : LANES + det] = misfit.astype(bf16)
        square = misfit * misfit
        total = square[:, :LANES]
        for k in range(1, det // LANES):
            total = total + square[:, k * LANES : (k + 1) * LANES]
        sum_ref[...] += total

    def backward(view, line_ref, low_ref, tent_ref):
        for b in range(blocks):
            at = pl.ds(pl.multiple_of(window(view, b), LANES), 2 * LANES)
            back_ref[:, b * LANES : (b + 1) * LANES] += lax.dot_general(
                low_ref[:, at], tent_ref[b], (((1,), (1,)), ((), ())), preferred_element_type=f32
            )

    def two(it, carry):
        for k in range(2):
            forward(2 * it + k, *sets[k])
        for k in range(2):
            backward(2 * it + k, *sets[k])
        return carry

    lax.fori_loop(0, views // 2, two, 0)

    whole = jnp.sum(sum_ref[...], keepdims=True)
    high = whole.astype(bf16)
    rest = whole - high.astype(f32)
    middle = rest.astype(bf16)
    final = (rest - middle.astype(f32)).astype(bf16)
    spot = lax.broadcasted_iota(jnp.int32, (out_ref.shape[1] - depth, LANES), 1)
    note = jnp.where(spot == 0, high.astype(f32), 0.0)
    note = jnp.where(spot == 1, middle.astype(f32), note)
    note = jnp.where(spot == 2, final.astype(f32), note).astype(bf16)
    for tile in range(nx // LANES):
        turned = back_ref[:, tile * LANES : (tile + 1) * LANES].T
        for k in range(chunks):
            peer = tile * chunks + k
            own = turned[k * rows : (k + 1) * rows]
            wide = jnp.concatenate([own[i * depth : (i + 1) * depth] for i in range(chunks)], axis=1)
            out_ref[peer, :depth] = wide.astype(bf16)
            out_ref[peer, depth:] = note


def combine_kernel(step_ref, volume_ref, noise_ref, score_ref, back_ref, out_ref, *, count):
    rows, width = score_ref.shape
    peers = back_ref.shape[0]
    chunks = LANES // rows
    depth = rows // chunks
    total = jnp.zeros((1, LANES), f32)
    for peer in range(peers):
        total = total + back_ref[peer, depth : depth + 8].astype(f32)[0:1]
    misfit = jnp.sum(total, keepdims=True)
    step = jnp.full((1, 1), step_ref[0], f32)
    weight = data_gain / jnp.sqrt(misfit / count + 1e-06)
    sway = jnp.sqrt(2.0 * step)
    for tile in range(width // LANES):
        at = slice(tile * LANES, (tile + 1) * LANES)
        got = [back_ref[tile * chunks + k, :depth].astype(f32) for k in range(chunks)]
        back = jnp.concatenate(
            [jnp.concatenate([g[:, k * rows : (k + 1) * rows] for g in got], axis=1) for k in range(chunks)], axis=0
        )
        moved = step * (score_ref[:, at] - weight * back)
        out_ref[0, :, at] = volume_ref[0, :, at] + moved + sway * noise_ref[0, :, at]


def per_device(
    volume,
    noise,
    measured,
    angles,
    offsets,
    step_size,
    lift_w,
    lift_b,
    conv_a,
    bias_a,
    conv_b,
    out_w,
):
    slices, rows, width = volume.shape
    views, det = measured.shape[2:]
    channels = lift_w.shape[0]
    peers = lax.axis_size("slab")
    height = peers * rows
    chunks = LANES // rows
    depth = rows // chunks

    def call(kernel, mebibytes, **kwargs):
        return pl.pallas_call(
            kernel, compiler_params=pltpu.CompilerParams(vmem_limit_bytes=mebibytes << 20), **kwargs
        )

    def spec(shape, dtype):
        return jax.ShapeDtypeStruct(shape, dtype)

    payload, first, last = call(
        pack_kernel,
        2,
        out_shape=(spec((peers, depth, LANES), bf16), spec((2, width), f32), spec((2, width), f32)),
        in_specs=[VMEM],
        out_specs=(VMEM,) * 3,
    )(volume)
    cells = lax.all_to_all(payload, "slab", 0, 0)
    low = lax.ppermute(last, "slab", [(i, i + 1) for i in range(peers - 1)])
    high = lax.ppermute(first, "slab", [(i + 1, i) for i in range(peers - 1)])

    def line(array):
        return array.reshape(1, -1)

    wa, wb, wr, lift, bias, spread = call(
        prep_kernel,
        4,
        out_shape=(
            spec((2 * channels, 12 * channels), bf16),
            spec((48, 10 * channels), bf16),
            spec((16, 8 * channels), bf16),
            spec((2, channels, LANES), f32),
            spec((2 * channels, LANES), f32),
            spec((1, views), f32),
        ),
        in_specs=[VMEM] * 7,
        out_specs=(VMEM,) * 6,
    )(line(angles), line(lift_w), line(lift_b), conv_a, line(bias_a), conv_b, line(out_w))

    anchor = (lax.axis_index("slab") * rows).astype(jnp.int32).reshape(1)
    ring = pltpu.VMEM((3, 2 * channels, width), bf16)
    score = call(
        functools.partial(score_kernel, height=height),
        28,
        out_shape=spec((rows, width), f32),
        in_specs=[SMEM] + [VMEM] * 8,
        out_specs=VMEM,
        scratch_shapes=[
            pltpu.VMEM((rows + 16, width), f32),
            ring,
            ring,
            ring,
            pltpu.VMEM(((rows + 6) * channels, width), bf16),
            pltpu.VMEM(((rows + 2) * channels, width), bf16),
        ],
    )(anchor, low, volume, high, lift, bias, wa, wb, wr)

    nx = height
    wide = det + 2 * LANES
    lines = [
        pltpu.VMEM((rows, wide), f32),
        pltpu.VMEM((rows, wide), bf16),
        pltpu.VMEM((nx // LANES, LANES, 2 * LANES), bf16),
    ]
    sent = call(
        data_kernel,
        12,
        out_shape=spec((peers, depth + 8, LANES), bf16),
        in_specs=[SMEM] * 2 + [VMEM] * 2,
        out_specs=VMEM,
        scratch_shapes=[
            pltpu.VMEM((rows, nx), bf16),
            pltpu.VMEM((rows, nx), f32),
            pltpu.VMEM((rows, LANES), f32),
            *lines,
            *lines,
        ],
    )(spread, line(offsets), cells, measured)
    returned = lax.all_to_all(sent, "slab", 0, 0)
    return call(
        functools.partial(combine_kernel, count=slices * peers * rows * views * det),
        3,
        out_shape=spec(volume.shape, f32),
        in_specs=[SMEM] + [VMEM] * 4,
        out_specs=VMEM,
    )(step_size, volume, noise, score, returned)


def solution(mesh):
    placed = (
        P("groups", "slab", None),
        P("groups", "slab", None),
        P("groups", "slab", None, None),
        P("groups"),
        P("groups"),
        P("groups"),
        P(),
        P(),
        P(),
        P(),
        P(),
        P(),
    )
    return jax.shard_map(
        per_device, mesh=mesh, in_specs=placed, out_specs=P("groups", "slab", None), check_vma=False
    )
```

time: 842 us -> 61.8 us (0.07)
  the two profiles are of different devices: /device:TPU:0 before, /device:TPU:7 now
where the time goes in v1:
time: 61.8 us; the launch traced here: 61.3 us
  Pallas kernels  30.5 us (49%)
  starting transfers between devices  17.5 us (28%)
  local copies, waits for them, and re-layouts  8.89 us (14%)
  waiting for transfers between devices  3.76 us (6%)
  between operations  0.72 us (1%)
    pallas_call x1, Pallas kernels, per_device(): call(functools.partial(score_kernel, height=height), 28, out_shape=spec((...  17 us
    pallas_call x1, Pallas kernels, per_device(): call(data_kernel, 12, out_shape=spec((peers, depth + 8, LANES), bf16), in...  11.5 us
    unnamed x24, local copies, waits for them, and re-layouts  8.89 us
    all_to_all x1, starting transfers between devices, per_device(): cells = lax.all_to_all(payload, 'slab', 0, 0)  6.63 us
    all_to_all x1, starting transfers between devices, per_device(): returned = lax.all_to_all(sent, 'slab', 0, 0)  5.56 us
    ppermute x1, starting transfers between devices, per_device(): low = lax.ppermute(last, 'slab', [(i, i + 1) for i in range(peers - 1)])  3.36 us
    ppermute x1, waiting for transfers between devices, per_device(): high = lax.ppermute(first, 'slab', [(i + 1, i) for i in range(peers - 1)])  3.28 us
    ppermute x1, starting transfers between devices, per_device(): high = lax.ppermute(first, 'slab', [(i + 1, i) for i in range(peers - 1)])  1.92 us
  transfers between devices with their start and end apart: 4, of which 2 were waited for; matrix products, arithmetic and copies ran while one was open for 0% of the time, Pallas kernels for 28%

profile of v1, /device:TPU:7, one launch (start us, length us, event | category | flops | bytes accessed | tf_op | source)
XLA Modules:
  0.0 61.3 jit_solution(8963362498830600016)
XLA Ops:
  0.0 0.9 %copy-done.1 = f32[1,64,1024]{2,1,0:T(8,128)S(1)} copy-done((f32[1,64,1024]{2,1,0:T(8,128)S(1)}, f32[1,64,1024]{2,1,0:T(8,128)}, u32[]{:S(2)}) %copy-start.1) | copy-done | bytes 262168
  1.0 0.8 %shard_map.118 = (bf16[16,32,128]{2,1,0:T(8,128)(2,1)}, f32[2,1024]{1,0:T(2,128)S(1)}, f32[2,1024]{1,0:T(2,128)S(1)}) custom-call(f32[1,64,1024]{2,1,0:T(8,128)S(1)} %copy-done.1), custom_call_target="tpu_custom_call" | custom-call | tf_op jit(solution)/shard_map/pallas_call | solution.py:318
  1.7 6.6 %all-to-all-start = ((bf16[16,32,128]{2,1,0:T(8,128)(2,1)}), bf16[16,32,128]{2,1,0:T(8,128)(2,1)S(1)}, u32[]{:S(2)}, u32[]{:S(2)}) async-start(bf16[16,32,128]{2,1,0:T(8,128)(2,1)} %get-tuple-element.22), calls=%async_computation | async-start | bytes 262144 | tf_op jit(solution)/shard_map/all_to_all | solution.py:325
  8.4 0.9 %copy-done.4 = bf16[9,64,64]{2,1,0:T(8,128)(2,1)S(1)} copy-done((bf16[9,64,64]{2,1,0:T(8,128)(2,1)S(1)}, bf16[9,64,64]{2,1,0:T(8,128)(2,1)}, u32[]{:S(2)}) %copy-start.4) | copy-done | bytes 73752
  9.3 0.9 %copy-done.5 = bf16[9,64,64]{2,1,0:T(8,128)(2,1)S(1)} copy-done((bf16[9,64,64]{2,1,0:T(8,128)(2,1)S(1)}, bf16[9,64,64]{2,1,0:T(8,128)(2,1)}, u32[]{:S(2)}) %copy-start.5) | copy-done | bytes 73752
  10.2 0.7 %copy-done.6 = s32[16]{0:T(128)S(1)} copy-done((s32[16]{0:T(128)S(1)}, s32[16]{0:T(128)}, u32[]{:S(2)}) %copy-start.6) | copy-done | bytes 88
  10.8 0.7 %copy-done.7 = f32[64]{0:T(128)S(1)} copy-done((f32[64]{0:T(128)S(1)}, f32[64]{0:T(128)}, u32[]{:S(2)}) %copy-start.7) | copy-done | bytes 280
  11.5 0.7 %copy-done.8 = f32[64]{0:T(128)S(1)} copy-done((f32[64]{0:T(128)S(1)}, f32[64]{0:T(128)}, u32[]{:S(2)}) %copy-start.8) | copy-done | bytes 280
  12.1 0.7 %copy-done.9 = f32[64]{0:T(128)S(1)} copy-done((f32[64]{0:T(128)S(1)}, f32[64]{0:T(128)}, u32[]{:S(2)}) %copy-start.9) | copy-done | bytes 280
  12.8 0.7 %copy-done.10 = f32[64]{0:T(128)S(1)} copy-done((f32[64]{0:T(128)S(1)}, f32[64]{0:T(128)}, u32[]{:S(2)}) %copy-start.10) | copy-done | bytes 280
  13.4 0.3 shard_map.119
  13.8 0.5 all-to-all-done.cells_in_ref
  14.2 2.2 %copy-done = f32[1,64,16,1024]{3,2,1,0:T(8,128)S(1)} copy-done((f32[1,64,16,1024]{3,2,1,0:T(8,128)S(1)}, f32[1,64,16,1024]{3,2,1,0:T(8,128)}, u32[]{:S(2)}) %copy-start) | copy-done | bytes 4194328
  16.4 0.7 %copy-done.11 = s32[16]{0:T(128)S(1)} copy-done((s32[16]{0:T(128)S(1)}, s32[16]{0:T(128)}, u32[]{:S(2)}) %copy-start.11) | copy-done | bytes 88
  17.1 11.5 %shard_map.121 = bf16[16,40,128]{2,1,0:T(8,128)(2,1)} custom-call(f32[1,16]{1,0:T(1,128)S(1)} %get-tuple-element.21.spread_ref, s32[1,16]{1,0:T(1,128)S(1)} %bitcast.12, bf16[16,32,128]{2,1,0:T(8,128)(2,1)S(1)} %all-to-all-done.cells_in_ref, f32[1,64,16,1024]{3,2,1,0:T(8,128)S(1)} %copy-done), custom_call_target="tpu_custom_call" | custom-call | tf_op jit(solution)/shard_map/pallas_call | solution.py:372
  28.6 5.6 %all-to-all-start.1 = ((bf16[16,40,128]{2,1,0:T(8,128)(2,1)}), bf16[16,40,128]{2,1,0:T(8,128)(2,1)S(1)}, u32[]{:S(2)}, u32[]{:S(2)}) async-start(bf16[16,40,128]{2,1,0:T(8,128)(2,1)} %shard_map.121), calls=%async_computation.1 | async-start | bytes 327680 | tf_op jit(solution)/shard_map/all_to_all | solution.py:386
  34.2 3.4 %collective-permute-start = (f32[2,1024]{1,0:T(2,128)S(1)}, f32[2,1024]{1,0:T(2,128)S(1)}, u32[]{:S(2)}, u32[]{:S(2)}) collective-permute-start(f32[2,1024]{1,0:T(2,128)S(1)} %get-tuple-element.14), channel_id=1, source_target_pairs={{0,1},{1,2},{2,3},{3,4},{4,5},{5,6},{6,7},{7,8},{8,9},{9,10},{10,1... | collective-permute-start | bytes 24584 | tf_op jit(solution)/shard_map/ppermute | solution.py:326
  37.6 1.9 %collective-permute-start.1 = (f32[2,1024]{1,0:T(2,128)S(1)}, f32[2,1024]{1,0:T(2,128)S(1)}, u32[]{:S(2)}, u32[]{:S(2)}) collective-permute-start(f32[2,1024]{1,0:T(2,128)S(1)} %get-tuple-element.15), channel_id=1, source_target_pairs={{1,0},{2,1},{3,2},{4,3},{5,4},{6,5},{7,6},{8,7},{9,8},{10,9},{11,1... | collective-permute-start | bytes 24584 | tf_op jit(solution)/shard_map/ppermute | solution.py:327
  40.1 0.0 collective-permute-done.low_ref
  40.1 3.3 %collective-permute-done.1.high_ref = f32[2,1024]{1,0:T(2,128)S(1)} collective-permute-done((f32[2,1024]{1,0:T(2,128)S(1)}, f32[2,1024]{1,0:T(2,128)S(1)}, u32[]{:S(2)}, u32[]{:S(2)}) %collective-permute-start.1) | collective-permute-done | bytes 8224 | tf_op jit(solution)/shard_map/ppermute | solution.py:327
  43.4 0.0 copy-done.2
  43.4 17.0 %shard_map.120.score_ref = f32[64,1024]{1,0:T(8,128)S(1)} custom-call(s32[1]{0:T(128)} %bitcast.anchor_ref, f32[2,1024]{1,0:T(2,128)S(1)} %collective-permute-done.low_ref, f32[1,64,1024]{2,1,0:T(8,128)S(1)} %copy-done.2, f32[2,1024]{1,0:T(2,128)S(1)} %collective-permute-done.1.high_ref, f32[2,64,128]{2,1,0:T(8,128)S(1)} %get-tuple-element.16.lift_ref, ...), custom_call_target="tpu_custom_call" | custom-call | tf_op jit(solution)/shard_map/pallas_call | solution.py:349
  60.4 0.0 all-to-all-done.1.back_ref
  60.4 0.9 %shard_map.122 = f32[1,64,1024]{2,1,0:T(8,128)} custom-call(f32[1]{0:T(128)S(6)} %copy.13.step_ref, f32[1,64,1024]{2,1,0:T(8,128)S(1)} %copy-done.2, f32[1,64,1024]{2,1,0:T(8,128)S(1)} %copy-done.3, f32[64,1024]{1,0:T(8,128)S(1)} %shard_map.120.score_ref, bf16[16,40,128]{2,1,0:T(8,128)(2,1)S(1)} %all-to-all-done.1.back_ref), custom_call_target="tpu_custom_call" | custom-call | tf_op jit(solution)/shard_map/pallas_call | solution.py:387
  (13 shorter events, 0.0 us)
Async XLA Ops:
  0.0 0.9 %copy-start.1 = (f32[1,64,1024]{2,1,0:T(8,128)S(1)}, f32[1,64,1024]{2,1,0:T(8,128)}, u32[]{:S(2)}) copy-start(f32[1,64,1024]{2,1,0:T(8,128)} %volume_ref.5) | copy-start | bytes 786436
  1.0 42.5 %copy-start.2 = (f32[1,64,1024]{2,1,0:T(8,128)S(1)}, f32[1,64,1024]{2,1,0:T(8,128)}, u32[]{:S(2)}) copy-start(f32[1,64,1024]{2,1,0:T(8,128)} %volume_ref.5) | copy-start | bytes 786436
  1.0 59.5 %copy-start.3 = (f32[1,64,1024]{2,1,0:T(8,128)S(1)}, f32[1,64,1024]{2,1,0:T(8,128)}, u32[]{:S(2)}) copy-start(f32[1,64,1024]{2,1,0:T(8,128)} %noise_ref.1) | copy-start | bytes 786436
  1.7 12.5 %all-to-all-start = ((bf16[16,32,128]{2,1,0:T(8,128)(2,1)}), bf16[16,32,128]{2,1,0:T(8,128)(2,1)S(1)}, u32[]{:S(2)}, u32[]{:S(2)}) async-start(bf16[16,32,128]{2,1,0:T(8,128)(2,1)} %get-tuple-element.22), calls=%async_computation | async-start | bytes 262144 | tf_op jit(solution)/shard_map/all_to_all | solution.py:325
  8.3 0.9 %copy-start.4 = (bf16[9,64,64]{2,1,0:T(8,128)(2,1)S(1)}, bf16[9,64,64]{2,1,0:T(8,128)(2,1)}, u32[]{:S(2)}) copy-start(bf16[9,64,64]{2,1,0:T(8,128)(2,1)} %conv_a_ref.1) | copy-start | bytes 221188
  9.3 0.9 %copy-start.5 = (bf16[9,64,64]{2,1,0:T(8,128)(2,1)S(1)}, bf16[9,64,64]{2,1,0:T(8,128)(2,1)}, u32[]{:S(2)}) copy-start(bf16[9,64,64]{2,1,0:T(8,128)(2,1)} %conv_b_ref.1) | copy-start | bytes 221188
  10.2 0.7 %copy-start.6 = (s32[16]{0:T(128)S(1)}, s32[16]{0:T(128)}, u32[]{:S(2)}) copy-start(s32[16]{0:T(128)} %param.15) | copy-start | bytes 196
  10.8 0.7 %copy-start.7 = (f32[64]{0:T(128)S(1)}, f32[64]{0:T(128)}, u32[]{:S(2)}) copy-start(f32[64]{0:T(128)} %param.18) | copy-start | bytes 772
  11.5 0.7 %copy-start.8 = (f32[64]{0:T(128)S(1)}, f32[64]{0:T(128)}, u32[]{:S(2)}) copy-start(f32[64]{0:T(128)} %param.19) | copy-start | bytes 772
  12.1 0.7 %copy-start.9 = (f32[64]{0:T(128)S(1)}, f32[64]{0:T(128)}, u32[]{:S(2)}) copy-start(f32[64]{0:T(128)} %param.21) | copy-start | bytes 772
  12.8 0.7 %copy-start.10 = (f32[64]{0:T(128)S(1)}, f32[64]{0:T(128)}, u32[]{:S(2)}) copy-start(f32[64]{0:T(128)} %param.23) | copy-start | bytes 772
  14.2 2.2 %copy-start = (f32[1,64,16,1024]{3,2,1,0:T(8,128)S(1)}, f32[1,64,16,1024]{3,2,1,0:T(8,128)}, u32[]{:S(2)}) copy-start(f32[1,64,16,1024]{3,2,1,0:T(8,128)} %measured_ref.1) | copy-start | bytes 12582916
  16.4 0.7 %copy-start.11 = (s32[16]{0:T(128)S(1)}, s32[16]{0:T(128)}, u32[]{:S(2)}) copy-start(s32[16]{0:T(128)} %param.16) | copy-start | bytes 196
  28.6 31.8 %all-to-all-start.1 = ((bf16[16,40,128]{2,1,0:T(8,128)(2,1)}), bf16[16,40,128]{2,1,0:T(8,128)(2,1)S(1)}, u32[]{:S(2)}, u32[]{:S(2)}) async-start(bf16[16,40,128]{2,1,0:T(8,128)(2,1)} %shard_map.121), calls=%async_computation.1 | async-start | bytes 327680 | tf_op jit(solution)/shard_map/all_to_all | solution.py:386
  34.2 6.0 %collective-permute-start = (f32[2,1024]{1,0:T(2,128)S(1)}, f32[2,1024]{1,0:T(2,128)S(1)}, u32[]{:S(2)}, u32[]{:S(2)}) collective-permute-start(f32[2,1024]{1,0:T(2,128)S(1)} %get-tuple-element.14), channel_id=1, source_target_pairs={{0,1},{1,2},{2,3},{3,4},{4,5},{5,6},{6,7},{7,8},{8,9},{9,10},{10,1... | collective-permute-start | bytes 24584 | tf_op jit(solution)/shard_map/ppermute | solution.py:326
  37.6 5.9 %collective-permute-start.1 = (f32[2,1024]{1,0:T(2,128)S(1)}, f32[2,1024]{1,0:T(2,128)S(1)}, u32[]{:S(2)}, u32[]{:S(2)}) collective-permute-start(f32[2,1024]{1,0:T(2,128)S(1)} %get-tuple-element.15), channel_id=1, source_target_pairs={{1,0},{2,1},{3,2},{4,3},{5,4},{6,5},{7,6},{8,7},{9,8},{10,9},{11,1... | collective-permute-start | bytes 24584 | tf_op jit(solution)/shard_map/ppermute | solution.py:327

commit v2 on v1

--- a/solution.py
+++ b/solution.py
@@ -7,6 +7,7 @@
 from jax.experimental.pallas import tpu as pltpu
 from jax.sharding import PartitionSpec as P
 
+
 ANGLES = 180
 LANES = 128
 
@@ -16,6 +17,7 @@
 bf16 = jnp.bfloat16
 VMEM = pl.BlockSpec(memory_space=pltpu.VMEM)
 SMEM = pl.BlockSpec(memory_space=pltpu.SMEM)
+HBM = pl.BlockSpec(memory_space=pltpu.HBM)
 
 
 def pack_kernel(volume_ref, out_ref, first_ref, last_ref):
@@ -36,10 +38,17 @@
     return high, (value - high).astype(bf16).astype(f32)
 
 
-def prep_kernel(
-    angles_ref, gain_ref, base_ref, conv_a_ref, bias_ref, conv_b_ref, own_ref,
-    wa_ref, wb_ref, wr_ref, lift_ref, shift_ref, spread_ref,
-):
+def prep_kernel(*refs):
+    sources, (wa_ref, wb_ref, wr_ref, lift_ref, shift_ref, spread_ref) = refs[:7], refs[7:13]
+    held, sems = refs[13:20], refs[20]
+    copies = [
+        pltpu.make_async_copy(source, target, sems.at[k]) for k, (source, target) in enumerate(zip(sources, held))
+    ]
+    for copy in copies:
+        copy.start()
+    for copy in copies:
+        copy.wait()
+    angles_ref, gain_ref, base_ref, conv_a_ref, bias_ref, conv_b_ref, own_ref = held
     channels = conv_a_ref.shape[1]
 
     def column(row):
@@ -175,13 +184,20 @@
 
 def data_kernel(spread_ref, offset_ref, cells_in_ref, measured_ref, out_ref, cells_ref, *scratch):
     rows, views, det = measured_ref.shape[1:]
-    peers = cells_in_ref.shape[0]
     nx = cells_ref.shape[1]
     chunks = LANES // rows
     depth = rows // chunks
     blocks = nx // LANES
-    back_ref, sum_ref = scratch[:2]
-    sets = [scratch[2 + 3 * k : 5 + 3 * k] for k in range(2)]
+    back_ref, sum_ref, seen_ref, sems = scratch[:4]
+    sets = [scratch[4 + 3 * k : 7 + 3 * k] for k in range(2)]
+    part = views // 2
+
+    def fetch(k):
+        span = pl.ds(k * part, part)
+        return pltpu.make_async_copy(measured_ref.at[0, :, span], seen_ref.at[:, span], sems.at[k])
+
+    fetch(0).start()
+    fetch(1).start()
 
     for tile in range(nx // LANES):
         pieces = []
@@ -209,7 +225,7 @@
         offset = offset_ref[0, view].astype(f32)
         line_ref[:, :LANES] = jnp.zeros((rows, LANES), f32)
         line_ref[:, LANES + det :] = jnp.zeros((rows, LANES), f32)
-        line_ref[:, LANES : LANES + det] = -measured_ref[0, :, view, :]
+        line_ref[:, LANES : LANES + det] = -seen_ref[:, view, :]
         for b in range(blocks):
             first = window(view, b)
             target = (det - 1) * 0.5 + (cell + (b * LANES - (nx - 1) * 0.5)) * spread + offset
@@ -242,7 +258,10 @@
             backward(2 * it + k, *sets[k])
         return carry
 
-    lax.fori_loop(0, views // 2, two, 0)
+    fetch(0).wait()
+    lax.fori_loop(0, views // 4, two, 0)
+    fetch(1).wait()
+    lax.fori_loop(views // 4, views // 2, two, 0)
 
     whole = jnp.sum(sum_ref[...], keepdims=True)
     high = whole.astype(bf16)
@@ -329,9 +348,10 @@
     def line(array):
         return array.reshape(1, -1)
 
+    small = (line(angles), line(lift_w), line(lift_b), conv_a, line(bias_a), conv_b, line(out_w))
     wa, wb, wr, lift, bias, spread = call(
         prep_kernel,
-        4,
+        6,
         out_shape=(
             spec((2 * channels, 12 * channels), bf16),
             spec((48, 10 * channels), bf16),
@@ -340,9 +360,35 @@
             spec((2 * channels, LANES), f32),
             spec((1, views), f32),
         ),
-        in_specs=[VMEM] * 7,
+        in_specs=[HBM] * 7,
         out_specs=(VMEM,) * 6,
-    )(line(angles), line(lift_w), line(lift_b), conv_a, line(bias_a), conv_b, line(out_w))
+        scratch_shapes=[pltpu.VMEM(a.shape, a.dtype) for a in small] + [pltpu.SemaphoreType.DMA((7,))],
+    )(*[pltpu.with_memory_space_constraint(a, pltpu.HBM) for a in small])
+
+    nx = height
+    wide = det + 2 * LANES
+    lines = [
+        pltpu.VMEM((rows, wide), f32),
+        pltpu.VMEM((rows, wide), bf16),
+        pltpu.VMEM((nx // LANES, LANES, 2 * LANES), bf16),
+    ]
+    sent = call(
+        data_kernel,
+        12,
+        out_shape=spec((peers, depth + 8, LANES), bf16),
+        in_specs=[SMEM] * 2 + [VMEM, HBM],
+        out_specs=VMEM,
+        scratch_shapes=[
+            pltpu.VMEM((rows, nx), bf16),
+            pltpu.VMEM((rows, nx), f32),
+            pltpu.VMEM((rows, LANES), f32),
+            pltpu.VMEM((rows, views, det), f32),
+            pltpu.SemaphoreType.DMA((2,)),
+            *lines,
+            *lines,
+        ],
+    )(spread, pltpu.with_memory_space_constraint(line(offsets), pltpu.HBM), cells, pltpu.with_memory_space_constraint(measured, pltpu.HBM))
+    returned = lax.all_to_all(sent, "slab", 0, 0)
 
     anchor = (lax.axis_index("slab") * rows).astype(jnp.int32).reshape(1)
     ring = pltpu.VMEM((3, 2 * channels, width), bf16)
@@ -361,29 +407,6 @@
             pltpu.VMEM(((rows + 2) * channels, width), bf16),
         ],
     )(anchor, low, volume, high, lift, bias, wa, wb, wr)
-
-    nx = height
-    wide = det + 2 * LANES
-    lines = [
-        pltpu.VMEM((rows, wide), f32),
-        pltpu.VMEM((rows, wide), bf16),
-        pltpu.VMEM((nx // LANES, LANES, 2 * LANES), bf16),
-    ]
-    sent = call(
-        data_kernel,
-        12,
-        out_shape=spec((peers, depth + 8, LANES), bf16),
-        in_specs=[SMEM] * 2 + [VMEM] * 2,
-        out_specs=VMEM,
-        scratch_shapes=[
-            pltpu.VMEM((rows, nx), bf16),
-            pltpu.VMEM((rows, nx), f32),
-            pltpu.VMEM((rows, LANES), f32),
-            *lines,
-            *lines,
-        ],
-    )(spread, line(offsets), cells, measured)
-    returned = lax.all_to_all(sent, "slab", 0, 0)
     return call(
         functools.partial(combine_kernel, count=slices * peers * rows * views * det),
         3,

time: 61.8 us -> 60.5 us (0.979)
  local copies, waits for them, and re-layouts: 8.89 us -> 0.96 us
  waiting for transfers between devices: 3.76 us -> 7.76 us
  Pallas kernels: 30.5 us -> 33.3 us
    unnamed x24 -> x6, local copies, waits for them, and re-layouts: 8.89 us -> 0.96 us
    all_to_all x1, waiting for transfers between devices: 0.48 us -> 4.47 us  [per_device(): cells = lax.all_to_all(payload, 'slab', 0, 0)]
    pallas_call x1, Pallas kernels: 11.5 us -> 13.3 us  [per_device(): call(data_kernel, 12, out_shape=spec((peers, depth + 8, LANES), bf16), in...]
    pallas_call x1, Pallas kernels: 0.31 us -> 1.41 us  [per_device(): call(prep_kernel, 6, out_shape=(spec((2 * channels, 12 * channels), bf16)...]
  transfers between devices with their start and end apart: 4 -> 4, of which waited for: 2 -> 2; matrix products, arithmetic and copies ran while one was open for 0% -> 0% of each run, Pallas kernels for 28% -> 31%
where the time goes in v2:
time: 60.5 us; the launch traced here: 60.1 us
  Pallas kernels  33.3 us (55%)
  starting transfers between devices  17.4 us (29%)
  waiting for transfers between devices  7.76 us (13%)
  local copies, waits for them, and re-layouts  0.96 us (2%)
  between operations  0.71 us (1%)
    pallas_call x1, Pallas kernels, per_device(): call(functools.partial(score_kernel, height=height), 28, out_shape=spec((...  17 us
    pallas_call x1, Pallas kernels, per_device(): call(data_kernel, 12, out_shape=spec((peers, depth + 8, LANES), bf16), in...  13.3 us
    all_to_all x1, starting transfers between devices, per_device(): cells = lax.all_to_all(payload, 'slab', 0, 0)  6.63 us
    all_to_all x1, starting transfers between devices, per_device(): returned = lax.all_to_all(sent, 'slab', 0, 0)  5.44 us
    all_to_all x1, waiting for transfers between devices, per_device(): cells = lax.all_to_all(payload, 'slab', 0, 0)  4.47 us
    ppermute x1, starting transfers between devices, per_device(): low = lax.ppermute(last, 'slab', [(i, i + 1) for i in range(peers - 1)])  3.37 us
    ppermute x1, waiting for transfers between devices, per_device(): high = lax.ppermute(first, 'slab', [(i + 1, i) for i in range(peers - 1)])  3.28 us
    ppermute x1, starting transfers between devices, per_device(): high = lax.ppermute(first, 'slab', [(i + 1, i) for i in range(peers - 1)])  1.92 us
  transfers between devices with their start and end apart: 4, of which 2 were waited for; matrix products, arithmetic and copies ran while one was open for 0% of the time, Pallas kernels for 31%

profile of v2, /device:TPU:7, one launch (start us, length us, event | category | flops | bytes accessed | tf_op | source)
XLA Modules:
  0.0 60.1 jit_solution(13713707982432880356)
XLA Ops:
  0.0 0.0 copy-start
  0.0 0.9 %copy-done = f32[1,64,1024]{2,1,0:T(8,128)S(1)} copy-done((f32[1,64,1024]{2,1,0:T(8,128)S(1)}, f32[1,64,1024]{2,1,0:T(8,128)}, u32[]{:S(2)}) %copy-start) | copy-done | bytes 262168
  1.0 0.0 copy-start.1
  1.0 0.0 copy-start.2
  1.0 0.8 %shard_map.118 = (bf16[16,32,128]{2,1,0:T(8,128)(2,1)}, f32[2,1024]{1,0:T(2,128)S(1)}, f32[2,1024]{1,0:T(2,128)S(1)}) custom-call(f32[1,64,1024]{2,1,0:T(8,128)S(1)} %copy-done), custom_call_target="tpu_custom_call" | custom-call | tf_op jit(solution)/shard_map/pallas_call | solution.py:337
  1.7 6.6 %all-to-all-start = ((bf16[16,32,128]{2,1,0:T(8,128)(2,1)}), bf16[16,32,128]{2,1,0:T(8,128)(2,1)S(1)}, u32[]{:S(2)}, u32[]{:S(2)}) async-start(bf16[16,32,128]{2,1,0:T(8,128)(2,1)} %get-tuple-element.22), calls=%async_computation | async-start | bytes 262144 | tf_op jit(solution)/shard_map/all_to_all | solution.py:344
  8.3 1.4 %shard_map.119 = (bf16[128,768]{1,0:T(8,128)(2,1)S(1)}, bf16[48,640]{1,0:T(8,128)(2,1)S(1)}, bf16[16,512]{1,0:T(8,128)(2,1)S(1)}, f32[2,64,128]{2,1,0:T(8,128)S(...) custom-call(s32[1,16]{1,0:T(1,128)} %bitcast.7, f32[1,64]{1,0:T(1,128)} %bitcast.8, f32[1,64]{1,0:T(1,128)} %bitcast.9, ...), custom_call_target="tpu_custom_call" | custom-call | tf_op jit(solution)/shard_map/pallas_call | solution.py:352
  9.8 4.5 %all-to-all-done.cells_in_ref = bf16[16,32,128]{2,1,0:T(8,128)(2,1)S(1)} async-done(((bf16[16,32,128]{2,1,0:T(8,128)(2,1)}), bf16[16,32,128]{2,1,0:T(8,128)(2,1)S(1)}, u32[]{:S(2)}, u32[]{:S(2)}) %all-to-all-start) | async-done | bytes 131104 | tf_op jit(solution)/shard_map/all_to_all | solution.py:344
  14.2 13.3 %shard_map.121 = bf16[16,40,128]{2,1,0:T(8,128)(2,1)} custom-call(f32[1,16]{1,0:T(1,128)S(1)} %get-tuple-element.21.spread_ref, s32[1,16]{1,0:T(1,128)} %bitcast.12, bf16[16,32,128]{2,1,0:T(8,128)(2,1)S(1)} %all-to-all-done.cells_in_ref, f32[1,64,16,1024]{3,2,1,0:T(8,128)} %measured_ref.1), custom_call_target="tpu_custom_call" | custom-call | tf_op jit(solution)/shard_map/pallas_call | solution.py:375
  27.5 5.4 %all-to-all-start.1 = ((bf16[16,40,128]{2,1,0:T(8,128)(2,1)}), bf16[16,40,128]{2,1,0:T(8,128)(2,1)S(1)}, u32[]{:S(2)}, u32[]{:S(2)}) async-start(bf16[16,40,128]{2,1,0:T(8,128)(2,1)} %shard_map.121), calls=%async_computation.1 | async-start | bytes 327680 | tf_op jit(solution)/shard_map/all_to_all | solution.py:391
  32.9 3.4 %collective-permute-start = (f32[2,1024]{1,0:T(2,128)S(1)}, f32[2,1024]{1,0:T(2,128)S(1)}, u32[]{:S(2)}, u32[]{:S(2)}) collective-permute-start(f32[2,1024]{1,0:T(2,128)S(1)} %get-tuple-element.14), channel_id=1, source_target_pairs={{0,1},{1,2},{2,3},{3,4},{4,5},{5,6},{6,7},{7,8},{8,9},{9,10},{10,1... | collective-permute-start | bytes 24584 | tf_op jit(solution)/shard_map/ppermute | solution.py:345
  36.3 1.9 %collective-permute-start.1 = (f32[2,1024]{1,0:T(2,128)S(1)}, f32[2,1024]{1,0:T(2,128)S(1)}, u32[]{:S(2)}, u32[]{:S(2)}) collective-permute-start(f32[2,1024]{1,0:T(2,128)S(1)} %get-tuple-element.15), channel_id=1, source_target_pairs={{1,0},{2,1},{3,2},{4,3},{5,4},{6,5},{7,6},{8,7},{9,8},{10,9},{11,1... | collective-permute-start | bytes 24584 | tf_op jit(solution)/shard_map/ppermute | solution.py:346
  38.9 0.0 collective-permute-done.low_ref
  38.9 3.3 %collective-permute-done.1.high_ref = f32[2,1024]{1,0:T(2,128)S(1)} collective-permute-done((f32[2,1024]{1,0:T(2,128)S(1)}, f32[2,1024]{1,0:T(2,128)S(1)}, u32[]{:S(2)}, u32[]{:S(2)}) %collective-permute-start.1) | collective-permute-done | bytes 8224 | tf_op jit(solution)/shard_map/ppermute | solution.py:346
  42.2 0.0 copy-done.1
  42.2 17.0 %shard_map.120.score_ref = f32[64,1024]{1,0:T(8,128)S(1)} custom-call(s32[1]{0:T(128)} %bitcast.anchor_ref, f32[2,1024]{1,0:T(2,128)S(1)} %collective-permute-done.low_ref, f32[1,64,1024]{2,1,0:T(8,128)S(1)} %copy-done.1, f32[2,1024]{1,0:T(2,128)S(1)} %collective-permute-done.1.high_ref, f32[2,64,128]{2,1,0:T(8,128)S(1)} %get-tuple-element.16.lift_ref, ...), custom_call_target="tpu_custom_call" | custom-call | tf_op jit(solution)/shard_map/pallas_call | solution.py:395
  59.2 0.0 all-to-all-done.1.back_ref
  59.2 0.0 copy-done.2
  59.2 0.9 %shard_map.122 = f32[1,64,1024]{2,1,0:T(8,128)} custom-call(f32[1]{0:T(128)S(6)} %copy.13.step_ref, f32[1,64,1024]{2,1,0:T(8,128)S(1)} %copy-done.1, f32[1,64,1024]{2,1,0:T(8,128)S(1)} %copy-done.2, f32[64,1024]{1,0:T(8,128)S(1)} %shard_map.120.score_ref, bf16[16,40,128]{2,1,0:T(8,128)(2,1)S(1)} %all-to-all-done.1.back_ref), custom_call_target="tpu_custom_call" | custom-call | tf_op jit(solution)/shard_map/pallas_call | solution.py:410
Async XLA Ops:
  0.0 0.9 %copy-start = (f32[1,64,1024]{2,1,0:T(8,128)S(1)}, f32[1,64,1024]{2,1,0:T(8,128)}, u32[]{:S(2)}) copy-start(f32[1,64,1024]{2,1,0:T(8,128)} %volume_ref.5) | copy-start | bytes 786436
  1.0 41.2 %copy-start.1 = (f32[1,64,1024]{2,1,0:T(8,128)S(1)}, f32[1,64,1024]{2,1,0:T(8,128)}, u32[]{:S(2)}) copy-start(f32[1,64,1024]{2,1,0:T(8,128)} %volume_ref.5) | copy-start | bytes 786436
  1.0 58.2 %copy-start.2 = (f32[1,64,1024]{2,1,0:T(8,128)S(1)}, f32[1,64,1024]{2,1,0:T(8,128)}, u32[]{:S(2)}) copy-start(f32[1,64,1024]{2,1,0:T(8,128)} %noise_ref.1) | copy-start | bytes 786436
  1.7 12.5 %all-to-all-start = ((bf16[16,32,128]{2,1,0:T(8,128)(2,1)}), bf16[16,32,128]{2,1,0:T(8,128)(2,1)S(1)}, u32[]{:S(2)}, u32[]{:S(2)}) async-start(bf16[16,32,128]{2,1,0:T(8,128)(2,1)} %get-tuple-element.22), calls=%async_computation | async-start | bytes 262144 | tf_op jit(solution)/shard_map/all_to_all | solution.py:344
  27.5 31.7 %all-to-all-start.1 = ((bf16[16,40,128]{2,1,0:T(8,128)(2,1)}), bf16[16,40,128]{2,1,0:T(8,128)(2,1)S(1)}, u32[]{:S(2)}, u32[]{:S(2)}) async-start(bf16[16,40,128]{2,1,0:T(8,128)(2,1)} %shard_map.121), calls=%async_computation.1 | async-start | bytes 327680 | tf_op jit(solution)/shard_map/all_to_all | solution.py:391
  32.9 6.0 %collective-permute-start = (f32[2,1024]{1,0:T(2,128)S(1)}, f32[2,1024]{1,0:T(2,128)S(1)}, u32[]{:S(2)}, u32[]{:S(2)}) collective-permute-start(f32[2,1024]{1,0:T(2,128)S(1)} %get-tuple-element.14), channel_id=1, source_target_pairs={{0,1},{1,2},{2,3},{3,4},{4,5},{5,6},{6,7},{7,8},{8,9},{9,10},{10,1... | collective-permute-start | bytes 24584 | tf_op jit(solution)/shard_map/ppermute | solution.py:345
  36.3 5.9 %collective-permute-start.1 = (f32[2,1024]{1,0:T(2,128)S(1)}, f32[2,1024]{1,0:T(2,128)S(1)}, u32[]{:S(2)}, u32[]{:S(2)}) collective-permute-start(f32[2,1024]{1,0:T(2,128)S(1)} %get-tuple-element.15), channel_id=1, source_target_pairs={{1,0},{2,1},{3,2},{4,3},{5,4},{6,5},{7,6},{8,7},{9,8},{10,9},{11,1... | collective-permute-start | bytes 24584 | tf_op jit(solution)/shard_map/ppermute | solution.py:346

commit v3 on v2

--- a/solution.py
+++ b/solution.py
@@ -182,86 +182,89 @@
     lax.fori_loop(0, rows // 8, eight, 0)
 
 
-def data_kernel(spread_ref, offset_ref, cells_in_ref, measured_ref, out_ref, cells_ref, *scratch):
+def data_kernel(spread_ref, offset_ref, cells_in_ref, measured_ref, out_ref, cells_ref, back_ref, sum_ref, bin_ref, line_ref, sems, *scratch):
     rows, views, det = measured_ref.shape[1:]
     nx = cells_ref.shape[1]
     chunks = LANES // rows
     depth = rows // chunks
     blocks = nx // LANES
-    back_ref, sum_ref, seen_ref, sems = scratch[:4]
-    sets = [scratch[4 + 3 * k : 7 + 3 * k] for k in range(2)]
-    part = views // 2
-
-    def fetch(k):
-        span = pl.ds(k * part, part)
-        return pltpu.make_async_copy(measured_ref.at[0, :, span], seen_ref.at[:, span], sems.at[k])
-
-    fetch(0).start()
-    fetch(1).start()
+    sets = [scratch[2 * k : 2 * k + 2] for k in range(len(scratch) // 2)]
+    body = slice(LANES, LANES + det)
+
+    def fetch(view):
+        return pltpu.make_async_copy(measured_ref.at[0, :, view], line_ref.at[view, :, body], sems.at[view])
+
+    for view in range(views):
+        fetch(view).start()
 
     for tile in range(nx // LANES):
         pieces = []
         for peer in range(tile * chunks, (tile + 1) * chunks):
             got = cells_in_ref[peer].astype(f32)
             pieces += [got[:, k * rows : (k + 1) * rows] for k in range(chunks)]
-        cells_ref[:, tile * LANES : (tile + 1) * LANES] = jnp.concatenate(pieces, axis=0).T.astype(bf16)
+        cells_ref[:, tile * LANES : (tile + 1) * LANES] = (-jnp.concatenate(pieces, axis=0).T).astype(bf16)
 
     back_ref[...] = jnp.zeros_like(back_ref)
     sum_ref[...] = jnp.zeros_like(sum_ref)
-    for line_ref, low_ref, _ in sets:
+    bin_ref[...] = lax.broadcasted_iota(jnp.int32, bin_ref.shape, 0).astype(jnp.int16)
+    line_ref[:, :, :LANES] = jnp.zeros((views, rows, LANES), f32)
+    line_ref[:, :, LANES + det :] = jnp.zeros((views, rows, LANES), f32)
+    for low_ref, _ in sets:
         low_ref[...] = jnp.zeros_like(low_ref)
 
-    lane = lax.broadcasted_iota(jnp.int32, (LANES, 2 * LANES), 1).astype(f32)
-    cell = lax.broadcasted_iota(jnp.int32, (LANES, 2 * LANES), 0).astype(f32)
-
-    def window(view, b):
+    cell = lax.broadcasted_iota(jnp.int32, (16, LANES), 1).astype(f32)
+
+    def forward(view, low_ref, tent_ref):
         spread = spread_ref[0, view]
         offset = offset_ref[0, view].astype(f32)
-        begin = (det - 1) * 0.5 + (b * LANES - (nx - 1) * 0.5) * spread + offset
-        return (begin + LANES).astype(jnp.int32) // LANES * LANES
-
-    def forward(view, line_ref, low_ref, tent_ref):
-        spread = spread_ref[0, view]
-        offset = offset_ref[0, view].astype(f32)
-        line_ref[:, :LANES] = jnp.zeros((rows, LANES), f32)
-        line_ref[:, LANES + det :] = jnp.zeros((rows, LANES), f32)
-        line_ref[:, LANES : LANES + det] = -seen_ref[:, view, :]
+        windows = []
         for b in range(blocks):
-            first = window(view, b)
-            target = (det - 1) * 0.5 + (cell + (b * LANES - (nx - 1) * 0.5)) * spread + offset
-            bins = lane + (first - LANES).astype(f32)
-            tent = jnp.maximum(0.0, 1.0 - jnp.abs(bins - target)).astype(bf16)
+            begin = (det - 1) * 0.5 + (b * LANES - (nx - 1) * 0.5) * spread + offset
+            first = jnp.floor(begin * (1.0 / LANES))
+            at = pl.ds(pl.multiple_of((first.astype(jnp.int32) + 1) * LANES, LANES), 2 * LANES)
+            windows.append(at)
+            target = cell * spread + (begin - first * LANES)
+            under = jnp.floor(target)
+            near = (1.0 - (target - under)).astype(bf16)
+            far = (1.0 - ((under + 1.0) - target)).astype(bf16)
+            spot = under.astype(jnp.int32)
+            this = jnp.concatenate([spot.astype(jnp.int16)] * 16, axis=0)
+            after = jnp.concatenate([(spot + 1).astype(jnp.int16)] * 16, axis=0)
+            near = jnp.concatenate([near] * 16, axis=0)
+            far = jnp.concatenate([far] * 16, axis=0)
+            bins = bin_ref[...]
+            tent = jnp.where(bins == this, near, jnp.where(bins == after, far, jnp.zeros_like(far)))
             tent_ref[b] = tent
-            at = pl.ds(pl.multiple_of(first, LANES), 2 * LANES)
-            line_ref[:, at] += jnp.dot(
-                cells_ref[:, b * LANES : (b + 1) * LANES], tent, preferred_element_type=f32
+            line_ref[view, :, at] += lax.dot_general(
+                cells_ref[:, b * LANES : (b + 1) * LANES],
+                tent,
+                (((1,), (1,)), ((), ())),
+                preferred_element_type=f32,
             )
-        misfit = line_ref[:, LANES : LANES + det]
-        low_ref[:, LANES : LANES + det] = misfit.astype(bf16)
+        misfit = line_ref[view, :, body]
+        low_ref[:, body] = misfit.astype(bf16)
         square = misfit * misfit
         total = square[:, :LANES]
         for k in range(1, det // LANES):
             total = total + square[:, k * LANES : (k + 1) * LANES]
         sum_ref[...] += total
-
-    def backward(view, line_ref, low_ref, tent_ref):
-        for b in range(blocks):
-            at = pl.ds(pl.multiple_of(window(view, b), LANES), 2 * LANES)
-            back_ref[:, b * LANES : (b + 1) * LANES] += lax.dot_general(
-                low_ref[:, at], tent_ref[b], (((1,), (1,)), ((), ())), preferred_element_type=f32
+        return windows
+
+    def backward(windows, low_ref, tent_ref):
+        for b, at in enumerate(windows):
+            back_ref[:, b * LANES : (b + 1) * LANES] += jnp.dot(
+                low_ref[:, at], tent_ref[b], preferred_element_type=f32
             )
 
-    def two(it, carry):
-        for k in range(2):
-            forward(2 * it + k, *sets[k])
-        for k in range(2):
-            backward(2 * it + k, *sets[k])
+    def several(it, carry):
+        for k in range(len(sets)):
+            fetch(len(sets) * it + k).wait()
+        windows = [forward(len(sets) * it + k, *sets[k]) for k in range(len(sets))]
+        for k in range(len(sets)):
+            backward(windows[k], *sets[k])
         return carry
 
-    fetch(0).wait()
-    lax.fori_loop(0, views // 4, two, 0)
-    fetch(1).wait()
-    lax.fori_loop(views // 4, views // 2, two, 0)
+    lax.fori_loop(0, views // len(sets), several, 0)
 
     whole = jnp.sum(sum_ref[...], keepdims=True)
     high = whole.astype(bf16)
@@ -300,7 +303,7 @@
         back = jnp.concatenate(
             [jnp.concatenate([g[:, k * rows : (k + 1) * rows] for g in got], axis=1) for k in range(chunks)], axis=0
         )
-        moved = step * (score_ref[:, at] - weight * back)
+        moved = step * (score_ref[:, at] + weight * back)
         out_ref[0, :, at] = volume_ref[0, :, at] + moved + sway * noise_ref[0, :, at]
 
 
@@ -368,9 +371,8 @@
     nx = height
     wide = det + 2 * LANES
     lines = [
-        pltpu.VMEM((rows, wide), f32),
         pltpu.VMEM((rows, wide), bf16),
-        pltpu.VMEM((nx // LANES, LANES, 2 * LANES), bf16),
+        pltpu.VMEM((nx // LANES, 2 * LANES, LANES), bf16),
     ]
     sent = call(
         data_kernel,
@@ -382,8 +384,9 @@
             pltpu.VMEM((rows, nx), bf16),
             pltpu.VMEM((rows, nx), f32),
             pltpu.VMEM((rows, LANES), f32),
-            pltpu.VMEM((rows, views, det), f32),
-            pltpu.SemaphoreType.DMA((2,)),
+            pltpu.VMEM((2 * LANES, LANES), jnp.int16),
+            pltpu.VMEM((views, rows, wide), f32),
+            pltpu.SemaphoreType.DMA((views,)),
             *lines,
             *lines,
         ],

time: 60.5 us -> 57.3 us (0.947)
  the two profiles are of different devices: /device:TPU:7 before, /device:TPU:5 now
where the time goes in v3:
time: 57.3 us; the launch traced here: 56.8 us
  Pallas kernels  30 us (52%)
  starting transfers between devices  17.4 us (30%)
  waiting for transfers between devices  7.76 us (14%)
  local copies, waits for them, and re-layouts  0.96 us (2%)
  between operations  0.71 us (1%)
    pallas_call x1, Pallas kernels, per_device(): call(functools.partial(score_kernel, height=height), 28, out_shape=spec((...  17 us
    pallas_call x1, Pallas kernels, per_device(): call(data_kernel, 12, out_shape=spec((peers, depth + 8, LANES), bf16), in...  9.98 us
    all_to_all x1, starting transfers between devices, per_device(): cells = lax.all_to_all(payload, 'slab', 0, 0)  6.63 us
    all_to_all x1, starting transfers between devices, per_device(): returned = lax.all_to_all(sent, 'slab', 0, 0)  5.44 us
    all_to_all x1, waiting for transfers between devices, per_device(): cells = lax.all_to_all(payload, 'slab', 0, 0)  4.47 us
    ppermute x1, starting transfers between devices, per_device(): low = lax.ppermute(last, 'slab', [(i, i + 1) for i in range(peers - 1)])  3.37 us
    ppermute x1, waiting for transfers between devices, per_device(): high = lax.ppermute(first, 'slab', [(i + 1, i) for i in range(peers - 1)])  3.28 us
    ppermute x1, starting transfers between devices, per_device(): high = lax.ppermute(first, 'slab', [(i + 1, i) for i in range(peers - 1)])  1.92 us
  transfers between devices with their start and end apart: 4, of which 2 were waited for; matrix products, arithmetic and copies ran while one was open for 0% of the time, Pallas kernels for 32%

profile of v3, /device:TPU:5, one launch (start us, length us, event | category | flops | bytes accessed | tf_op | source)
XLA Modules:
  0.0 56.8 jit_solution(8942932559246321901)
XLA Ops:
  0.0 0.0 copy-start
  0.0 0.9 %copy-done = f32[1,64,1024]{2,1,0:T(8,128)S(1)} copy-done((f32[1,64,1024]{2,1,0:T(8,128)S(1)}, f32[1,64,1024]{2,1,0:T(8,128)}, u32[]{:S(2)}) %copy-start) | copy-done | bytes 262168
  1.0 0.0 copy-start.1
  1.0 0.0 copy-start.2
  1.0 0.8 %shard_map.118 = (bf16[16,32,128]{2,1,0:T(8,128)(2,1)}, f32[2,1024]{1,0:T(2,128)S(1)}, f32[2,1024]{1,0:T(2,128)S(1)}) custom-call(f32[1,64,1024]{2,1,0:T(8,128)S(1)} %copy-done), custom_call_target="tpu_custom_call" | custom-call | tf_op jit(solution)/shard_map/pallas_call | solution.py:340
  1.7 6.6 %all-to-all-start = ((bf16[16,32,128]{2,1,0:T(8,128)(2,1)}), bf16[16,32,128]{2,1,0:T(8,128)(2,1)S(1)}, u32[]{:S(2)}, u32[]{:S(2)}) async-start(bf16[16,32,128]{2,1,0:T(8,128)(2,1)} %get-tuple-element.22), calls=%async_computation | async-start | bytes 262144 | tf_op jit(solution)/shard_map/all_to_all | solution.py:347
  8.3 1.4 %shard_map.119 = (bf16[128,768]{1,0:T(8,128)(2,1)S(1)}, bf16[48,640]{1,0:T(8,128)(2,1)S(1)}, bf16[16,512]{1,0:T(8,128)(2,1)S(1)}, f32[2,64,128]{2,1,0:T(8,128)S(...) custom-call(s32[1,16]{1,0:T(1,128)} %bitcast.7, f32[1,64]{1,0:T(1,128)} %bitcast.8, f32[1,64]{1,0:T(1,128)} %bitcast.9, ...), custom_call_target="tpu_custom_call" | custom-call | tf_op jit(solution)/shard_map/pallas_call | solution.py:355
  9.8 4.5 %all-to-all-done.cells_in_ref = bf16[16,32,128]{2,1,0:T(8,128)(2,1)S(1)} async-done(((bf16[16,32,128]{2,1,0:T(8,128)(2,1)}), bf16[16,32,128]{2,1,0:T(8,128)(2,1)S(1)}, u32[]{:S(2)}, u32[]{:S(2)}) %all-to-all-start) | async-done | bytes 131104 | tf_op jit(solution)/shard_map/all_to_all | solution.py:347
  14.2 10.0 %shard_map.121 = bf16[16,40,128]{2,1,0:T(8,128)(2,1)} custom-call(f32[1,16]{1,0:T(1,128)S(1)} %get-tuple-element.21.spread_ref, s32[1,16]{1,0:T(1,128)} %bitcast.12, bf16[16,32,128]{2,1,0:T(8,128)(2,1)S(1)} %all-to-all-done.cells_in_ref, f32[1,64,16,1024]{3,2,1,0:T(8,128)} %measured_ref.1), custom_call_target="tpu_custom_call" | custom-call | tf_op jit(solution)/shard_map/pallas_call | solution.py:377
  24.2 5.4 %all-to-all-start.1 = ((bf16[16,40,128]{2,1,0:T(8,128)(2,1)}), bf16[16,40,128]{2,1,0:T(8,128)(2,1)S(1)}, u32[]{:S(2)}, u32[]{:S(2)}) async-start(bf16[16,40,128]{2,1,0:T(8,128)(2,1)} %shard_map.121), calls=%async_computation.1 | async-start | bytes 327680 | tf_op jit(solution)/shard_map/all_to_all | solution.py:394
  29.7 3.4 %collective-permute-start = (f32[2,1024]{1,0:T(2,128)S(1)}, f32[2,1024]{1,0:T(2,128)S(1)}, u32[]{:S(2)}, u32[]{:S(2)}) collective-permute-start(f32[2,1024]{1,0:T(2,128)S(1)} %get-tuple-element.14), channel_id=1, source_target_pairs={{0,1},{1,2},{2,3},{3,4},{4,5},{5,6},{6,7},{7,8},{8,9},{9,10},{10,1... | collective-permute-start | bytes 24584 | tf_op jit(solution)/shard_map/ppermute | solution.py:348
  33.0 1.9 %collective-permute-start.1 = (f32[2,1024]{1,0:T(2,128)S(1)}, f32[2,1024]{1,0:T(2,128)S(1)}, u32[]{:S(2)}, u32[]{:S(2)}) collective-permute-start(f32[2,1024]{1,0:T(2,128)S(1)} %get-tuple-element.15), channel_id=1, source_target_pairs={{1,0},{2,1},{3,2},{4,3},{5,4},{6,5},{7,6},{8,7},{9,8},{10,9},{11,1... | collective-permute-start | bytes 24584 | tf_op jit(solution)/shard_map/ppermute | solution.py:349
  35.6 0.0 collective-permute-done.low_ref
  35.6 3.3 %collective-permute-done.1.high_ref = f32[2,1024]{1,0:T(2,128)S(1)} collective-permute-done((f32[2,1024]{1,0:T(2,128)S(1)}, f32[2,1024]{1,0:T(2,128)S(1)}, u32[]{:S(2)}, u32[]{:S(2)}) %collective-permute-start.1) | collective-permute-done | bytes 8224 | tf_op jit(solution)/shard_map/ppermute | solution.py:349
  38.9 0.0 copy-done.1
  38.9 17.0 %shard_map.120.score_ref = f32[64,1024]{1,0:T(8,128)S(1)} custom-call(s32[1]{0:T(128)} %bitcast.anchor_ref, f32[2,1024]{1,0:T(2,128)S(1)} %collective-permute-done.low_ref, f32[1,64,1024]{2,1,0:T(8,128)S(1)} %copy-done.1, f32[2,1024]{1,0:T(2,128)S(1)} %collective-permute-done.1.high_ref, f32[2,64,128]{2,1,0:T(8,128)S(1)} %get-tuple-element.16.lift_ref, ...), custom_call_target="tpu_custom_call" | custom-call | tf_op jit(solution)/shard_map/pallas_call | solution.py:398
  55.9 0.0 all-to-all-done.1.back_ref
  55.9 0.0 copy-done.2
  55.9 0.9 %shard_map.122 = f32[1,64,1024]{2,1,0:T(8,128)} custom-call(f32[1]{0:T(128)S(6)} %copy.13.step_ref, f32[1,64,1024]{2,1,0:T(8,128)S(1)} %copy-done.1, f32[1,64,1024]{2,1,0:T(8,128)S(1)} %copy-done.2, f32[64,1024]{1,0:T(8,128)S(1)} %shard_map.120.score_ref, bf16[16,40,128]{2,1,0:T(8,128)(2,1)S(1)} %all-to-all-done.1.back_ref), custom_call_target="tpu_custom_call" | custom-call | tf_op jit(solution)/shard_map/pallas_call | solution.py:413
Async XLA Ops:
  0.0 0.9 %copy-start = (f32[1,64,1024]{2,1,0:T(8,128)S(1)}, f32[1,64,1024]{2,1,0:T(8,128)}, u32[]{:S(2)}) copy-start(f32[1,64,1024]{2,1,0:T(8,128)} %volume_ref.5) | copy-start | bytes 786436
  1.0 38.0 %copy-start.1 = (f32[1,64,1024]{2,1,0:T(8,128)S(1)}, f32[1,64,1024]{2,1,0:T(8,128)}, u32[]{:S(2)}) copy-start(f32[1,64,1024]{2,1,0:T(8,128)} %volume_ref.5) | copy-start | bytes 786436
  1.0 55.0 %copy-start.2 = (f32[1,64,1024]{2,1,0:T(8,128)S(1)}, f32[1,64,1024]{2,1,0:T(8,128)}, u32[]{:S(2)}) copy-start(f32[1,64,1024]{2,1,0:T(8,128)} %noise_ref.1) | copy-start | bytes 786436
  1.7 12.5 %all-to-all-start = ((bf16[16,32,128]{2,1,0:T(8,128)(2,1)}), bf16[16,32,128]{2,1,0:T(8,128)(2,1)S(1)}, u32[]{:S(2)}, u32[]{:S(2)}) async-start(bf16[16,32,128]{2,1,0:T(8,128)(2,1)} %get-tuple-element.22), calls=%async_computation | async-start | bytes 262144 | tf_op jit(solution)/shard_map/all_to_all | solution.py:347
  24.2 31.7 %all-to-all-start.1 = ((bf16[16,40,128]{2,1,0:T(8,128)(2,1)}), bf16[16,40,128]{2,1,0:T(8,128)(2,1)S(1)}, u32[]{:S(2)}, u32[]{:S(2)}) async-start(bf16[16,40,128]{2,1,0:T(8,128)(2,1)} %shard_map.121), calls=%async_computation.1 | async-start | bytes 327680 | tf_op jit(solution)/shard_map/all_to_all | solution.py:394
  29.7 6.0 %collective-permute-start = (f32[2,1024]{1,0:T(2,128)S(1)}, f32[2,1024]{1,0:T(2,128)S(1)}, u32[]{:S(2)}, u32[]{:S(2)}) collective-permute-start(f32[2,1024]{1,0:T(2,128)S(1)} %get-tuple-element.14), channel_id=1, source_target_pairs={{0,1},{1,2},{2,3},{3,4},{4,5},{5,6},{6,7},{7,8},{8,9},{9,10},{10,1... | collective-permute-start | bytes 24584 | tf_op jit(solution)/shard_map/ppermute | solution.py:348
  33.0 5.9 %collective-permute-start.1 = (f32[2,1024]{1,0:T(2,128)S(1)}, f32[2,1024]{1,0:T(2,128)S(1)}, u32[]{:S(2)}, u32[]{:S(2)}) collective-permute-start(f32[2,1024]{1,0:T(2,128)S(1)} %get-tuple-element.15), channel_id=1, source_target_pairs={{1,0},{2,1},{3,2},{4,3},{5,4},{6,5},{7,6},{8,7},{9,8},{10,9},{11,1... | collective-permute-start | bytes 24584 | tf_op jit(solution)/shard_map/ppermute | solution.py:349

commit v4 on v3

v4 whole, which is shorter than its diff:
```python
import functools

import jax
import jax.numpy as jnp
from jax import lax
from jax.experimental import pallas as pl
from jax.experimental.pallas import tpu as pltpu
from jax.sharding import PartitionSpec as P


ANGLES = 180
LANES = 128
GROUP = 16

data_gain = 0.25

f32 = jnp.float32
bf16 = jnp.bfloat16
VMEM = pl.BlockSpec(memory_space=pltpu.VMEM)
SMEM = pl.BlockSpec(memory_space=pltpu.SMEM)
HBM = pl.BlockSpec(memory_space=pltpu.HBM)


def split(value, pieces=2):
    parts = []
    for _ in range(pieces):
        parts.append(value.astype(bf16).astype(f32))
        value = value - parts[-1]
    return parts


def pack_kernel(volume_ref, out_ref):
    rows = volume_ref.shape[1]
    peers = out_ref.shape[0]
    chunks = LANES // rows
    depth = rows // chunks
    edge = jnp.concatenate([volume_ref[0, :2], volume_ref[0, rows - 2 :]], axis=0)
    _, middle, final = split(edge, 3)
    blank = [jnp.zeros((4, LANES - 2 * rows), f32)] if 2 * rows < LANES else []
    none = jnp.zeros((4, LANES), f32)
    for peer in range(peers):
        at = slice(peer * rows, (peer + 1) * rows)
        piece = volume_ref[0, :, at]
        wide = jnp.concatenate([piece[k * depth : (k + 1) * depth] for k in range(chunks)], axis=1)
        out_ref[peer, :depth] = wide.astype(bf16)
        lower = jnp.concatenate([middle[:, at], final[:, at]] + blank, axis=1)
        out_ref[peer, depth:] = jnp.concatenate([lower, none], axis=0).astype(bf16)


def prep_kernel(*refs):
    sources, (wa_ref, wb_ref, wr_ref, lift_ref, shift_ref, spread_ref) = refs[:7], refs[7:13]
    held, sems = refs[13:20], refs[20]
    copies = [
        pltpu.make_async_copy(source, target, sems.at[k]) for k, (source, target) in enumerate(zip(sources, held))
    ]
    for copy in copies:
        copy.start()
    for copy in copies:
        copy.wait()
    angles_ref, gain_ref, base_ref, conv_a_ref, bias_ref, conv_b_ref, own_ref = held
    channels = conv_a_ref.shape[1]

    def column(row):
        return jnp.broadcast_to(row, (LANES, channels)).T

    lift_ref[0] = column(0.5 * gain_ref[...])
    lift_ref[1] = column(0.5 * base_ref[...])
    shift = column(0.5 * bias_ref[...])
    shift_ref[:channels] = shift
    shift_ref[channels:] = shift

    taps = [conv_a_ref[t].astype(f32) * 0.5 for t in range(9)]
    zero = jnp.zeros((channels, channels), f32)
    for r in range(2):
        for j in range(3):
            for e in range(0, 4, 2):
                pair = [taps[3 * (k - r) + j] if 0 <= k - r < 3 else zero for k in (e, e + 1)]
                at = (4 * j + e) * channels
                wa_ref[r * channels : (r + 1) * channels, at : at + 2 * channels] = jnp.concatenate(
                    pair, axis=1
                ).astype(bf16)

    own = column(own_ref[...])[:, :channels]
    row = lax.broadcasted_iota(jnp.int32, (GROUP, LANES), 0)
    half = lax.broadcasted_iota(jnp.int32, (GROUP, LANES), 1) // channels

    def both(line):
        return jnp.broadcast_to(jnp.concatenate([line, line], axis=1), (GROUP, LANES))

    folded = [split(jnp.sum(own * conv_b_ref[t].astype(f32), axis=0, keepdims=True)) for t in range(9)]
    mine = split(own_ref[...])
    for q in range(GROUP // 2 + 1):
        at = slice(q * LANES, (q + 1) * LANES)
        for j in range(3):
            for s in range(2):
                block = jnp.zeros((GROUP, LANES), f32)
                for i in range(3):
                    block = jnp.where(half + 2 * q - row == i, both(folded[3 * i + j][s]), block)
                first = (2 * j + s) * GROUP
                wb_ref[first : first + GROUP, at] = block.astype(bf16)
        if q < GROUP // 2:
            for s in range(2):
                block = jnp.where(half + 2 * q == row, both(mine[s]), 0.0)
                wr_ref[s * GROUP : (s + 1) * GROUP, at] = block.astype(bf16)

    level = jnp.abs(jnp.cos(jnp.pi * angles_ref[...].astype(f32) / ANGLES))
    spread_ref[...] = 0.6 + 0.4 * level


def shifted(block, step):
    width = block.shape[1]
    moved = pltpu.roll(block, (-step) % width, 1)
    lane = lax.broadcasted_iota(jnp.int32, (block.shape[0], LANES), 1)
    if step < 0:
        edge = jnp.where(lane == 0, jnp.zeros_like(moved[:, :LANES]), moved[:, :LANES])
        return jnp.concatenate([edge, moved[:, LANES:]], axis=1)
    edge = jnp.where(lane == LANES - 1, jnp.zeros_like(moved[:, -LANES:]), moved[:, -LANES:])
    return jnp.concatenate([moved[:, :-LANES], edge], axis=1)


def lifted(line, lift_ref, ring, at, kept_ref=None, kept_at=None, keep=None):
    channels = lift_ref.shape[1]
    tiles = line.shape[1] // LANES
    for c in range(0, channels, 16):
        gain, base = lift_ref[0, c : c + 16], lift_ref[1, c : c + 16]
        if keep is not None:
            gain, base = gain * keep, base * keep
        z = jnp.concatenate([gain] * tiles, axis=1) * line + jnp.concatenate([base] * tiles, axis=1)
        h = (z * jnp.tanh(z) + z).astype(bf16)
        ring[0, at + c : at + c + 16] = shifted(h, -1)
        ring[1, at + c : at + c + 16] = h
        ring[2, at + c : at + c + 16] = shifted(h, 1)
        if kept_ref is not None:
            kept_ref[pl.ds(pl.multiple_of(kept_at + c, 16), 16), :] = h


def convolved(p0, p1, wa_ref, bias_ref, store):
    width = p0.shape[2]
    for n in range(0, width, 256):
        rhs = jnp.concatenate([r[j, :, n : n + 256] for j in range(3) for r in (p0, p1)], axis=0)
        acc = jnp.dot(wa_ref[...], rhs, preferred_element_type=f32)
        z = acc + jnp.concatenate([bias_ref[...]] * 2, axis=1)
        store(slice(n, n + 256), (z * jnp.tanh(z) + z).astype(bf16))


def projected(h1, h0, wb_ref, wr_ref):
    conv = jnp.dot(wb_ref[:, : h1.shape[0]], h1, preferred_element_type=f32)
    kept = jnp.dot(wr_ref[:, : h0.shape[0]], h0, preferred_element_type=f32)
    taps = [conv[2 * j * GROUP : (2 * j + 1) * GROUP] + conv[(2 * j + 1) * GROUP : (2 * j + 2) * GROUP] for j in range(3)]
    total = kept[:GROUP] + kept[GROUP:] + taps[1]
    return total + shifted(taps[0], -1) + shifted(taps[2], 1)


def score_kernel(*refs, begin, count):
    given, refs = refs[: 1 if begin else 0], refs[1 if begin else 0 :]
    volume_ref, lift_ref, bias_ref, wa_ref, wb_ref, wr_ref, out_ref, edge_ref = refs[:8]
    last_ref, refs = (refs[8], refs[9:]) if not begin else (None, refs[8:])
    ring_a, ring_b, ring_c, h0_ref, h1_ref = refs
    rings = (ring_a, ring_b, ring_c)
    channels = lift_ref.shape[1]
    lead = 2 * channels if begin else 0

    def lift(pair, ring):
        for k in range(2):
            row = 2 * pair + k
            line = volume_ref[0, pl.ds(2 * begin + row, 1), :]
            lifted(line, lift_ref, ring, k * channels, h0_ref, row * channels)

    def step(g, p0, p1, p2):
        if p2 is not None:
            lift(g + 2, p2)

        def store(at, h):
            h1_ref[pl.ds(pl.multiple_of(lead + g * 2 * channels, 128), 2 * channels), at] = h

        convolved(p0, p1, wa_ref, bias_ref, store)

    lift(0, ring_a)
    lift(1, ring_b)
    if begin:
        h1_ref[:lead] = given[0][...]

    def three(it, carry):
        for k in range(3):
            step(it * 3 + k, *[rings[(k + i) % 3] for i in range(3)])
        return carry

    lax.fori_loop(0, count // 3, three, 0)
    for k in range(count % 3):
        assert k == count % 3 - 1
        step(count - 1, rings[k], rings[k + 1], None)

    low = 2 * begin if begin else 2
    high = 2 * (begin + count)
    for row in range(low, high, GROUP):
        size = min(GROUP, high - row)
        at = (row - low) * channels
        own = (row - 2 * begin) * channels
        total = projected(h1_ref[at : at + (size + 2) * channels], h0_ref[own : own + size * channels], wb_ref, wr_ref)
        out_ref[row : row + size] = total[:size]

    total = (2 * count) * channels + lead
    if begin:
        edge_ref[...] = h1_ref[total - 2 * channels : total]
    else:
        edge_ref[...] = h1_ref[: 2 * channels]
        last_ref[...] = h1_ref[total - 2 * channels : total]


def data_kernel(spread_ref, offset_ref, cells_in_ref, measured_ref, out_ref, cells_ref, back_ref, sum_ref, line_ref, sems, *scratch):
    rows, views, det = measured_ref.shape[1:]
    peers = cells_in_ref.shape[0]
    nx = cells_ref.shape[1]
    chunks = LANES // rows
    depth = rows // chunks
    blocks = nx // LANES
    sets = [scratch[2 * k : 2 * k + 2] for k in range(len(scratch) // 2)]
    body = slice(LANES, LANES + det)

    def fetch(view):
        return pltpu.make_async_copy(measured_ref.at[0, :, view], line_ref.at[view, :, body], sems.at[view])

    for view in range(views):
        fetch(view).start()

    for tile in range(nx // LANES):
        pieces = []
        for peer in range(tile * chunks, (tile + 1) * chunks):
            got = cells_in_ref[peer, :depth].astype(f32)
            pieces += [got[:, k * rows : (k + 1) * rows] for k in range(chunks)]
        cells_ref[:, tile * LANES : (tile + 1) * LANES] = (-jnp.concatenate(pieces, axis=0).T).astype(bf16)

    back_ref[...] = jnp.zeros_like(back_ref)
    sum_ref[...] = jnp.zeros_like(sum_ref)
    line_ref[:, :, :LANES] = jnp.zeros((views, rows, LANES), f32)
    line_ref[:, :, LANES + det :] = jnp.zeros((views, rows, LANES), f32)
    for low_ref, _ in sets:
        low_ref[...] = jnp.zeros_like(low_ref)

    cell = lax.broadcasted_iota(jnp.int32, (16, LANES), 1).astype(f32)
    place = lax.broadcasted_iota(jnp.int32, (16, LANES), 0)
    bins = jnp.concatenate([(place + 16 * k).astype(jnp.int16) for k in range(16)], axis=0)

    def forward(view, low_ref, tent_ref):
        spread = spread_ref[0, view]
        offset = offset_ref[0, view].astype(f32)
        windows = []
        for b in range(blocks):
            begin = (det - 1) * 0.5 + (b * LANES - (nx - 1) * 0.5) * spread + offset
            first = jnp.floor(begin * (1.0 / LANES))
            at = pl.ds(pl.multiple_of((first.astype(jnp.int32) + 1) * LANES, LANES), 2 * LANES)
            windows.append(at)
            target = cell * spread + (begin - first * LANES)
            under = jnp.floor(target)
            near = (1.0 - (target - under)).astype(bf16)
            far = (1.0 - ((under + 1.0) - target)).astype(bf16)
            spot = under.astype(jnp.int32)
            this = jnp.concatenate([spot.astype(jnp.int16)] * 16, axis=0)
            after = jnp.concatenate([(spot + 1).astype(jnp.int16)] * 16, axis=0)
            near = jnp.concatenate([near] * 16, axis=0)
            far = jnp.concatenate([far] * 16, axis=0)
            tent = jnp.where(bins == this, near, jnp.where(bins == after, far, jnp.zeros_like(far)))
            tent_ref[b] = tent
            line_ref[view, :, at] += lax.dot_general(
                cells_ref[:, b * LANES : (b + 1) * LANES],
                tent,
                (((1,), (1,)), ((), ())),
                preferred_element_type=f32,
            )
        misfit = line_ref[view, :, body]
        low_ref[:, body] = misfit.astype(bf16)
        square = misfit * misfit
        total = square[:, :LANES]
        for k in range(1, det // LANES):
            total = total + square[:, k * LANES : (k + 1) * LANES]
        sum_ref[...] += total
        return windows

    def backward(windows, low_ref, tent_ref):
        for b, at in enumerate(windows):
            back_ref[:, b * LANES : (b + 1) * LANES] += jnp.dot(
                low_ref[:, at], tent_ref[b], preferred_element_type=f32
            )

    def several(it, carry):
        for k in range(len(sets)):
            fetch(len(sets) * it + k).wait()
        windows = [forward(len(sets) * it + k, *sets[k]) for k in range(len(sets))]
        for k in range(len(sets)):
            backward(windows[k], *sets[k])
        return carry

    lax.fori_loop(0, views // len(sets), several, 0)

    whole = split(jnp.sum(sum_ref[...], keepdims=True), 3)
    lane = lax.broadcasted_iota(jnp.int32, (8, LANES), 1)
    third = lax.broadcasted_iota(jnp.int32, (8, LANES), 0) == 2
    got = [cells_in_ref[peer].astype(f32) for peer in range(peers)]
    for peer in range(peers):
        low, high = got[max(peer - 1, 0)], got[min(peer + 1, peers - 1)]
        note = jnp.concatenate(
            [low[depth - 2 : depth], high[:2], low[depth + 2 : depth + 4], high[depth : depth + 2]], axis=0
        )
        for k in range(3):
            note = jnp.where(third & (lane == rows + k), whole[k], note)
        out_ref[peer, depth:] = note.astype(bf16)
    for tile in range(nx // LANES):
        turned = back_ref[:, tile * LANES : (tile + 1) * LANES].T
        for k in range(chunks):
            peer = tile * chunks + k
            own = turned[k * rows : (k + 1) * rows]
            wide = jnp.concatenate([own[i * depth : (i + 1) * depth] for i in range(chunks)], axis=1)
            out_ref[peer, :depth] = wide.astype(bf16)


def finish_kernel(
    step_ref, anchor_ref, volume_ref, noise_ref, one_ref, two_ref, back_ref, head_ref, tail_ref, lift_ref, bias_ref,
    wa_ref, wb_ref, wr_ref, out_ref, ext_ref, ring_a, ring_b, h1_ref, score_ref, *, count, height, border,
):
    rows, width = score_ref.shape
    channels = lift_ref.shape[1]
    peers = back_ref.shape[0]
    chunks = LANES // rows
    depth = rows // chunks
    anchor = anchor_ref[0]

    tails = [back_ref[peer, depth:].astype(f32) for peer in range(peers)]
    lane = lax.broadcasted_iota(jnp.int32, (8, LANES), 1)
    third = lax.broadcasted_iota(jnp.int32, (8, LANES), 0) == 2
    total = tails[0]
    for tail in tails[1:]:
        total = total + tail
    misfit = jnp.sum(jnp.where(third & (lane >= rows) & (lane < rows + 3), total, 0.0), keepdims=True)

    ext_ref[2:4] = volume_ref[0, :2]
    ext_ref[8:10] = volume_ref[0, rows - 2 :]
    for tile in range(width // LANES):
        mine = tails[tile * chunks : (tile + 1) * chunks]
        upper = [t[0:2, LANES - rows :] for t in mine], [t[2:4, :rows] for t in mine]
        for side, target in ((0, 0), (1, 10)):
            parts = [upper[side]] + [
                [t[4 + 2 * side : 6 + 2 * side, k * rows : (k + 1) * rows] for t in mine] for k in range(2)
            ]
            parts = [jnp.concatenate(p, axis=1) for p in parts]
            ext_ref[target : target + 2, tile * LANES : (tile + 1) * LANES] = parts[0] + parts[1] + parts[2]

    score_ref[:border] = one_ref[:border]
    score_ref[border:] = two_ref[border:]
    inside = jnp.where(anchor > 0, 1.0, 0.0).astype(f32), jnp.where(anchor + rows < height, 1.0, 0.0).astype(f32)
    for side in range(2):
        for k in range(4):
            line = ext_ref[8 * side + k : 8 * side + k + 1, :]
            halo = (k < 2) == (side == 0)
            ring = (ring_a, ring_b)[k // 2]
            lifted(line, lift_ref, ring, (k % 2) * channels, keep=inside[side] if halo else None)

        def store(at, h):
            h1_ref[2 * channels * side : 2 * channels * (side + 1), at] = h

        convolved(ring_a, ring_b, wa_ref, bias_ref, store)
        if side == 0:
            h1_ref[2 * channels :] = head_ref[...]

            @pl.when(anchor == 0)
            def _():
                h1_ref[:channels] = jnp.zeros((channels, width), bf16)
        else:
            h1_ref[: 2 * channels] = tail_ref[...]

            @pl.when(anchor + rows == height)
            def _():
                h1_ref[3 * channels :] = jnp.zeros((channels, width), bf16)

        scores = projected(h1_ref[...], (ring_b, ring_a)[side][1], wb_ref, wr_ref)
        at = (rows - 2) * side
        score_ref[at : at + 2] = scores[:2]

    step = jnp.full((1, 1), step_ref[0], f32)
    weight = data_gain / jnp.sqrt(misfit / count + 1e-06)
    sway = jnp.sqrt(2.0 * step)
    for tile in range(width // LANES):
        at = slice(tile * LANES, (tile + 1) * LANES)
        got = [back_ref[tile * chunks + k, :depth].astype(f32) for k in range(chunks)]
        back = jnp.concatenate(
            [jnp.concatenate([g[:, k * rows : (k + 1) * rows] for g in got], axis=1) for k in range(chunks)], axis=0
        )
        moved = step * (score_ref[:, at] + weight * back)
        out_ref[0, :, at] = volume_ref[0, :, at] + moved + sway * noise_ref[0, :, at]


def per_device(
    volume,
    noise,
    measured,
    angles,
    offsets,
    step_size,
    lift_w,
    lift_b,
    conv_a,
    bias_a,
    conv_b,
    out_w,
):
    slices, rows, width = volume.shape
    views, det = measured.shape[2:]
    channels = lift_w.shape[0]
    peers = lax.axis_size("slab")
    height = peers * rows
    chunks = LANES // rows
    depth = rows // chunks

    def call(kernel, mebibytes, **kwargs):
        return pl.pallas_call(
            kernel, compiler_params=pltpu.CompilerParams(vmem_limit_bytes=mebibytes << 20), **kwargs
        )

    def spec(shape, dtype):
        return jax.ShapeDtypeStruct(shape, dtype)

    def line(array):
        return array.reshape(1, -1)

    def apart(array):
        return pltpu.with_memory_space_constraint(array, pltpu.HBM)

    nx = height
    wide = det + 2 * LANES
    pairs = rows // 2 - 1
    half = pairs // 6 * 3
    ring = pltpu.VMEM((3, 2 * channels, width), bf16)
    pair = spec((2 * channels, width), bf16)
    anchor = (lax.axis_index("slab") * rows).astype(jnp.int32).reshape(1)
    small = (line(angles), line(lift_w), line(lift_b), conv_a, line(bias_a), conv_b, line(out_w))

    def score_part(begin, count, *args):
        return call(
            functools.partial(score_kernel, begin=begin, count=count),
            20,
            out_shape=(spec((rows, width), f32), pair) + (() if begin else (pair,)),
            in_specs=[VMEM] * len(args),
            out_specs=(VMEM,) * (2 if begin else 3),
            scratch_shapes=[
                ring,
                ring,
                ring,
                pltpu.VMEM(((2 * count + 4) * channels, width), bf16),
                pltpu.VMEM(((2 * count + 2) * channels, width), bf16),
            ],
        )(*args)

    payload = call(
        pack_kernel, 2, out_shape=spec((peers, depth + 8, LANES), bf16), in_specs=[VMEM], out_specs=VMEM
    )(volume)
    cells = lax.all_to_all(payload, "slab", 0, 0)
    wa, wb, wr, lift, bias, spread = call(
        prep_kernel,
        6,
        out_shape=(
            spec((2 * channels, 12 * channels), bf16),
            spec((6 * GROUP, (GROUP + 2) * channels), bf16),
            spec((2 * GROUP, GROUP * channels), bf16),
            spec((2, channels, LANES), f32),
            spec((2 * channels, LANES), f32),
            spec((1, views), f32),
        ),
        in_specs=[HBM] * 7,
        out_specs=(VMEM,) * 6,
        scratch_shapes=[pltpu.VMEM(a.shape, a.dtype) for a in small] + [pltpu.SemaphoreType.DMA((7,))],
    )(*[apart(a) for a in small])
    consts = (lift, bias, wa, wb, wr)
    one, head, middle = score_part(0, half, volume, *consts)

    lines = [
        pltpu.VMEM((rows, wide), bf16),
        pltpu.VMEM((nx // LANES, 2 * LANES, LANES), bf16),
    ]
    sent = call(
        data_kernel,
        12,
        out_shape=spec((peers, depth + 8, LANES), bf16),
        in_specs=[SMEM] * 2 + [VMEM, HBM],
        out_specs=VMEM,
        scratch_shapes=[
            pltpu.VMEM((rows, nx), bf16),
            pltpu.VMEM((rows, nx), f32),
            pltpu.VMEM((rows, LANES), f32),
            pltpu.VMEM((views, rows, wide), f32),
            pltpu.SemaphoreType.DMA((views,)),
            *lines,
            *lines,
        ],
    )(spread, apart(line(offsets)), cells, apart(measured))
    returned = lax.all_to_all(sent, "slab", 0, 0)
    two, tail = score_part(half, pairs - half, middle, volume, *consts)
    return call(
        functools.partial(finish_kernel, count=slices * peers * rows * views * det, height=height, border=2 * half),
        12,
        out_shape=spec(volume.shape, f32),
        in_specs=[SMEM] * 2 + [VMEM] * 12,
        out_specs=VMEM,
        scratch_shapes=[
            pltpu.VMEM((16, width), f32),
            ring,
            ring,
            pltpu.VMEM((4 * channels, width), bf16),
            pltpu.VMEM((rows, width), f32),
        ],
    )(step_size, anchor, volume, noise, one, two, returned, head, tail, *consts)


def solution(mesh):
    placed = (
        P("groups", "slab", None),
        P("groups", "slab", None),
        P("groups", "slab", None, None),
        P("groups"),
        P("groups"),
        P("groups"),
        P(),
        P(),
        P(),
        P(),
        P(),
        P(),
    )
    return jax.shard_map(
        per_device, mesh=mesh, in_specs=placed, out_specs=P("groups", "slab", None), check_vma=False
    )
```

time: 57.3 us -> 50.1 us (0.87)
  the two profiles are of different devices: /device:TPU:5 before, /device:TPU:0 now
where the time goes in v4:
time: 50.1 us; the launch traced here: 49.7 us
  Pallas kernels  30.2 us (60%)
  starting transfers between devices  10.9 us (22%)
  waiting for transfers between devices  6.95 us (14%)
  local copies, waits for them, and re-layouts  0.96 us (2%)
  between operations  0.73 us (1%)
    pallas_call x2, Pallas kernels, score_part(): call(functools.partial(score_kernel, begin=begin, count=count), 20, out_s...  16.1 us
    pallas_call x1, Pallas kernels, per_device(): call(data_kernel, 12, out_shape=spec((peers, depth + 8, LANES), bf16), in...  9.27 us
    all_to_all x1, starting transfers between devices, per_device(): cells = lax.all_to_all(payload, 'slab', 0, 0)  7.41 us
    all_to_all x1, waiting for transfers between devices, per_device(): cells = lax.all_to_all(payload, 'slab', 0, 0)  6.94 us
    all_to_all x1, starting transfers between devices, per_device(): returned = lax.all_to_all(sent, 'slab', 0, 0)  3.53 us
    pallas_call x1, Pallas kernels, per_device(): call(functools.partial(finish_kernel, count=slices * peers * rows * views...  2.52 us
    pallas_call x1, Pallas kernels, per_device(): call(prep_kernel, 6, out_shape=(spec((2 * channels, 12 * channels), bf16)...  1.48 us
  transfers between devices with their start and end apart: 2, of which 1 were waited for; matrix products, arithmetic and copies ran while one was open for 0% of the time, Pallas kernels for 35%

profile of v4, /device:TPU:0, one launch (start us, length us, event | category | flops | bytes accessed | tf_op | source)
XLA Modules:
  0.0 49.7 jit_solution(8320270500977536865)
XLA Ops:
  0.0 0.0 copy-start
  0.0 0.9 %copy-done = f32[1,64,1024]{2,1,0:T(8,128)S(1)} copy-done((f32[1,64,1024]{2,1,0:T(8,128)S(1)}, f32[1,64,1024]{2,1,0:T(8,128)}, u32[]{:S(2)}) %copy-start) | copy-done | bytes 262168
  1.0 0.0 copy-start.1
  1.0 0.0 copy-start.2
  1.0 0.8 %shard_map.121 = bf16[16,40,128]{2,1,0:T(8,128)(2,1)} custom-call(f32[1,64,1024]{2,1,0:T(8,128)S(1)} %copy-done), custom_call_target="tpu_custom_call" | custom-call | tf_op jit(solution)/shard_map/pallas_call | solution.py:452
  1.7 7.4 %all-to-all-start = ((bf16[16,40,128]{2,1,0:T(8,128)(2,1)}), bf16[16,40,128]{2,1,0:T(8,128)(2,1)S(1)}, u32[]{:S(2)}, u32[]{:S(2)}) async-start(bf16[16,40,128]{2,1,0:T(8,128)(2,1)} %shard_map.121), calls=%async_computation | async-start | bytes 327680 | tf_op jit(solution)/shard_map/all_to_all | solution.py:455
  9.2 1.5 %shard_map.118 = (bf16[128,768]{1,0:T(8,128)(2,1)S(1)}, bf16[96,1152]{1,0:T(8,128)(2,1)S(1)}, bf16[32,1024]{1,0:T(8,128)(2,1)S(1)}, f32[2,64,128]{2,1,0:T(8,128)...) custom-call(s32[1,16]{1,0:T(1,128)} %bitcast.7, f32[1,64]{1,0:T(1,128)} %bitcast.8, f32[1,64]{1,0:T(1,128)} %bitcast.9, ...), custom_call_target="tpu_custom_call" | custom-call | tf_op jit(solution)/shard_map/pallas_call | solution.py:456
  10.6 6.9 %all-to-all-done.cells_in_ref = bf16[16,40,128]{2,1,0:T(8,128)(2,1)S(1)} async-done(((bf16[16,40,128]{2,1,0:T(8,128)(2,1)}), bf16[16,40,128]{2,1,0:T(8,128)(2,1)S(1)}, u32[]{:S(2)}, u32[]{:S(2)}) %all-to-all-start) | async-done | bytes 163872 | tf_op jit(solution)/shard_map/all_to_all | solution.py:455
  17.6 9.3 %shard_map.122 = bf16[16,40,128]{2,1,0:T(8,128)(2,1)} custom-call(f32[1,16]{1,0:T(1,128)S(1)} %get-tuple-element.24.spread_ref, s32[1,16]{1,0:T(1,128)} %bitcast.12, bf16[16,40,128]{2,1,0:T(8,128)(2,1)S(1)} %all-to-all-done.cells_in_ref, f32[1,64,16,1024]{3,2,1,0:T(8,128)} %measured_ref.1), custom_call_target="tpu_custom_call" | custom-call | tf_op jit(solution)/shard_map/pallas_call | solution.py:478
  26.9 3.5 %all-to-all-start.1 = ((bf16[16,40,128]{2,1,0:T(8,128)(2,1)}), bf16[16,40,128]{2,1,0:T(8,128)(2,1)S(1)}, u32[]{:S(2)}, u32[]{:S(2)}) async-start(bf16[16,40,128]{2,1,0:T(8,128)(2,1)} %shard_map.122), calls=%async_computation.1 | async-start | bytes 327680 | tf_op jit(solution)/shard_map/all_to_all | solution.py:494
  30.4 0.0 copy-done.1
  30.4 7.9 %shard_map.119 = (f32[64,1024]{1,0:T(8,128)S(1)}, bf16[128,1024]{1,0:T(8,128)(2,1)S(1)}, bf16[128,1024]{1,0:T(8,128)(2,1)S(1)}) custom-call(f32[1,64,1024]{2,1,0:T(8,128)S(1)} %copy-done.1, f32[2,64,128]{2,1,0:T(8,128)S(1)} %get-tuple-element.16.refs_1_.refs_2_.lift_ref, f32[128,128]{1,0:T(8,128)S(1)} %get-tuple-element.17.refs_2_.refs_3_.bias_ref, ...), custom_call_target="tpu_custom_call" | custom-call | tf_op jit(solution)/shard_map/pallas_call | solution.py:437
  38.3 8.3 %shard_map.120 = (f32[64,1024]{1,0:T(8,128)S(1)}, bf16[128,1024]{1,0:T(8,128)(2,1)S(1)}) custom-call(bf16[128,1024]{1,0:T(8,128)(2,1)S(1)} %get-tuple-element.22.refs_0_, f32[1,64,1024]{2,1,0:T(8,128)S(1)} %copy-done.1, f32[2,64,128]{2,1,0:T(8,128)S(1)} %get-tuple-element.16.refs_1_.refs_2_.lift_ref, ...), custom_call_target="tpu_custom_call" | custom-call | tf_op jit(solution)/shard_map/pallas_call | solution.py:437
  47.2 0.0 all-to-all-done.1.back_ref
  47.2 0.0 copy-done.2
  47.2 2.5 %shard_map.123 = f32[1,64,1024]{2,1,0:T(8,128)} custom-call(f32[1]{0:T(128)S(6)} %copy.13.step_ref, s32[1]{0:T(128)} %bitcast.anchor_ref, f32[1,64,1024]{2,1,0:T(8,128)S(1)} %copy-done.1, f32[1,64,1024]{2,1,0:T(8,128)S(1)} %copy-done.2, f32[64,1024]{1,0:T(8,128)S(1)} %get-tuple-element.21.one_ref, f32[64,1024]{1,0:T(8,128)S(1)} %get-tuple-element.23.two_ref, ...), custom_call_target="tpu_custom_call" | custom-call | tf_op jit(solution)/shard_map/pallas_call | solution.py:496
Async XLA Ops:
  0.0 0.9 %copy-start = (f32[1,64,1024]{2,1,0:T(8,128)S(1)}, f32[1,64,1024]{2,1,0:T(8,128)}, u32[]{:S(2)}) copy-start(f32[1,64,1024]{2,1,0:T(8,128)} %volume_ref.3) | copy-start | bytes 786436
  1.0 29.5 %copy-start.1 = (f32[1,64,1024]{2,1,0:T(8,128)S(1)}, f32[1,64,1024]{2,1,0:T(8,128)}, u32[]{:S(2)}) copy-start(f32[1,64,1024]{2,1,0:T(8,128)} %volume_ref.3) | copy-start | bytes 786436
  1.0 46.3 %copy-start.2 = (f32[1,64,1024]{2,1,0:T(8,128)S(1)}, f32[1,64,1024]{2,1,0:T(8,128)}, u32[]{:S(2)}) copy-start(f32[1,64,1024]{2,1,0:T(8,128)} %noise_ref.1) | copy-start | bytes 786436
  1.7 15.9 %all-to-all-start = ((bf16[16,40,128]{2,1,0:T(8,128)(2,1)}), bf16[16,40,128]{2,1,0:T(8,128)(2,1)S(1)}, u32[]{:S(2)}, u32[]{:S(2)}) async-start(bf16[16,40,128]{2,1,0:T(8,128)(2,1)} %shard_map.121), calls=%async_computation | async-start | bytes 327680 | tf_op jit(solution)/shard_map/all_to_all | solution.py:455
  26.9 20.3 %all-to-all-start.1 = ((bf16[16,40,128]{2,1,0:T(8,128)(2,1)}), bf16[16,40,128]{2,1,0:T(8,128)(2,1)S(1)}, u32[]{:S(2)}, u32[]{:S(2)}) async-start(bf16[16,40,128]{2,1,0:T(8,128)(2,1)} %shard_map.122), calls=%async_computation.1 | async-start | bytes 327680 | tf_op jit(solution)/shard_map/all_to_all | solution.py:494

commit v5 on v4

--- a/solution.py
+++ b/solution.py
@@ -11,6 +11,8 @@
 ANGLES = 180
 LANES = 128
 GROUP = 16
+TURN = 5
+SETS = 4
 
 data_gain = 0.25
 
@@ -29,7 +31,16 @@
     return parts
 
 
-def pack_kernel(volume_ref, out_ref):
+def pack_kernel(*refs):
+    count = (len(refs) - 2) // 2
+    sources, out_ref, held, sems = refs[:count], refs[count], refs[count + 1 : -1], refs[-1]
+    copies = [
+        pltpu.make_async_copy(source, target, sems.at[k]) for k, (source, target) in enumerate(zip(sources, held))
+    ]
+    for copy in copies:
+        copy.start()
+    copies[0].wait()
+    volume_ref = held[0]
     rows = volume_ref.shape[1]
     peers = out_ref.shape[0]
     chunks = LANES // rows
@@ -45,19 +56,14 @@
         out_ref[peer, :depth] = wide.astype(bf16)
         lower = jnp.concatenate([middle[:, at], final[:, at]] + blank, axis=1)
         out_ref[peer, depth:] = jnp.concatenate([lower, none], axis=0).astype(bf16)
-
-
-def prep_kernel(*refs):
-    sources, (wa_ref, wb_ref, wr_ref, lift_ref, shift_ref, spread_ref) = refs[:7], refs[7:13]
-    held, sems = refs[13:20], refs[20]
-    copies = [
-        pltpu.make_async_copy(source, target, sems.at[k]) for k, (source, target) in enumerate(zip(sources, held))
-    ]
-    for copy in copies:
-        copy.start()
-    for copy in copies:
+    for copy in copies[1:]:
         copy.wait()
-    angles_ref, gain_ref, base_ref, conv_a_ref, bias_ref, conv_b_ref, own_ref = held
+
+
+def prep_kernel(
+    angles_ref, offsets_ref, gain_ref, base_ref, conv_a_ref, bias_ref, conv_b_ref, own_ref,
+    wa_ref, wb_ref, wr_ref, lift_ref, shift_ref, table_ref,
+):
     channels = conv_a_ref.shape[1]
 
     def column(row):
@@ -104,7 +110,8 @@
                 wr_ref[s * GROUP : (s + 1) * GROUP, at] = block.astype(bf16)
 
     level = jnp.abs(jnp.cos(jnp.pi * angles_ref[...].astype(f32) / ANGLES))
-    spread_ref[...] = 0.6 + 0.4 * level
+    table_ref[0:1] = 0.6 + 0.4 * level
+    table_ref[1:2] = offsets_ref[...].astype(f32)
 
 
 def shifted(block, step):
@@ -155,8 +162,8 @@
     given, refs = refs[: 1 if begin else 0], refs[1 if begin else 0 :]
     volume_ref, lift_ref, bias_ref, wa_ref, wb_ref, wr_ref, out_ref, edge_ref = refs[:8]
     last_ref, refs = (refs[8], refs[9:]) if not begin else (None, refs[8:])
-    ring_a, ring_b, ring_c, h0_ref, h1_ref = refs
-    rings = (ring_a, ring_b, ring_c)
+    rings, (h0_ref, h1_ref) = refs[:-2], refs[-2:]
+    turn = len(rings)
     channels = lift_ref.shape[1]
     lead = 2 * channels if begin else 0
 
@@ -175,20 +182,20 @@
 
         convolved(p0, p1, wa_ref, bias_ref, store)
 
-    lift(0, ring_a)
-    lift(1, ring_b)
+    lift(0, rings[0])
+    lift(1, rings[1])
     if begin:
         h1_ref[:lead] = given[0][...]
 
-    def three(it, carry):
-        for k in range(3):
-            step(it * 3 + k, *[rings[(k + i) % 3] for i in range(3)])
+    def several(it, carry):
+        for k in range(turn):
+            step(it * turn + k, *[rings[(k + i) % turn] for i in range(3)])
         return carry
 
-    lax.fori_loop(0, count // 3, three, 0)
-    for k in range(count % 3):
-        assert k == count % 3 - 1
-        step(count - 1, rings[k], rings[k + 1], None)
+    lax.fori_loop(0, count // turn, several, 0)
+    for k in range(count % turn):
+        last = k == count % turn - 1
+        step(count - count % turn + k, rings[k], rings[(k + 1) % turn], None if last else rings[(k + 2) % turn])
 
     low = 2 * begin if begin else 2
     high = 2 * (begin + count)
@@ -207,7 +214,7 @@
         last_ref[...] = h1_ref[total - 2 * channels : total]
 
 
-def data_kernel(spread_ref, offset_ref, cells_in_ref, measured_ref, out_ref, cells_ref, back_ref, sum_ref, line_ref, sems, *scratch):
+def data_kernel(table_ref, cells_in_ref, measured_ref, out_ref, cells_ref, back_ref, sum_ref, line_ref, sems, *scratch):
     rows, views, det = measured_ref.shape[1:]
     peers = cells_in_ref.shape[0]
     nx = cells_ref.shape[1]
@@ -232,8 +239,6 @@
 
     back_ref[...] = jnp.zeros_like(back_ref)
     sum_ref[...] = jnp.zeros_like(sum_ref)
-    line_ref[:, :, :LANES] = jnp.zeros((views, rows, LANES), f32)
-    line_ref[:, :, LANES + det :] = jnp.zeros((views, rows, LANES), f32)
     for low_ref, _ in sets:
         low_ref[...] = jnp.zeros_like(low_ref)
 
@@ -241,16 +246,16 @@
     place = lax.broadcasted_iota(jnp.int32, (16, LANES), 0)
     bins = jnp.concatenate([(place + 16 * k).astype(jnp.int16) for k in range(16)], axis=0)
 
+    def window(view, b):
+        begin = (det - 1) * 0.5 + (b * LANES - (nx - 1) * 0.5) * table_ref[0, view] + table_ref[1, view]
+        first = jnp.floor(begin * (1.0 / LANES))
+        at = pl.ds(pl.multiple_of((first.astype(jnp.int32) + 1) * LANES, LANES), 2 * LANES)
+        return at, begin - first * LANES
+
     def forward(view, low_ref, tent_ref):
-        spread = spread_ref[0, view]
-        offset = offset_ref[0, view].astype(f32)
-        windows = []
         for b in range(blocks):
-            begin = (det - 1) * 0.5 + (b * LANES - (nx - 1) * 0.5) * spread + offset
-            first = jnp.floor(begin * (1.0 / LANES))
-            at = pl.ds(pl.multiple_of((first.astype(jnp.int32) + 1) * LANES, LANES), 2 * LANES)
-            windows.append(at)
-            target = cell * spread + (begin - first * LANES)
+            at, begin = window(view, b)
+            target = cell * table_ref[0, view] + begin
             under = jnp.floor(target)
             near = (1.0 - (target - under)).astype(bf16)
             far = (1.0 - ((under + 1.0) - target)).astype(bf16)
@@ -274,23 +279,37 @@
         for k in range(1, det // LANES):
             total = total + square[:, k * LANES : (k + 1) * LANES]
         sum_ref[...] += total
-        return windows
-
-    def backward(windows, low_ref, tent_ref):
-        for b, at in enumerate(windows):
+
+    def backward(view, low_ref, tent_ref):
+        for b in range(blocks):
+            at, _ = window(view, b)
             back_ref[:, b * LANES : (b + 1) * LANES] += jnp.dot(
                 low_ref[:, at], tent_ref[b], preferred_element_type=f32
             )
 
+    turn = len(sets)
+    lead = turn // 2
+    rounds = (views - lead) // turn
+    for view in range(lead):
+        fetch(view).wait()
+    for view in range(lead):
+        forward(view, *sets[view])
+
     def several(it, carry):
-        for k in range(len(sets)):
-            fetch(len(sets) * it + k).wait()
-        windows = [forward(len(sets) * it + k, *sets[k]) for k in range(len(sets))]
-        for k in range(len(sets)):
-            backward(windows[k], *sets[k])
+        for k in range(turn):
+            fetch(it * turn + lead + k).wait()
+        for k in range(turn):
+            forward(it * turn + lead + k, *sets[(lead + k) % turn])
+            backward(it * turn + k, *sets[k])
         return carry
 
-    lax.fori_loop(0, views // len(sets), several, 0)
+    lax.fori_loop(0, rounds, several, 0)
+    for view in range(rounds * turn + lead, views):
+        fetch(view).wait()
+    for view in range(rounds * turn, views):
+        if view + lead < views:
+            forward(view + lead, *sets[(view + lead) % turn])
+        backward(view, *sets[view % turn])
 
     whole = split(jnp.sum(sum_ref[...], keepdims=True), 3)
     lane = lax.broadcasted_iota(jnp.int32, (8, LANES), 1)
@@ -314,7 +333,7 @@
 
 
 def finish_kernel(
-    step_ref, anchor_ref, volume_ref, noise_ref, one_ref, two_ref, back_ref, head_ref, tail_ref, lift_ref, bias_ref,
+    anchor_ref, step_ref, volume_ref, noise_ref, one_ref, two_ref, back_ref, head_ref, tail_ref, lift_ref, bias_ref,
     wa_ref, wb_ref, wr_ref, out_ref, ext_ref, ring_a, ring_b, h1_ref, score_ref, *, count, height, border,
 ):
     rows, width = score_ref.shape
@@ -375,7 +394,7 @@
         at = (rows - 2) * side
         score_ref[at : at + 2] = scores[:2]
 
-    step = jnp.full((1, 1), step_ref[0], f32)
+    step = step_ref[...].reshape(1, 1)
     weight = data_gain / jnp.sqrt(misfit / count + 1e-06)
     sway = jnp.sqrt(2.0 * step)
     for tile in range(width // LANES):
@@ -386,6 +405,45 @@
         )
         moved = step * (score_ref[:, at] + weight * back)
         out_ref[0, :, at] = volume_ref[0, :, at] + moved + sway * noise_ref[0, :, at]
+
+
+def call(kernel, mebibytes, **kwargs):
+    params = pltpu.CompilerParams(vmem_limit_bytes=mebibytes << 20)
+    return pl.pallas_call(kernel, compiler_params=params, **kwargs)
+
+
+def spec(shape, dtype):
+    return jax.ShapeDtypeStruct(shape, dtype)
+
+
+def apart(array):
+    return pltpu.with_memory_space_constraint(array, pltpu.HBM)
+
+
+def data_call(table, cells, measured):
+    rows, views, det = measured.shape[1:]
+    peers = cells.shape[0]
+    nx = peers * rows
+    wide = det + 2 * LANES
+    lines = [
+        pltpu.VMEM((rows, wide), bf16),
+        pltpu.VMEM((nx // LANES, 2 * LANES, LANES), bf16),
+    ]
+    return call(
+        data_kernel,
+        12,
+        out_shape=spec((peers, rows * rows // LANES + 8, LANES), bf16),
+        in_specs=[SMEM, VMEM, HBM],
+        out_specs=VMEM,
+        scratch_shapes=[
+            pltpu.VMEM((rows, nx), bf16),
+            pltpu.VMEM((rows, nx), f32),
+            pltpu.VMEM((rows, LANES), f32),
+            pltpu.VMEM((views, rows, wide), f32),
+            pltpu.SemaphoreType.DMA((views,)),
+            *lines * SETS,
+        ],
+    )(table, cells, apart(measured))
 
 
 def per_device(
@@ -410,50 +468,40 @@
     chunks = LANES // rows
     depth = rows // chunks
 
-    def call(kernel, mebibytes, **kwargs):
-        return pl.pallas_call(
-            kernel, compiler_params=pltpu.CompilerParams(vmem_limit_bytes=mebibytes << 20), **kwargs
-        )
-
-    def spec(shape, dtype):
-        return jax.ShapeDtypeStruct(shape, dtype)
-
     def line(array):
         return array.reshape(1, -1)
 
-    def apart(array):
-        return pltpu.with_memory_space_constraint(array, pltpu.HBM)
-
-    nx = height
-    wide = det + 2 * LANES
     pairs = rows // 2 - 1
-    half = pairs // 6 * 3
+    half = pairs // 2
     ring = pltpu.VMEM((3, 2 * channels, width), bf16)
     pair = spec((2 * channels, width), bf16)
     anchor = (lax.axis_index("slab") * rows).astype(jnp.int32).reshape(1)
-    small = (line(angles), line(lift_w), line(lift_b), conv_a, line(bias_a), conv_b, line(out_w))
+    small = (volume, line(angles), line(offsets), line(lift_w), line(lift_b), conv_a, line(bias_a), conv_b, line(out_w))
 
     def score_part(begin, count, *args):
         return call(
             functools.partial(score_kernel, begin=begin, count=count),
-            20,
+            24,
             out_shape=(spec((rows, width), f32), pair) + (() if begin else (pair,)),
             in_specs=[VMEM] * len(args),
             out_specs=(VMEM,) * (2 if begin else 3),
             scratch_shapes=[
-                ring,
-                ring,
-                ring,
+                *[ring] * min(TURN, half),
                 pltpu.VMEM(((2 * count + 4) * channels, width), bf16),
                 pltpu.VMEM(((2 * count + 2) * channels, width), bf16),
             ],
         )(*args)
 
-    payload = call(
-        pack_kernel, 2, out_shape=spec((peers, depth + 8, LANES), bf16), in_specs=[VMEM], out_specs=VMEM
-    )(volume)
+    payload, volume, *small = call(
+        pack_kernel,
+        4,
+        out_shape=(spec((peers, depth + 8, LANES), bf16),) + tuple(spec(a.shape, a.dtype) for a in small),
+        in_specs=[HBM] * len(small),
+        out_specs=(VMEM,) * (len(small) + 1),
+        scratch_shapes=[pltpu.SemaphoreType.DMA((len(small),))],
+    )(*[apart(a) for a in small])
     cells = lax.all_to_all(payload, "slab", 0, 0)
-    wa, wb, wr, lift, bias, spread = call(
+    wa, wb, wr, lift, bias, table = call(
         prep_kernel,
         6,
         out_shape=(
@@ -462,42 +510,22 @@
             spec((2 * GROUP, GROUP * channels), bf16),
             spec((2, channels, LANES), f32),
             spec((2 * channels, LANES), f32),
-            spec((1, views), f32),
+            spec((2, views), f32),
         ),
-        in_specs=[HBM] * 7,
+        in_specs=[VMEM] * 8,
         out_specs=(VMEM,) * 6,
-        scratch_shapes=[pltpu.VMEM(a.shape, a.dtype) for a in small] + [pltpu.SemaphoreType.DMA((7,))],
-    )(*[apart(a) for a in small])
+    )(*small)
     consts = (lift, bias, wa, wb, wr)
     one, head, middle = score_part(0, half, volume, *consts)
 
-    lines = [
-        pltpu.VMEM((rows, wide), bf16),
-        pltpu.VMEM((nx // LANES, 2 * LANES, LANES), bf16),
-    ]
-    sent = call(
-        data_kernel,
-        12,
-        out_shape=spec((peers, depth + 8, LANES), bf16),
-        in_specs=[SMEM] * 2 + [VMEM, HBM],
-        out_specs=VMEM,
-        scratch_shapes=[
-            pltpu.VMEM((rows, nx), bf16),
-            pltpu.VMEM((rows, nx), f32),
-            pltpu.VMEM((rows, LANES), f32),
-            pltpu.VMEM((views, rows, wide), f32),
-            pltpu.SemaphoreType.DMA((views,)),
-            *lines,
-            *lines,
-        ],
-    )(spread, apart(line(offsets)), cells, apart(measured))
+    sent = data_call(table, cells, measured)
     returned = lax.all_to_all(sent, "slab", 0, 0)
     two, tail = score_part(half, pairs - half, middle, volume, *consts)
     return call(
         functools.partial(finish_kernel, count=slices * peers * rows * views * det, height=height, border=2 * half),
         12,
         out_shape=spec(volume.shape, f32),
-        in_specs=[SMEM] * 2 + [VMEM] * 12,
+        in_specs=[SMEM] + [VMEM] * 13,
         out_specs=VMEM,
         scratch_shapes=[
             pltpu.VMEM((16, width), f32),
@@ -506,7 +534,7 @@
             pltpu.VMEM((4 * channels, width), bf16),
             pltpu.VMEM((rows, width), f32),
         ],
-    )(step_size, anchor, volume, noise, one, two, returned, head, tail, *consts)
+    )(anchor, step_size, volume, noise, one, two, returned, head, tail, *consts)
 
 
 def solution(mesh):

time: 50.1 us -> 47.7 us (0.952)
  Pallas kernels: 30.2 us -> 27.6 us
  waiting for transfers between devices: 6.95 us -> 8.04 us
  local copies, waits for them, and re-layouts: 0.96 us -> 0.01 us
    pallas_call x4, Pallas kernels: 26.2 us -> 24.7 us  [the longest x2 15.1 us: score_part(): call(functools.partial(score_kernel, begin=begin, count=count), 24, out_s...]
    all_to_all x1, waiting for transfers between devices: 6.94 us -> 8.03 us  [per_device(): cells = lax.all_to_all(payload, 'slab', 0, 0)]
    pallas_call x1, Pallas kernels: 1.48 us -> 0.4 us  [per_device(): call(prep_kernel, 6, out_shape=(spec((2 * channels, 12 * channels), bf16)...]
    unnamed x6 -> x2, local copies, waits for them, and re-layouts: 0.96 us -> 0.01 us
  transfers between devices with their start and end apart: 2 -> 2, of which waited for: 1 -> 1; matrix products, arithmetic and copies ran while one was open for 0% -> 0% of each run, Pallas kernels for 35% -> 33%
where the time goes in v5:
time: 47.7 us; the launch traced here: 47.3 us
  Pallas kernels  27.6 us (58%)
  starting transfers between devices  11 us (23%)
  waiting for transfers between devices  8.04 us (17%)
  between operations  0.71 us (1%)
    pallas_call x2, Pallas kernels, score_part(): call(functools.partial(score_kernel, begin=begin, count=count), 24, out_s...  15.1 us
    all_to_all x1, waiting for transfers between devices, per_device(): cells = lax.all_to_all(payload, 'slab', 0, 0)  8.03 us
    pallas_call x1, Pallas kernels, data_call(): call(data_kernel, 12, out_shape=spec((peers, rows * rows // LANES + 8, LA...  7.65 us
    all_to_all x1, starting transfers between devices, per_device(): cells = lax.all_to_all(payload, 'slab', 0, 0)  7.43 us
    all_to_all x1, starting transfers between devices, per_device(): returned = lax.all_to_all(sent, 'slab', 0, 0)  3.53 us
    pallas_call x1, Pallas kernels, per_device(): call(functools.partial(finish_kernel, count=slices * peers * rows * views...  2.52 us
    pallas_call x1, Pallas kernels, per_device(): call(pack_kernel, 4, out_shape=(spec((peers, depth + 8, LANES), bf16),) +...  1.93 us
  transfers between devices with their start and end apart: 2, of which 1 were waited for; matrix products, arithmetic and copies ran while one was open for 0% of the time, Pallas kernels for 33%

profile of v5, /device:TPU:0, one launch (start us, length us, event | category | flops | bytes accessed | tf_op | source)
XLA Modules:
  0.0 47.3 jit_solution(13362235166027386823)
XLA Ops:
  0.0 0.0 copy-start
  0.0 1.9 %shard_map.118 = (bf16[16,40,128]{2,1,0:T(8,128)(2,1)}, f32[1,64,1024]{2,1,0:T(8,128)S(1)}, s32[1,16]{1,0:T(1,128)S(1)}, s32[1,16]{1,0:T(1,128)S(1)}, f32[1,64]{...) custom-call(f32[1,64,1024]{2,1,0:T(8,128)} %refs_0_.1, ...), custom_call_target="tpu_custom_call" | custom-call | tf_op jit(solution)/shard_map/pallas_call | solution.py:495
  1.9 7.4 %all-to-all-start = ((bf16[16,40,128]{2,1,0:T(8,128)(2,1)}), bf16[16,40,128]{2,1,0:T(8,128)(2,1)S(1)}, u32[]{:S(2)}, u32[]{:S(2)}) async-start(bf16[16,40,128]{2,1,0:T(8,128)(2,1)} %get-tuple-element.44), calls=%async_computation | async-start | bytes 327680 | tf_op jit(solution)/shard_map/all_to_all | solution.py:503
  9.4 0.4 shard_map.119
  9.8 8.0 %all-to-all-done.cells_in_ref = bf16[16,40,128]{2,1,0:T(8,128)(2,1)S(1)} async-done(((bf16[16,40,128]{2,1,0:T(8,128)(2,1)}), bf16[16,40,128]{2,1,0:T(8,128)(2,1)S(1)}, u32[]{:S(2)}, u32[]{:S(2)}) %all-to-all-start) | async-done | bytes 163872 | tf_op jit(solution)/shard_map/all_to_all | solution.py:503
  17.8 7.6 %shard_map.122 = bf16[16,40,128]{2,1,0:T(8,128)(2,1)} custom-call(f32[2,16]{1,0:T(2,128)S(1)} %get-tuple-element.43.table_ref, bf16[16,40,128]{2,1,0:T(8,128)(2,1)S(1)} %all-to-all-done.cells_in_ref, f32[1,64,16,1024]{3,2,1,0:T(8,128)} %measured_ref.1), custom_call_target="tpu_custom_call" | custom-call | tf_op jit(solution)/shard_map/pallas_call | solution.py:432
  25.5 3.5 %all-to-all-start.1 = ((bf16[16,40,128]{2,1,0:T(8,128)(2,1)}), bf16[16,40,128]{2,1,0:T(8,128)(2,1)S(1)}, u32[]{:S(2)}, u32[]{:S(2)}) async-start(bf16[16,40,128]{2,1,0:T(8,128)(2,1)} %shard_map.122), calls=%async_computation.1 | async-start | bytes 327680 | tf_op jit(solution)/shard_map/all_to_all | solution.py:522
  29.6 7.3 %shard_map.120 = (f32[64,1024]{1,0:T(8,128)S(1)}, bf16[128,1024]{1,0:T(8,128)(2,1)S(1)}, bf16[128,1024]{1,0:T(8,128)(2,1)S(1)}) custom-call(f32[1,64,1024]{2,1,0:T(8,128)S(1)} %get-tuple-element.26.refs_0_.refs_1_.volume_ref, f32[2,64,128]{2,1,0:T(8,128)S(1)} %get-tuple-element.35.refs_1_.refs_2_.lift_ref, ...), custom_call_target="tpu_custom_call" | custom-call | tf_op jit(solution)/shard_map/pallas_call | solution.py:482
  37.0 7.8 %shard_map.121 = (f32[64,1024]{1,0:T(8,128)S(1)}, bf16[128,1024]{1,0:T(8,128)(2,1)S(1)}) custom-call(bf16[128,1024]{1,0:T(8,128)(2,1)S(1)} %get-tuple-element.41.refs_0_, f32[1,64,1024]{2,1,0:T(8,128)S(1)} %get-tuple-element.26.refs_0_.refs_1_.volume_ref, f32[2,64,128]{2,1,0:T(8,128)S(1)} %get-tuple-element.35.refs_1_.refs_2_.lift_ref, ...), custom_call_target="tpu_custom_call" | custom-call | tf_op jit(solution)/shard_map/pallas_call | solution.py:482
  44.8 0.0 all-to-all-done.1.back_ref
  44.8 0.0 copy-done
  44.8 2.5 %shard_map.123 = f32[1,64,1024]{2,1,0:T(8,128)} custom-call(s32[1]{0:T(128)} %bitcast.anchor_ref, f32[1]{0:T(128)S(6)} %copy.13.step_ref, f32[1,64,1024]{2,1,0:T(8,128)S(1)} %get-tuple-element.26.refs_0_.refs_1_.volume_ref, f32[1,64,1024]{2,1,0:T(8,128)S(1)} %copy-done, f32[64,1024]{1,0:T(8,128)S(1)} %get-tuple-element.40.one_ref, ...), custom_call_target="tpu_custom_call" | custom-call | tf_op jit(solution)/shard_map/pallas_call | solution.py:524
Async XLA Ops:
  0.0 44.8 %copy-start = (f32[1,64,1024]{2,1,0:T(8,128)S(1)}, f32[1,64,1024]{2,1,0:T(8,128)}, u32[]{:S(2)}) copy-start(f32[1,64,1024]{2,1,0:T(8,128)} %noise_ref.1) | copy-start | bytes 786436
  1.9 15.9 %all-to-all-start = ((bf16[16,40,128]{2,1,0:T(8,128)(2,1)}), bf16[16,40,128]{2,1,0:T(8,128)(2,1)S(1)}, u32[]{:S(2)}, u32[]{:S(2)}) async-start(bf16[16,40,128]{2,1,0:T(8,128)(2,1)} %get-tuple-element.44), calls=%async_computation | async-start | bytes 327680 | tf_op jit(solution)/shard_map/all_to_all | solution.py:503
  25.5 19.3 %all-to-all-start.1 = ((bf16[16,40,128]{2,1,0:T(8,128)(2,1)}), bf16[16,40,128]{2,1,0:T(8,128)(2,1)S(1)}, u32[]{:S(2)}, u32[]{:S(2)}) async-start(bf16[16,40,128]{2,1,0:T(8,128)(2,1)} %shard_map.122), calls=%async_computation.1 | async-start | bytes 327680 | tf_op jit(solution)/shard_map/all_to_all | solution.py:522

commit v6 on v5

--- a/solution.py
+++ b/solution.py
@@ -11,7 +11,8 @@
 ANGLES = 180
 LANES = 128
 GROUP = 16
-TURN = 5
+TURN = 4
+WAIT = 14
 SETS = 4
 
 data_gain = 0.25
@@ -138,7 +139,7 @@
         ring[1, at + c : at + c + 16] = h
         ring[2, at + c : at + c + 16] = shifted(h, 1)
         if kept_ref is not None:
-            kept_ref[pl.ds(pl.multiple_of(kept_at + c, 16), 16), :] = h
+            kept_ref[kept_at + c : kept_at + c + 16, :] = h
 
 
 def convolved(p0, p1, wa_ref, bias_ref, store):
@@ -159,7 +160,7 @@
 
 
 def score_kernel(*refs, begin, count):
-    given, refs = refs[: 1 if begin else 0], refs[1 if begin else 0 :]
+    given, refs = refs[: int(begin > 0)], refs[int(begin > 0) :]
     volume_ref, lift_ref, bias_ref, wa_ref, wb_ref, wr_ref, out_ref, edge_ref = refs[:8]
     last_ref, refs = (refs[8], refs[9:]) if not begin else (None, refs[8:])
     rings, (h0_ref, h1_ref) = refs[:-2], refs[-2:]
@@ -170,7 +171,7 @@
     def lift(pair, ring):
         for k in range(2):
             row = 2 * pair + k
-            line = volume_ref[0, pl.ds(2 * begin + row, 1), :]
+            line = volume_ref[0, 2 * begin + row : 2 * begin + row + 1, :]
             lifted(line, lift_ref, ring, k * channels, h0_ref, row * channels)
 
     def step(g, p0, p1, p2):
@@ -178,7 +179,7 @@
             lift(g + 2, p2)
 
         def store(at, h):
-            h1_ref[pl.ds(pl.multiple_of(lead + g * 2 * channels, 128), 2 * channels), at] = h
+            h1_ref[lead + g * 2 * channels : lead + (g + 1) * 2 * channels, at] = h
 
         convolved(p0, p1, wa_ref, bias_ref, store)
 
@@ -187,24 +188,18 @@
     if begin:
         h1_ref[:lead] = given[0][...]
 
-    def several(it, carry):
-        for k in range(turn):
-            step(it * turn + k, *[rings[(k + i) % turn] for i in range(3)])
-        return carry
-
-    lax.fori_loop(0, count // turn, several, 0)
-    for k in range(count % turn):
-        last = k == count % turn - 1
-        step(count - count % turn + k, rings[k], rings[(k + 1) % turn], None if last else rings[(k + 2) % turn])
-
     low = 2 * begin if begin else 2
-    high = 2 * (begin + count)
-    for row in range(low, high, GROUP):
-        size = min(GROUP, high - row)
-        at = (row - low) * channels
-        own = (row - 2 * begin) * channels
-        total = projected(h1_ref[at : at + (size + 2) * channels], h0_ref[own : own + size * channels], wb_ref, wr_ref)
-        out_ref[row : row + size] = total[:size]
+    done = low
+    for k in range(count):
+        step(k, rings[k % turn], rings[(k + 1) % turn], rings[(k + 2) % turn] if k + 1 < count else None)
+        ready = 2 * (begin + k + 1)
+        if ready - done >= WAIT or k + 1 == count:
+            at = (done - low) * channels
+            own = (done - 2 * begin) * channels
+            size = ready - done
+            total = projected(h1_ref[at : at + (size + 2) * channels], h0_ref[own : own + size * channels], wb_ref, wr_ref)
+            out_ref[done : done + size] = total[:size]
+            done = ready
 
     total = (2 * count) * channels + lead
     if begin:
@@ -334,7 +329,7 @@
 
 def finish_kernel(
     anchor_ref, step_ref, volume_ref, noise_ref, one_ref, two_ref, back_ref, head_ref, tail_ref, lift_ref, bias_ref,
-    wa_ref, wb_ref, wr_ref, out_ref, ext_ref, ring_a, ring_b, h1_ref, score_ref, *, count, height, border,
+    wa_ref, wb_ref, wr_ref, out_ref, ext_ref, ring_a, ring_b, h1_ref, score_ref, done_ref, sems, *, count, height, border,
 ):
     rows, width = score_ref.shape
     channels = lift_ref.shape[1]
@@ -365,6 +360,24 @@
 
     score_ref[:border] = one_ref[:border]
     score_ref[border:] = two_ref[border:]
+    step = step_ref[...].reshape(1, 1)
+    weight = data_gain / jnp.sqrt(misfit / count + 1e-06)
+    sway = jnp.sqrt(2.0 * step)
+
+    def combine(low, high, sem):
+        for tile in range(width // LANES):
+            at = slice(tile * LANES, (tile + 1) * LANES)
+            got = [back_ref[tile * chunks + k, :depth].astype(f32) for k in range(chunks)]
+            back = jnp.concatenate(
+                [jnp.concatenate([g[:, k * rows : (k + 1) * rows] for g in got], axis=1) for k in range(chunks)], axis=0
+            )[low:high]
+            moved = step * (score_ref[low:high, at] + weight * back)
+            done_ref[low:high, at] = volume_ref[0, low:high, at] + moved + sway * noise_ref[0, low:high, at]
+        copy = pltpu.make_async_copy(done_ref.at[pl.ds(low, high - low)], out_ref.at[0, pl.ds(low, high - low)], sem)
+        copy.start()
+        return copy
+
+    copies = [combine(8, rows - 8, sems.at[0])] if rows > 16 else []
     inside = jnp.where(anchor > 0, 1.0, 0.0).astype(f32), jnp.where(anchor + rows < height, 1.0, 0.0).astype(f32)
     for side in range(2):
         for k in range(4):
@@ -394,17 +407,10 @@
         at = (rows - 2) * side
         score_ref[at : at + 2] = scores[:2]
 
-    step = step_ref[...].reshape(1, 1)
-    weight = data_gain / jnp.sqrt(misfit / count + 1e-06)
-    sway = jnp.sqrt(2.0 * step)
-    for tile in range(width // LANES):
-        at = slice(tile * LANES, (tile + 1) * LANES)
-        got = [back_ref[tile * chunks + k, :depth].astype(f32) for k in range(chunks)]
-        back = jnp.concatenate(
-            [jnp.concatenate([g[:, k * rows : (k + 1) * rows] for g in got], axis=1) for k in range(chunks)], axis=0
-        )
-        moved = step * (score_ref[:, at] + weight * back)
-        out_ref[0, :, at] = volume_ref[0, :, at] + moved + sway * noise_ref[0, :, at]
+    for k, low in enumerate((0, rows - 8)):
+        copies.append(combine(low, low + 8, sems.at[k + 1]))
+    for copy in copies:
+        copy.wait()
 
 
 def call(kernel, mebibytes, **kwargs):
@@ -526,13 +532,15 @@
         12,
         out_shape=spec(volume.shape, f32),
         in_specs=[SMEM] + [VMEM] * 13,
-        out_specs=VMEM,
+        out_specs=HBM,
         scratch_shapes=[
             pltpu.VMEM((16, width), f32),
             ring,
             ring,
             pltpu.VMEM((4 * channels, width), bf16),
             pltpu.VMEM((rows, width), f32),
+            pltpu.VMEM((rows, width), f32),
+            pltpu.SemaphoreType.DMA((3,)),
         ],
     )(anchor, step_size, volume, noise, one, two, returned, head, tail, *consts)
 

time: 47.7 us -> 46.2 us (0.969)
  Pallas kernels: 27.6 us -> 25.9 us
    pallas_call x2, Pallas kernels: 15.1 us -> 13.4 us  [score_part(): call(functools.partial(score_kernel, begin=begin, count=count), 24, out_s...]
  transfers between devices with their start and end apart: 2 -> 2, of which waited for: 1 -> 1; matrix products, arithmetic and copies ran while one was open for 0% -> 0% of each run, Pallas kernels for 33% -> 30%
where the time goes in v6:
time: 46.2 us; the launch traced here: 45.9 us
  Pallas kernels  25.9 us (56%)
  starting transfers between devices  11.1 us (24%)
  waiting for transfers between devices  8.03 us (17%)
  between operations  0.87 us (2%)
    pallas_call x2, Pallas kernels, score_part(): call(functools.partial(score_kernel, begin=begin, count=count), 24, out_s...  13.4 us
    all_to_all x1, waiting for transfers between devices, per_device(): cells = lax.all_to_all(payload, 'slab', 0, 0)  8.03 us
    pallas_call x1, Pallas kernels, data_call(): call(data_kernel, 12, out_shape=spec((peers, rows * rows // LANES + 8, LA...  7.65 us
    all_to_all x1, starting transfers between devices, per_device(): cells = lax.all_to_all(payload, 'slab', 0, 0)  7.43 us
    all_to_all x1, starting transfers between devices, per_device(): returned = lax.all_to_all(sent, 'slab', 0, 0)  3.71 us
    pallas_call x1, Pallas kernels, per_device(): call(functools.partial(finish_kernel, count=slices * peers * rows * views...  2.49 us
    pallas_call x1, Pallas kernels, per_device(): call(pack_kernel, 4, out_shape=(spec((peers, depth + 8, LANES), bf16),) +...  1.93 us
  transfers between devices with their start and end apart: 2, of which 1 were waited for; matrix products, arithmetic and copies ran while one was open for 0% of the time, Pallas kernels for 30%

profile of v6, /device:TPU:0, one launch (start us, length us, event | category | flops | bytes accessed | tf_op | source)
XLA Modules:
  0.0 45.9 jit_solution(11931570801588067672)
XLA Ops:
  0.0 0.0 copy-start
  0.0 1.9 %shard_map.118 = (bf16[16,40,128]{2,1,0:T(8,128)(2,1)}, f32[1,64,1024]{2,1,0:T(8,128)S(1)}, s32[1,16]{1,0:T(1,128)S(1)}, s32[1,16]{1,0:T(1,128)S(1)}, f32[1,64]{...) custom-call(f32[1,64,1024]{2,1,0:T(8,128)} %refs_0_.1, ...), custom_call_target="tpu_custom_call" | custom-call | tf_op jit(solution)/shard_map/pallas_call | solution.py:501
  1.9 7.4 %all-to-all-start = ((bf16[16,40,128]{2,1,0:T(8,128)(2,1)}), bf16[16,40,128]{2,1,0:T(8,128)(2,1)S(1)}, u32[]{:S(2)}, u32[]{:S(2)}) async-start(bf16[16,40,128]{2,1,0:T(8,128)(2,1)} %get-tuple-element.44), calls=%async_computation | async-start | bytes 327680 | tf_op jit(solution)/shard_map/all_to_all | solution.py:509
  9.4 0.4 shard_map.119
  9.8 8.0 %all-to-all-done.cells_in_ref = bf16[16,40,128]{2,1,0:T(8,128)(2,1)S(1)} async-done(((bf16[16,40,128]{2,1,0:T(8,128)(2,1)}), bf16[16,40,128]{2,1,0:T(8,128)(2,1)S(1)}, u32[]{:S(2)}, u32[]{:S(2)}) %all-to-all-start) | async-done | bytes 163872 | tf_op jit(solution)/shard_map/all_to_all | solution.py:509
  17.8 7.6 %shard_map.122 = bf16[16,40,128]{2,1,0:T(8,128)(2,1)} custom-call(f32[2,16]{1,0:T(2,128)S(1)} %get-tuple-element.43.table_ref, bf16[16,40,128]{2,1,0:T(8,128)(2,1)S(1)} %all-to-all-done.cells_in_ref, f32[1,64,16,1024]{3,2,1,0:T(8,128)} %measured_ref.1), custom_call_target="tpu_custom_call" | custom-call | tf_op jit(solution)/shard_map/pallas_call | solution.py:438
  25.5 3.7 %all-to-all-start.1 = ((bf16[16,40,128]{2,1,0:T(8,128)(2,1)}), bf16[16,40,128]{2,1,0:T(8,128)(2,1)S(1)}, u32[]{:S(2)}, u32[]{:S(2)}) async-start(bf16[16,40,128]{2,1,0:T(8,128)(2,1)} %shard_map.122), calls=%async_computation.1 | async-start | bytes 327680 | tf_op jit(solution)/shard_map/all_to_all | solution.py:528
  29.8 6.4 %shard_map.120 = (f32[64,1024]{1,0:T(8,128)S(1)}, bf16[128,1024]{1,0:T(8,128)(2,1)S(1)}, bf16[128,1024]{1,0:T(8,128)(2,1)S(1)}) custom-call(f32[1,64,1024]{2,1,0:T(8,128)S(1)} %get-tuple-element.26.refs_0_.refs_1_.volume_ref, f32[2,64,128]{2,1,0:T(8,128)S(1)} %get-tuple-element.35.refs_1_.refs_2_.lift_ref, ...), custom_call_target="tpu_custom_call" | custom-call | tf_op jit(solution)/shard_map/pallas_call | solution.py:488
  36.3 7.0 %shard_map.121 = (f32[64,1024]{1,0:T(8,128)S(1)}, bf16[128,1024]{1,0:T(8,128)(2,1)S(1)}) custom-call(bf16[128,1024]{1,0:T(8,128)(2,1)S(1)} %get-tuple-element.41.refs_0_, f32[1,64,1024]{2,1,0:T(8,128)S(1)} %get-tuple-element.26.refs_0_.refs_1_.volume_ref, f32[2,64,128]{2,1,0:T(8,128)S(1)} %get-tuple-element.35.refs_1_.refs_2_.lift_ref, ...), custom_call_target="tpu_custom_call" | custom-call | tf_op jit(solution)/shard_map/pallas_call | solution.py:488
  43.2 0.0 all-to-all-done.1.back_ref
  43.2 0.0 copy-done
  43.3 2.5 %shard_map.123 = f32[1,64,1024]{2,1,0:T(8,128)} custom-call(s32[1]{0:T(128)} %bitcast.anchor_ref, f32[1]{0:T(128)S(6)} %copy.13.step_ref, f32[1,64,1024]{2,1,0:T(8,128)S(1)} %get-tuple-element.26.refs_0_.refs_1_.volume_ref, f32[1,64,1024]{2,1,0:T(8,128)S(1)} %copy-done, f32[64,1024]{1,0:T(8,128)S(1)} %get-tuple-element.40.one_ref, ...), custom_call_target="tpu_custom_call" | custom-call | tf_op jit(solution)/shard_map/pallas_call | solution.py:530
Async XLA Ops:
  0.0 43.2 %copy-start = (f32[1,64,1024]{2,1,0:T(8,128)S(1)}, f32[1,64,1024]{2,1,0:T(8,128)}, u32[]{:S(2)}) copy-start(f32[1,64,1024]{2,1,0:T(8,128)} %noise_ref.1) | copy-start | bytes 786436
  1.9 15.9 %all-to-all-start = ((bf16[16,40,128]{2,1,0:T(8,128)(2,1)}), bf16[16,40,128]{2,1,0:T(8,128)(2,1)S(1)}, u32[]{:S(2)}, u32[]{:S(2)}) async-start(bf16[16,40,128]{2,1,0:T(8,128)(2,1)} %get-tuple-element.44), calls=%async_computation | async-start | bytes 327680 | tf_op jit(solution)/shard_map/all_to_all | solution.py:509
  25.5 17.8 %all-to-all-start.1 = ((bf16[16,40,128]{2,1,0:T(8,128)(2,1)}), bf16[16,40,128]{2,1,0:T(8,128)(2,1)S(1)}, u32[]{:S(2)}, u32[]{:S(2)}) async-start(bf16[16,40,128]{2,1,0:T(8,128)(2,1)} %shard_map.122), calls=%async_computation.1 | async-start | bytes 327680 | tf_op jit(solution)/shard_map/all_to_all | solution.py:528

commit v7 on v6

--- a/solution.py
+++ b/solution.py
@@ -13,6 +13,7 @@
 GROUP = 16
 TURN = 4
 WAIT = 14
+EARLY = 4
 SETS = 4
 
 data_gain = 0.25
@@ -160,9 +161,16 @@
 
 
 def score_kernel(*refs, begin, count):
-    given, refs = refs[: int(begin > 0)], refs[int(begin > 0) :]
+    given, refs = refs[0], refs[1:]
     volume_ref, lift_ref, bias_ref, wa_ref, wb_ref, wr_ref, out_ref, edge_ref = refs[:8]
-    last_ref, refs = (refs[8], refs[9:]) if not begin else (None, refs[8:])
+    copies = []
+    if begin:
+        refs = refs[8:]
+    else:
+        last_ref, seen_ref, sems, refs = refs[8], refs[9], refs[10], refs[11:]
+        for view in range(seen_ref.shape[0]):
+            copies.append(pltpu.make_async_copy(given.at[0, :, view], seen_ref.at[view], sems.at[view]))
+            copies[-1].start()
     rings, (h0_ref, h1_ref) = refs[:-2], refs[-2:]
     turn = len(rings)
     channels = lift_ref.shape[1]
@@ -186,7 +194,7 @@
     lift(0, rings[0])
     lift(1, rings[1])
     if begin:
-        h1_ref[:lead] = given[0][...]
+        h1_ref[:lead] = given[...]
 
     low = 2 * begin if begin else 2
     done = low
@@ -207,9 +215,11 @@
     else:
         edge_ref[...] = h1_ref[: 2 * channels]
         last_ref[...] = h1_ref[total - 2 * channels : total]
-
-
-def data_kernel(table_ref, cells_in_ref, measured_ref, out_ref, cells_ref, back_ref, sum_ref, line_ref, sems, *scratch):
+    for copy in copies:
+        copy.wait()
+
+
+def data_kernel(table_ref, cells_in_ref, seen_ref, measured_ref, out_ref, cells_ref, back_ref, sum_ref, line_ref, sems, *scratch):
     rows, views, det = measured_ref.shape[1:]
     peers = cells_in_ref.shape[0]
     nx = cells_ref.shape[1]
@@ -222,8 +232,11 @@
     def fetch(view):
         return pltpu.make_async_copy(measured_ref.at[0, :, view], line_ref.at[view, :, body], sems.at[view])
 
-    for view in range(views):
+    early = seen_ref.shape[0]
+    for view in range(early, views):
         fetch(view).start()
+    for view in range(early):
+        line_ref[view, :, body] = seen_ref[view]
 
     for tile in range(nx // LANES):
         pieces = []
@@ -285,21 +298,26 @@
     turn = len(sets)
     lead = turn // 2
     rounds = (views - lead) // turn
-    for view in range(lead):
+    for view in range(early, lead):
         fetch(view).wait()
     for view in range(lead):
         forward(view, *sets[view])
 
     def several(it, carry):
         for k in range(turn):
-            fetch(it * turn + lead + k).wait()
+            view = it * turn + lead + k
+
+            @pl.when(view >= early)
+            def _():
+                fetch(view).wait()
+
         for k in range(turn):
             forward(it * turn + lead + k, *sets[(lead + k) % turn])
             backward(it * turn + k, *sets[k])
         return carry
 
     lax.fori_loop(0, rounds, several, 0)
-    for view in range(rounds * turn + lead, views):
+    for view in range(max(rounds * turn + lead, early), views):
         fetch(view).wait()
     for view in range(rounds * turn, views):
         if view + lead < views:
@@ -426,7 +444,7 @@
     return pltpu.with_memory_space_constraint(array, pltpu.HBM)
 
 
-def data_call(table, cells, measured):
+def data_call(table, cells, seen, measured):
     rows, views, det = measured.shape[1:]
     peers = cells.shape[0]
     nx = peers * rows
@@ -439,7 +457,7 @@
         data_kernel,
         12,
         out_shape=spec((peers, rows * rows // LANES + 8, LANES), bf16),
-        in_specs=[SMEM, VMEM, HBM],
+        in_specs=[SMEM, VMEM, VMEM, HBM],
         out_specs=VMEM,
         scratch_shapes=[
             pltpu.VMEM((rows, nx), bf16),
@@ -449,7 +467,7 @@
             pltpu.SemaphoreType.DMA((views,)),
             *lines * SETS,
         ],
-    )(table, cells, apart(measured))
+    )(table, cells, seen, apart(measured))
 
 
 def per_device(
@@ -485,13 +503,15 @@
     small = (volume, line(angles), line(offsets), line(lift_w), line(lift_b), conv_a, line(bias_a), conv_b, line(out_w))
 
     def score_part(begin, count, *args):
+        more = () if begin else (pair, spec((EARLY, rows, det), f32))
         return call(
             functools.partial(score_kernel, begin=begin, count=count),
-            24,
-            out_shape=(spec((rows, width), f32), pair) + (() if begin else (pair,)),
-            in_specs=[VMEM] * len(args),
-            out_specs=(VMEM,) * (2 if begin else 3),
-            scratch_shapes=[
+            20,
+            out_shape=(spec((rows, width), f32), pair) + more,
+            in_specs=[VMEM if begin else HBM] + [VMEM] * (len(args) - 1),
+            out_specs=(VMEM,) * (2 + len(more)),
+            scratch_shapes=([] if begin else [pltpu.SemaphoreType.DMA((EARLY,))])
+            + [
                 *[ring] * min(TURN, half),
                 pltpu.VMEM(((2 * count + 4) * channels, width), bf16),
                 pltpu.VMEM(((2 * count + 2) * channels, width), bf16),
@@ -522,9 +542,9 @@
         out_specs=(VMEM,) * 6,
     )(*small)
     consts = (lift, bias, wa, wb, wr)
-    one, head, middle = score_part(0, half, volume, *consts)
-
-    sent = data_call(table, cells, measured)
+    one, head, middle, seen = score_part(0, half, apart(measured), volume, *consts)
+
+    sent = data_call(table, cells, seen, measured)
     returned = lax.all_to_all(sent, "slab", 0, 0)
     two, tail = score_part(half, pairs - half, middle, volume, *consts)
     return call(

time: 46.2 us -> 40.8 us (0.88)
  waiting for transfers between devices: 8.03 us -> 2.33 us
  starting transfers between devices: 11.1 us -> 11.9 us
  Pallas kernels: 25.9 us -> 25.3 us
    all_to_all x1, waiting for transfers between devices: 8.03 us -> 1.53 us  [per_device(): cells = lax.all_to_all(payload, 'slab', 0, 0)]
    all_to_all x1, starting transfers between devices: 3.71 us -> 4.52 us  [per_device(): returned = lax.all_to_all(sent, 'slab', 0, 0)]
    all_to_all x1, waiting for transfers between devices: 0.01 us -> 0.8 us  [per_device(): returned = lax.all_to_all(sent, 'slab', 0, 0)]
    pallas_call x1, Pallas kernels: 7.65 us -> 7.08 us  [data_call(): call(data_kernel, 12, out_shape=spec((peers, rows * rows // LANES + 8, LA...]
  transfers between devices with their start and end apart: 2 -> 2, of which waited for: 1 -> 2; matrix products, arithmetic and copies ran while one was open for 0% -> 0% of each run, Pallas kernels for 30% -> 34%
where the time goes in v7:
time: 40.8 us; the launch traced here: 40.4 us
  Pallas kernels  25.3 us (62%)
  starting transfers between devices  11.9 us (29%)
  waiting for transfers between devices  2.33 us (6%)
  between operations  0.87 us (2%)
    pallas_call x2, Pallas kernels, score_part(): call(functools.partial(score_kernel, begin=begin, count=count), 20, out_s...  13.4 us
    all_to_all x1, starting transfers between devices, per_device(): cells = lax.all_to_all(payload, 'slab', 0, 0)  7.43 us
    pallas_call x1, Pallas kernels, data_call(): call(data_kernel, 12, out_shape=spec((peers, rows * rows // LANES + 8, LA...  7.08 us
    all_to_all x1, starting transfers between devices, per_device(): returned = lax.all_to_all(sent, 'slab', 0, 0)  4.52 us
    pallas_call x1, Pallas kernels, per_device(): call(functools.partial(finish_kernel, count=slices * peers * rows * views...  2.48 us
    pallas_call x1, Pallas kernels, per_device(): call(pack_kernel, 4, out_shape=(spec((peers, depth + 8, LANES), bf16),) +...  1.88 us
    all_to_all x1, waiting for transfers between devices, per_device(): cells = lax.all_to_all(payload, 'slab', 0, 0)  1.53 us
  transfers between devices with their start and end apart: 2, of which 2 were waited for; matrix products, arithmetic and copies ran while one was open for 0% of the time, Pallas kernels for 34%

profile of v7, /device:TPU:0, one launch (start us, length us, event | category | flops | bytes accessed | tf_op | source)
XLA Modules:
  0.0 40.4 jit_solution(7886500184627140181)
XLA Ops:
  0.0 1.9 %shard_map.118 = (bf16[16,40,128]{2,1,0:T(8,128)(2,1)}, f32[1,64,1024]{2,1,0:T(8,128)S(1)}, s32[1,16]{1,0:T(1,128)S(1)}, s32[1,16]{1,0:T(1,128)S(1)}, f32[1,64]{...) custom-call(f32[1,64,1024]{2,1,0:T(8,128)} %refs_0_.2, ...), custom_call_target="tpu_custom_call" | custom-call | tf_op jit(solution)/shard_map/pallas_call | solution.py:521
  1.9 7.4 %all-to-all-start = ((bf16[16,40,128]{2,1,0:T(8,128)(2,1)}), bf16[16,40,128]{2,1,0:T(8,128)(2,1)S(1)}, u32[]{:S(2)}, u32[]{:S(2)}) async-start(bf16[16,40,128]{2,1,0:T(8,128)(2,1)} %get-tuple-element.45), calls=%async_computation | async-start | bytes 327680 | tf_op jit(solution)/shard_map/all_to_all | solution.py:529
  9.3 0.4 shard_map.119
  9.7 6.5 %shard_map.120 = (f32[64,1024]{1,0:T(8,128)S(1)}, bf16[128,1024]{1,0:T(8,128)(2,1)S(1)}, bf16[128,1024]{1,0:T(8,128)(2,1)S(1)}, f32[4,64,1024]{2,1,0:T(8,128)S(1)}) custom-call(f32[1,64,16,1024]{3,2,1,0:T(8,128)} %measured_ref.1, f32[1,64,1024]{2,1,0:T(8,128)S(1)} %get-tuple-element.27.refs_1_.volume_ref, ...), custom_call_target="tpu_custom_call" | custom-call | tf_op jit(solution)/shard_map/pallas_call | solution.py:507
  16.2 0.0 copy-start
  16.2 1.5 %all-to-all-done.cells_in_ref = bf16[16,40,128]{2,1,0:T(8,128)(2,1)S(1)} async-done(((bf16[16,40,128]{2,1,0:T(8,128)(2,1)}), bf16[16,40,128]{2,1,0:T(8,128)(2,1)S(1)}, u32[]{:S(2)}, u32[]{:S(2)}) %all-to-all-start) | async-done | bytes 163872 | tf_op jit(solution)/shard_map/all_to_all | solution.py:529
  17.8 7.1 %shard_map.122 = bf16[16,40,128]{2,1,0:T(8,128)(2,1)} custom-call(f32[2,16]{1,0:T(2,128)S(1)} %get-tuple-element.44.table_ref, bf16[16,40,128]{2,1,0:T(8,128)(2,1)S(1)} %all-to-all-done.cells_in_ref, f32[4,64,1024]{2,1,0:T(8,128)S(1)} %get-tuple-element.46.seen_ref, f32[1,64,16,1024]{3,2,1,0:T(8,128)} %measured_ref.1), custom_call_target="tpu_custom_call" | custom-call | tf_op jit(solution)/shard_map/pallas_call | solution.py:456
  24.8 4.5 %all-to-all-start.1 = ((bf16[16,40,128]{2,1,0:T(8,128)(2,1)}), bf16[16,40,128]{2,1,0:T(8,128)(2,1)S(1)}, u32[]{:S(2)}, u32[]{:S(2)}) async-start(bf16[16,40,128]{2,1,0:T(8,128)(2,1)} %shard_map.122), calls=%async_computation.1 | async-start | bytes 327680 | tf_op jit(solution)/shard_map/all_to_all | solution.py:548
  30.0 7.0 %shard_map.121 = (f32[64,1024]{1,0:T(8,128)S(1)}, bf16[128,1024]{1,0:T(8,128)(2,1)S(1)}) custom-call(bf16[128,1024]{1,0:T(8,128)(2,1)S(1)} %get-tuple-element.42.refs_0_, f32[1,64,1024]{2,1,0:T(8,128)S(1)} %get-tuple-element.27.refs_1_.volume_ref, f32[2,64,128]{2,1,0:T(8,128)S(1)} %get-tuple-element.36.refs_2_.lift_ref, ...), custom_call_target="tpu_custom_call" | custom-call | tf_op jit(solution)/shard_map/pallas_call | solution.py:507
  37.0 0.8 %all-to-all-done.1.back_ref = bf16[16,40,128]{2,1,0:T(8,128)(2,1)S(1)} async-done(((bf16[16,40,128]{2,1,0:T(8,128)(2,1)}), bf16[16,40,128]{2,1,0:T(8,128)(2,1)S(1)}, u32[]{:S(2)}, u32[]{:S(2)}) %all-to-all-start.1) | async-done | bytes 163872 | tf_op jit(solution)/shard_map/all_to_all | solution.py:548
  37.8 0.0 copy-done
  37.8 2.5 %shard_map.123 = f32[1,64,1024]{2,1,0:T(8,128)} custom-call(s32[1]{0:T(128)} %bitcast.anchor_ref, f32[1]{0:T(128)S(6)} %copy.13.step_ref, f32[1,64,1024]{2,1,0:T(8,128)S(1)} %get-tuple-element.27.refs_1_.volume_ref, f32[1,64,1024]{2,1,0:T(8,128)S(1)} %copy-done, f32[64,1024]{1,0:T(8,128)S(1)} %get-tuple-element.41.one_ref, ...), custom_call_target="tpu_custom_call" | custom-call | tf_op jit(solution)/shard_map/pallas_call | solution.py:550
Async XLA Ops:
  1.9 15.9 %all-to-all-start = ((bf16[16,40,128]{2,1,0:T(8,128)(2,1)}), bf16[16,40,128]{2,1,0:T(8,128)(2,1)S(1)}, u32[]{:S(2)}, u32[]{:S(2)}) async-start(bf16[16,40,128]{2,1,0:T(8,128)(2,1)} %get-tuple-element.45), calls=%async_computation | async-start | bytes 327680 | tf_op jit(solution)/shard_map/all_to_all | solution.py:529
  16.2 21.6 %copy-start = (f32[1,64,1024]{2,1,0:T(8,128)S(1)}, f32[1,64,1024]{2,1,0:T(8,128)}, u32[]{:S(2)}) copy-start(f32[1,64,1024]{2,1,0:T(8,128)} %noise_ref.1) | copy-start | bytes 786436
  24.8 12.9 %all-to-all-start.1 = ((bf16[16,40,128]{2,1,0:T(8,128)(2,1)}), bf16[16,40,128]{2,1,0:T(8,128)(2,1)S(1)}, u32[]{:S(2)}, u32[]{:S(2)}) async-start(bf16[16,40,128]{2,1,0:T(8,128)(2,1)} %shard_map.122), calls=%async_computation.1 | async-start | bytes 327680 | tf_op jit(solution)/shard_map/all_to_all | solution.py:548

commit v8 on v7

--- a/solution.py
+++ b/solution.py
@@ -14,6 +14,7 @@
 TURN = 4
 WAIT = 14
 EARLY = 4
+PARTS = 2
 SETS = 4
 
 data_gain = 0.25
@@ -34,31 +35,42 @@
 
 
 def pack_kernel(*refs):
-    count = (len(refs) - 2) // 2
-    sources, out_ref, held, sems = refs[:count], refs[count], refs[count + 1 : -1], refs[-1]
+    count = (len(refs) - 4) // 2
+    sources, out_ref, held, (block_ref, sems, sent_sems) = refs[:count], refs[count], refs[count + 1 : -3], refs[-3:]
+    volume_ref = held[0]
+    rows, width = volume_ref.shape[1:]
+    peers = out_ref.shape[0]
+    chunks = LANES // rows
+    depth = rows // chunks
+    arriving = []
+    for k in range(PARTS):
+        at = pl.ds(k * width // PARTS, width // PARTS)
+        copy = pltpu.make_async_copy(sources[0].at[0, :, at], volume_ref.at[0, :, at], sems.at[k])
+        copy.start()
+        arriving.append(copy)
     copies = [
-        pltpu.make_async_copy(source, target, sems.at[k]) for k, (source, target) in enumerate(zip(sources, held))
+        pltpu.make_async_copy(source, target, sems.at[PARTS + k])
+        for k, (source, target) in enumerate(zip(sources[1:], held[1:]))
     ]
     for copy in copies:
         copy.start()
-    copies[0].wait()
-    volume_ref = held[0]
-    rows = volume_ref.shape[1]
-    peers = out_ref.shape[0]
-    chunks = LANES // rows
-    depth = rows // chunks
-    edge = jnp.concatenate([volume_ref[0, :2], volume_ref[0, rows - 2 :]], axis=0)
-    _, middle, final = split(edge, 3)
     blank = [jnp.zeros((4, LANES - 2 * rows), f32)] if 2 * rows < LANES else []
     none = jnp.zeros((4, LANES), f32)
-    for peer in range(peers):
-        at = slice(peer * rows, (peer + 1) * rows)
-        piece = volume_ref[0, :, at]
-        wide = jnp.concatenate([piece[k * depth : (k + 1) * depth] for k in range(chunks)], axis=1)
-        out_ref[peer, :depth] = wide.astype(bf16)
-        lower = jnp.concatenate([middle[:, at], final[:, at]] + blank, axis=1)
-        out_ref[peer, depth:] = jnp.concatenate([lower, none], axis=0).astype(bf16)
-    for copy in copies[1:]:
+    for k in range(PARTS):
+        arriving[k].wait()
+        mine = range(k * peers // PARTS, (k + 1) * peers // PARTS)
+        for peer in mine:
+            at = slice(peer * rows, (peer + 1) * rows)
+            piece = volume_ref[0, :, at]
+            wide = jnp.concatenate([piece[i * depth : (i + 1) * depth] for i in range(chunks)], axis=1)
+            block_ref[peer, :depth] = wide.astype(bf16)
+            _, middle, final = split(jnp.concatenate([piece[:2], piece[rows - 2 :]], axis=0), 3)
+            lower = jnp.concatenate([middle, final] + blank, axis=1)
+            block_ref[peer, depth:] = jnp.concatenate([lower, none], axis=0).astype(bf16)
+        at = pl.ds(mine.start, len(mine))
+        copies.append(pltpu.make_async_copy(block_ref.at[at], out_ref.at[at], sent_sems.at[k]))
+        copies[-1].start()
+    for copy in copies:
         copy.wait()
 
 
@@ -143,12 +155,17 @@
             kept_ref[kept_at + c : kept_at + c + 16, :] = h
 
 
-def convolved(p0, p1, wa_ref, bias_ref, store):
+def convolved(p0, p1, wa_ref, bias_ref, store, keep=None):
     width = p0.shape[2]
     for n in range(0, width, 256):
         rhs = jnp.concatenate([r[j, :, n : n + 256] for j in range(3) for r in (p0, p1)], axis=0)
         acc = jnp.dot(wa_ref[...], rhs, preferred_element_type=f32)
         z = acc + jnp.concatenate([bias_ref[...]] * 2, axis=1)
+        if keep is not None:
+            half = z.shape[0] // 2
+            z = jnp.concatenate(
+                [part if factor is None else part * factor for part, factor in zip((z[:half], z[half:]), keep)], axis=0
+            )
         store(slice(n, n + 256), (z * jnp.tanh(z) + z).astype(bf16))
 
 
@@ -347,7 +364,7 @@
 
 def finish_kernel(
     anchor_ref, step_ref, volume_ref, noise_ref, one_ref, two_ref, back_ref, head_ref, tail_ref, lift_ref, bias_ref,
-    wa_ref, wb_ref, wr_ref, out_ref, ext_ref, ring_a, ring_b, h1_ref, score_ref, done_ref, sems, *, count, height, border,
+    wa_ref, wb_ref, wr_ref, out_ref, ext_ref, score_ref, done_ref, sems, *scratch, count, height, border,
 ):
     rows, width = score_ref.shape
     channels = lift_ref.shape[1]
@@ -355,6 +372,7 @@
     chunks = LANES // rows
     depth = rows // chunks
     anchor = anchor_ref[0]
+    rings, h1_refs = scratch[:4], scratch[4:]
 
     tails = [back_ref[peer, depth:].astype(f32) for peer in range(peers)]
     lane = lax.broadcasted_iota(jnp.int32, (8, LANES), 1)
@@ -398,32 +416,24 @@
     copies = [combine(8, rows - 8, sems.at[0])] if rows > 16 else []
     inside = jnp.where(anchor > 0, 1.0, 0.0).astype(f32), jnp.where(anchor + rows < height, 1.0, 0.0).astype(f32)
     for side in range(2):
+        own = rings[2 * side : 2 * side + 2]
         for k in range(4):
             line = ext_ref[8 * side + k : 8 * side + k + 1, :]
             halo = (k < 2) == (side == 0)
-            ring = (ring_a, ring_b)[k // 2]
-            lifted(line, lift_ref, ring, (k % 2) * channels, keep=inside[side] if halo else None)
-
-        def store(at, h):
-            h1_ref[2 * channels * side : 2 * channels * (side + 1), at] = h
-
-        convolved(ring_a, ring_b, wa_ref, bias_ref, store)
-        if side == 0:
-            h1_ref[2 * channels :] = head_ref[...]
-
-            @pl.when(anchor == 0)
-            def _():
-                h1_ref[:channels] = jnp.zeros((channels, width), bf16)
-        else:
-            h1_ref[: 2 * channels] = tail_ref[...]
-
-            @pl.when(anchor + rows == height)
-            def _():
-                h1_ref[3 * channels :] = jnp.zeros((channels, width), bf16)
-
-        scores = projected(h1_ref[...], (ring_b, ring_a)[side][1], wb_ref, wr_ref)
-        at = (rows - 2) * side
-        score_ref[at : at + 2] = scores[:2]
+            lifted(line, lift_ref, own[k // 2], (k % 2) * channels, keep=inside[side] if halo else None)
+    for side in range(2):
+        own = rings[2 * side : 2 * side + 2]
+        h1_ref = h1_refs[side]
+        at = 2 * channels * side
+
+        def store(columns, h):
+            h1_ref[at : at + 2 * channels, columns] = h
+
+        convolved(*own, wa_ref, bias_ref, store, keep=((inside[0], None), (None, inside[1]))[side])
+        h1_ref[2 * channels - at : 4 * channels - at] = (head_ref, tail_ref)[side][...]
+        scores = projected(h1_ref[...], own[1 - side][1], wb_ref, wr_ref)
+        row = (rows - 2) * side
+        score_ref[row : row + 2] = scores[:2]
 
     for k, low in enumerate((0, rows - 8)):
         copies.append(combine(low, low + 8, sems.at[k + 1]))
@@ -523,8 +533,12 @@
         4,
         out_shape=(spec((peers, depth + 8, LANES), bf16),) + tuple(spec(a.shape, a.dtype) for a in small),
         in_specs=[HBM] * len(small),
-        out_specs=(VMEM,) * (len(small) + 1),
-        scratch_shapes=[pltpu.SemaphoreType.DMA((len(small),))],
+        out_specs=(HBM,) + (VMEM,) * len(small),
+        scratch_shapes=[
+            pltpu.VMEM((peers, depth + 8, LANES), bf16),
+            pltpu.SemaphoreType.DMA((len(small) - 1 + PARTS,)),
+            pltpu.SemaphoreType.DMA((PARTS,)),
+        ],
     )(*[apart(a) for a in small])
     cells = lax.all_to_all(payload, "slab", 0, 0)
     wa, wb, wr, lift, bias, table = call(
@@ -555,12 +569,11 @@
         out_specs=HBM,
         scratch_shapes=[
             pltpu.VMEM((16, width), f32),
-            ring,
-            ring,
-            pltpu.VMEM((4 * channels, width), bf16),
             pltpu.VMEM((rows, width), f32),
             pltpu.VMEM((rows, width), f32),
             pltpu.SemaphoreType.DMA((3,)),
+            *[ring] * 4,
+            *[pltpu.VMEM((4 * channels, width), bf16)] * 2,
         ],
     )(anchor, step_size, volume, noise, one, two, returned, head, tail, *consts)
 

time: 40.8 us -> 40.5 us (level)
  transfers between devices with their start and end apart: 2 -> 2, of which waited for: 2 -> 2; matrix products, arithmetic and copies ran while one was open for 0% -> 0% of each run, Pallas kernels for 34% -> 35%
where the time goes in v8:
time: 40.5 us; the launch traced here: 40.1 us
  Pallas kernels  25 us (62%)
  starting transfers between devices  12 us (30%)
  waiting for transfers between devices  2.33 us (6%)
  between operations  0.87 us (2%)
    pallas_call x2, Pallas kernels, score_part(): call(functools.partial(score_kernel, begin=begin, count=count), 20, out_s...  13.4 us
    all_to_all x1, starting transfers between devices, per_device(): cells = lax.all_to_all(payload, 'slab', 0, 0)  7.43 us
    pallas_call x1, Pallas kernels, data_call(): call(data_kernel, 12, out_shape=spec((peers, rows * rows // LANES + 8, LA...  7.08 us
    all_to_all x1, starting transfers between devices, per_device(): returned = lax.all_to_all(sent, 'slab', 0, 0)  4.53 us
    pallas_call x1, Pallas kernels, per_device(): call(functools.partial(finish_kernel, count=slices * peers * rows * views...  2.21 us
    pallas_call x1, Pallas kernels, per_device(): call(pack_kernel, 4, out_shape=(spec((peers, depth + 8, LANES), bf16),) +...  1.83 us
    all_to_all x1, waiting for transfers between devices, per_device(): cells = lax.all_to_all(payload, 'slab', 0, 0)  1.53 us
  transfers between devices with their start and end apart: 2, of which 2 were waited for; matrix products, arithmetic and copies ran while one was open for 0% of the time, Pallas kernels for 35%

profile of v8, /device:TPU:0, one launch (start us, length us, event | category | flops | bytes accessed | tf_op | source)
XLA Modules:
  0.0 40.1 jit_solution(13168317954824495652)
XLA Ops:
  0.0 1.8 %shard_map.118 = (bf16[16,40,128]{2,1,0:T(8,128)(2,1)}, f32[1,64,1024]{2,1,0:T(8,128)S(1)}, s32[1,16]{1,0:T(1,128)S(1)}, s32[1,16]{1,0:T(1,128)S(1)}, f32[1,64]{...) custom-call(f32[1,64,1024]{2,1,0:T(8,128)} %refs_0_.2, ...), custom_call_target="tpu_custom_call" | custom-call | tf_op jit(solution)/shard_map/pallas_call | solution.py:531
  1.8 7.4 %all-to-all-start = ((bf16[16,40,128]{2,1,0:T(8,128)(2,1)}), bf16[16,40,128]{2,1,0:T(8,128)(2,1)S(1)}, u32[]{:S(2)}, u32[]{:S(2)}) async-start(bf16[16,40,128]{2,1,0:T(8,128)(2,1)} %get-tuple-element.45), calls=%async_computation | async-start | bytes 327680 | tf_op jit(solution)/shard_map/all_to_all | solution.py:543
  9.3 0.4 shard_map.119
  9.7 6.5 %shard_map.120 = (f32[64,1024]{1,0:T(8,128)S(1)}, bf16[128,1024]{1,0:T(8,128)(2,1)S(1)}, bf16[128,1024]{1,0:T(8,128)(2,1)S(1)}, f32[4,64,1024]{2,1,0:T(8,128)S(1)}) custom-call(f32[1,64,16,1024]{3,2,1,0:T(8,128)} %measured_ref.1, f32[1,64,1024]{2,1,0:T(8,128)S(1)} %get-tuple-element.27.refs_1_.volume_ref, ...), custom_call_target="tpu_custom_call" | custom-call | tf_op jit(solution)/shard_map/pallas_call | solution.py:517
  16.2 0.0 copy-start
  16.2 1.5 %all-to-all-done.cells_in_ref = bf16[16,40,128]{2,1,0:T(8,128)(2,1)S(1)} async-done(((bf16[16,40,128]{2,1,0:T(8,128)(2,1)}), bf16[16,40,128]{2,1,0:T(8,128)(2,1)S(1)}, u32[]{:S(2)}, u32[]{:S(2)}) %all-to-all-start) | async-done | bytes 163872 | tf_op jit(solution)/shard_map/all_to_all | solution.py:543
  17.7 7.1 %shard_map.122 = bf16[16,40,128]{2,1,0:T(8,128)(2,1)} custom-call(f32[2,16]{1,0:T(2,128)S(1)} %get-tuple-element.44.table_ref, bf16[16,40,128]{2,1,0:T(8,128)(2,1)S(1)} %all-to-all-done.cells_in_ref, f32[4,64,1024]{2,1,0:T(8,128)S(1)} %get-tuple-element.46.seen_ref, f32[1,64,16,1024]{3,2,1,0:T(8,128)} %measured_ref.1), custom_call_target="tpu_custom_call" | custom-call | tf_op jit(solution)/shard_map/pallas_call | solution.py:466
  24.8 4.5 %all-to-all-start.1 = ((bf16[16,40,128]{2,1,0:T(8,128)(2,1)}), bf16[16,40,128]{2,1,0:T(8,128)(2,1)S(1)}, u32[]{:S(2)}, u32[]{:S(2)}) async-start(bf16[16,40,128]{2,1,0:T(8,128)(2,1)} %shard_map.122), calls=%async_computation.1 | async-start | bytes 327680 | tf_op jit(solution)/shard_map/all_to_all | solution.py:562
  30.0 7.0 %shard_map.121 = (f32[64,1024]{1,0:T(8,128)S(1)}, bf16[128,1024]{1,0:T(8,128)(2,1)S(1)}) custom-call(bf16[128,1024]{1,0:T(8,128)(2,1)S(1)} %get-tuple-element.42.refs_0_, f32[1,64,1024]{2,1,0:T(8,128)S(1)} %get-tuple-element.27.refs_1_.volume_ref, f32[2,64,128]{2,1,0:T(8,128)S(1)} %get-tuple-element.36.refs_2_.lift_ref, ...), custom_call_target="tpu_custom_call" | custom-call | tf_op jit(solution)/shard_map/pallas_call | solution.py:517
  37.0 0.8 %all-to-all-done.1.back_ref = bf16[16,40,128]{2,1,0:T(8,128)(2,1)S(1)} async-done(((bf16[16,40,128]{2,1,0:T(8,128)(2,1)}), bf16[16,40,128]{2,1,0:T(8,128)(2,1)S(1)}, u32[]{:S(2)}, u32[]{:S(2)}) %all-to-all-start.1) | async-done | bytes 163872 | tf_op jit(solution)/shard_map/all_to_all | solution.py:562
  37.7 0.0 copy-done
  37.8 2.2 %shard_map.123 = f32[1,64,1024]{2,1,0:T(8,128)} custom-call(s32[1]{0:T(128)} %bitcast.anchor_ref, f32[1]{0:T(128)S(6)} %copy.13.step_ref, f32[1,64,1024]{2,1,0:T(8,128)S(1)} %get-tuple-element.27.refs_1_.volume_ref, f32[1,64,1024]{2,1,0:T(8,128)S(1)} %copy-done, f32[64,1024]{1,0:T(8,128)S(1)} %get-tuple-element.41.one_ref, ...), custom_call_target="tpu_custom_call" | custom-call | tf_op jit(solution)/shard_map/pallas_call | solution.py:564
Async XLA Ops:
  1.8 15.9 %all-to-all-start = ((bf16[16,40,128]{2,1,0:T(8,128)(2,1)}), bf16[16,40,128]{2,1,0:T(8,128)(2,1)S(1)}, u32[]{:S(2)}, u32[]{:S(2)}) async-start(bf16[16,40,128]{2,1,0:T(8,128)(2,1)} %get-tuple-element.45), calls=%async_computation | async-start | bytes 327680 | tf_op jit(solution)/shard_map/all_to_all | solution.py:543
  16.2 21.6 %copy-start = (f32[1,64,1024]{2,1,0:T(8,128)S(1)}, f32[1,64,1024]{2,1,0:T(8,128)}, u32[]{:S(2)}) copy-start(f32[1,64,1024]{2,1,0:T(8,128)} %noise_ref.1) | copy-start | bytes 786436
  24.8 13.0 %all-to-all-start.1 = ((bf16[16,40,128]{2,1,0:T(8,128)(2,1)}), bf16[16,40,128]{2,1,0:T(8,128)(2,1)S(1)}, u32[]{:S(2)}, u32[]{:S(2)}) async-start(bf16[16,40,128]{2,1,0:T(8,128)(2,1)} %shard_map.122), calls=%async_computation.1 | async-start | bytes 327680 | tf_op jit(solution)/shard_map/all_to_all | solution.py:562

commit v9 on v8

--- a/solution.py
+++ b/solution.py
@@ -15,7 +15,7 @@
 WAIT = 14
 EARLY = 4
 PARTS = 2
-SETS = 4
+SETS = 3
 
 data_gain = 0.25
 
@@ -63,11 +63,12 @@
             at = slice(peer * rows, (peer + 1) * rows)
             piece = volume_ref[0, :, at]
             wide = jnp.concatenate([piece[i * depth : (i + 1) * depth] for i in range(chunks)], axis=1)
-            block_ref[peer, :depth] = wide.astype(bf16)
+            slot = peers - 1 - peer
+            block_ref[slot, :depth] = wide.astype(bf16)
             _, middle, final = split(jnp.concatenate([piece[:2], piece[rows - 2 :]], axis=0), 3)
             lower = jnp.concatenate([middle, final] + blank, axis=1)
-            block_ref[peer, depth:] = jnp.concatenate([lower, none], axis=0).astype(bf16)
-        at = pl.ds(mine.start, len(mine))
+            block_ref[slot, depth:] = jnp.concatenate([lower, none], axis=0).astype(bf16)
+        at = pl.ds(peers - mine.stop, len(mine))
         copies.append(pltpu.make_async_copy(block_ref.at[at], out_ref.at[at], sent_sems.at[k]))
         copies[-1].start()
     for copy in copies:
@@ -258,7 +259,7 @@
     for tile in range(nx // LANES):
         pieces = []
         for peer in range(tile * chunks, (tile + 1) * chunks):
-            got = cells_in_ref[peer, :depth].astype(f32)
+            got = cells_in_ref[peers - 1 - peer, :depth].astype(f32)
             pieces += [got[:, k * rows : (k + 1) * rows] for k in range(chunks)]
         cells_ref[:, tile * LANES : (tile + 1) * LANES] = (-jnp.concatenate(pieces, axis=0).T).astype(bf16)
 
@@ -344,7 +345,7 @@
     whole = split(jnp.sum(sum_ref[...], keepdims=True), 3)
     lane = lax.broadcasted_iota(jnp.int32, (8, LANES), 1)
     third = lax.broadcasted_iota(jnp.int32, (8, LANES), 0) == 2
-    got = [cells_in_ref[peer].astype(f32) for peer in range(peers)]
+    got = [cells_in_ref[peers - 1 - peer].astype(f32) for peer in range(peers)]
     for peer in range(peers):
         low, high = got[max(peer - 1, 0)], got[min(peer + 1, peers - 1)]
         note = jnp.concatenate(
@@ -352,14 +353,14 @@
         )
         for k in range(3):
             note = jnp.where(third & (lane == rows + k), whole[k], note)
-        out_ref[peer, depth:] = note.astype(bf16)
+        out_ref[peers - 1 - peer, depth:] = note.astype(bf16)
     for tile in range(nx // LANES):
         turned = back_ref[:, tile * LANES : (tile + 1) * LANES].T
         for k in range(chunks):
             peer = tile * chunks + k
             own = turned[k * rows : (k + 1) * rows]
             wide = jnp.concatenate([own[i * depth : (i + 1) * depth] for i in range(chunks)], axis=1)
-            out_ref[peer, :depth] = wide.astype(bf16)
+            out_ref[peers - 1 - peer, :depth] = wide.astype(bf16)
 
 
 def finish_kernel(
@@ -374,7 +375,7 @@
     anchor = anchor_ref[0]
     rings, h1_refs = scratch[:4], scratch[4:]
 
-    tails = [back_ref[peer, depth:].astype(f32) for peer in range(peers)]
+    tails = [back_ref[peers - 1 - peer, depth:].astype(f32) for peer in range(peers)]
     lane = lax.broadcasted_iota(jnp.int32, (8, LANES), 1)
     third = lax.broadcasted_iota(jnp.int32, (8, LANES), 0) == 2
     total = tails[0]
@@ -403,7 +404,7 @@
     def combine(low, high, sem):
         for tile in range(width // LANES):
             at = slice(tile * LANES, (tile + 1) * LANES)
-            got = [back_ref[tile * chunks + k, :depth].astype(f32) for k in range(chunks)]
+            got = [back_ref[peers - 1 - tile * chunks - k, :depth].astype(f32) for k in range(chunks)]
             back = jnp.concatenate(
                 [jnp.concatenate([g[:, k * rows : (k + 1) * rows] for g in got], axis=1) for k in range(chunks)], axis=0
             )[low:high]
@@ -506,6 +507,7 @@
         return array.reshape(1, -1)
 
     pairs = rows // 2 - 1
+    order = [list(reversed(range(peers)))]
     half = pairs // 2
     ring = pltpu.VMEM((3, 2 * channels, width), bf16)
     pair = spec((2 * channels, width), bf16)
@@ -540,7 +542,7 @@
             pltpu.SemaphoreType.DMA((PARTS,)),
         ],
     )(*[apart(a) for a in small])
-    cells = lax.all_to_all(payload, "slab", 0, 0)
+    cells = lax.all_to_all(payload, "slab", 0, 0, axis_index_groups=order)
     wa, wb, wr, lift, bias, table = call(
         prep_kernel,
         6,
@@ -559,7 +561,7 @@
     one, head, middle, seen = score_part(0, half, apart(measured), volume, *consts)
 
     sent = data_call(table, cells, seen, measured)
-    returned = lax.all_to_all(sent, "slab", 0, 0)
+    returned = lax.all_to_all(sent, "slab", 0, 0, axis_index_groups=order)
     two, tail = score_part(half, pairs - half, middle, volume, *consts)
     return call(
         functools.partial(finish_kernel, count=slices * peers * rows * views * det, height=height, border=2 * half),

time: 40.5 us -> 40.8 us (level)
  starting transfers between devices: 12 us -> 14.6 us
  waiting for transfers between devices: 2.33 us -> 0.01 us
    all_to_all x2, starting transfers between devices: 12 us -> 14.6 us  [the longest x1 8.89 us: per_device(): cells = lax.all_to_all(payload, 'slab', 0, 0, axis_index_groups=order)]
    all_to_all x2, waiting for transfers between devices: 2.33 us -> 0.01 us  [the longest x1 0.01 us: per_device(): returned = lax.all_to_all(sent, 'slab', 0, 0, axis_index_groups=order)]
  transfers between devices with their start and end apart: 2 -> 2, of which waited for: 2 -> 0; matrix products, arithmetic and copies ran while one was open for 0% -> 0% of each run, Pallas kernels for 35% -> 34%
where the time goes in v9:
time: 40.8 us; the launch traced here: 40.4 us
  Pallas kernels  24.9 us (61%)
  starting transfers between devices  14.6 us (36%)
  between operations  0.88 us (2%)
    pallas_call x2, Pallas kernels, score_part(): call(functools.partial(score_kernel, begin=begin, count=count), 20, out_s...  13.4 us
    all_to_all x1, starting transfers between devices, per_device(): cells = lax.all_to_all(payload, 'slab', 0, 0, axis_index_groups=order)  8.89 us
    pallas_call x1, Pallas kernels, data_call(): call(data_kernel, 12, out_shape=spec((peers, rows * rows // LANES + 8, LA...  7.03 us
    all_to_all x1, starting transfers between devices, per_device(): returned = lax.all_to_all(sent, 'slab', 0, 0, axis_index_groups=order)  5.75 us
    pallas_call x1, Pallas kernels, per_device(): call(functools.partial(finish_kernel, count=slices * peers * rows * views...  2.22 us
    pallas_call x1, Pallas kernels, per_device(): call(pack_kernel, 4, out_shape=(spec((peers, depth + 8, LANES), bf16),) +...  1.83 us
  transfers between devices with their start and end apart: 2, of which 0 were waited for; matrix products, arithmetic and copies ran while one was open for 0% of the time, Pallas kernels for 34%

profile of v9, /device:TPU:0, one launch (start us, length us, event | category | flops | bytes accessed | tf_op | source)
XLA Modules:
  0.0 40.4 jit_solution(17857707536262135928)
XLA Ops:
  0.0 1.8 %shard_map.118 = (bf16[16,40,128]{2,1,0:T(8,128)(2,1)}, f32[1,64,1024]{2,1,0:T(8,128)S(1)}, s32[1,16]{1,0:T(1,128)S(1)}, s32[1,16]{1,0:T(1,128)S(1)}, f32[1,64]{...) custom-call(f32[1,64,1024]{2,1,0:T(8,128)} %refs_0_.2, ...), custom_call_target="tpu_custom_call" | custom-call | tf_op jit(solution)/shard_map/pallas_call | solution.py:533
  1.8 8.9 %all-to-all-start = ((bf16[16,40,128]{2,1,0:T(8,128)(2,1)}), bf16[16,40,128]{2,1,0:T(8,128)(2,1)S(1)}, u32[]{:S(2)}, u32[]{:S(2)}) async-start(bf16[16,40,128]{2,1,0:T(8,128)(2,1)} %get-tuple-element.45), calls=%async_computation | async-start | bytes 327680 | tf_op jit(solution)/shard_map/all_to_all | solution.py:545
  10.7 0.4 shard_map.119
  11.1 6.5 %shard_map.120 = (f32[64,1024]{1,0:T(8,128)S(1)}, bf16[128,1024]{1,0:T(8,128)(2,1)S(1)}, bf16[128,1024]{1,0:T(8,128)(2,1)S(1)}, f32[4,64,1024]{2,1,0:T(8,128)S(1)}) custom-call(f32[1,64,16,1024]{3,2,1,0:T(8,128)} %measured_ref.1, f32[1,64,1024]{2,1,0:T(8,128)S(1)} %get-tuple-element.27.refs_1_.volume_ref, ...), custom_call_target="tpu_custom_call" | custom-call | tf_op jit(solution)/shard_map/pallas_call | solution.py:519
  17.6 0.0 copy-start
  17.6 0.0 all-to-all-done.cells_in_ref
  17.6 7.0 %shard_map.122 = bf16[16,40,128]{2,1,0:T(8,128)(2,1)} custom-call(f32[2,16]{1,0:T(2,128)S(1)} %get-tuple-element.44.table_ref, bf16[16,40,128]{2,1,0:T(8,128)(2,1)S(1)} %all-to-all-done.cells_in_ref, f32[4,64,1024]{2,1,0:T(8,128)S(1)} %get-tuple-element.46.seen_ref, f32[1,64,16,1024]{3,2,1,0:T(8,128)} %measured_ref.1), custom_call_target="tpu_custom_call" | custom-call | tf_op jit(solution)/shard_map/pallas_call | solution.py:467
  24.7 5.8 %all-to-all-start.1 = ((bf16[16,40,128]{2,1,0:T(8,128)(2,1)}), bf16[16,40,128]{2,1,0:T(8,128)(2,1)S(1)}, u32[]{:S(2)}, u32[]{:S(2)}) async-start(bf16[16,40,128]{2,1,0:T(8,128)(2,1)} %shard_map.122), calls=%async_computation.1 | async-start | bytes 327680 | tf_op jit(solution)/shard_map/all_to_all | solution.py:564
  31.1 7.0 %shard_map.121 = (f32[64,1024]{1,0:T(8,128)S(1)}, bf16[128,1024]{1,0:T(8,128)(2,1)S(1)}) custom-call(bf16[128,1024]{1,0:T(8,128)(2,1)S(1)} %get-tuple-element.42.refs_0_, f32[1,64,1024]{2,1,0:T(8,128)S(1)} %get-tuple-element.27.refs_1_.volume_ref, f32[2,64,128]{2,1,0:T(8,128)S(1)} %get-tuple-element.36.refs_2_.lift_ref, ...), custom_call_target="tpu_custom_call" | custom-call | tf_op jit(solution)/shard_map/pallas_call | solution.py:519
  38.0 0.0 all-to-all-done.1.back_ref
  38.0 0.0 copy-done
  38.1 2.2 %shard_map.123 = f32[1,64,1024]{2,1,0:T(8,128)} custom-call(s32[1]{0:T(128)} %bitcast.anchor_ref, f32[1]{0:T(128)S(6)} %copy.13.step_ref, f32[1,64,1024]{2,1,0:T(8,128)S(1)} %get-tuple-element.27.refs_1_.volume_ref, f32[1,64,1024]{2,1,0:T(8,128)S(1)} %copy-done, f32[64,1024]{1,0:T(8,128)S(1)} %get-tuple-element.41.one_ref, ...), custom_call_target="tpu_custom_call" | custom-call | tf_op jit(solution)/shard_map/pallas_call | solution.py:566
Async XLA Ops:
  1.8 15.8 %all-to-all-start = ((bf16[16,40,128]{2,1,0:T(8,128)(2,1)}), bf16[16,40,128]{2,1,0:T(8,128)(2,1)S(1)}, u32[]{:S(2)}, u32[]{:S(2)}) async-start(bf16[16,40,128]{2,1,0:T(8,128)(2,1)} %get-tuple-element.45), calls=%async_computation | async-start | bytes 327680 | tf_op jit(solution)/shard_map/all_to_all | solution.py:545
  17.6 20.4 %copy-start = (f32[1,64,1024]{2,1,0:T(8,128)S(1)}, f32[1,64,1024]{2,1,0:T(8,128)}, u32[]{:S(2)}) copy-start(f32[1,64,1024]{2,1,0:T(8,128)} %noise_ref.1) | copy-start | bytes 786436
  24.7 13.4 %all-to-all-start.1 = ((bf16[16,40,128]{2,1,0:T(8,128)(2,1)}), bf16[16,40,128]{2,1,0:T(8,128)(2,1)S(1)}, u32[]{:S(2)}, u32[]{:S(2)}) async-start(bf16[16,40,128]{2,1,0:T(8,128)(2,1)} %shard_map.122), calls=%async_computation.1 | async-start | bytes 327680 | tf_op jit(solution)/shard_map/all_to_all | solution.py:564
